TPU v7x, 512 devices: a whole 4x8x8 slice. The times are simulated.
512 devices in a mesh: doc: 16 (over y, x_hi), seq: 32 (over z, x_lo, core).
Axes of the slice: x: 4 (x_hi: 2, x_lo: 2; x = x_hi * 2 + x_lo), y: 8, z: 8, core: 2. Of those that a mesh axis runs over, the one named last changes fastest.
Arguments:
- enc_query: bfloat16 [16, 4096, 2048], P('doc', 'seq'), may hold values from -40 to 40
- enc_key: bfloat16 [16, 4096, 2048], P('doc', 'seq'), may hold values from -16 to 16
- enc_value: bfloat16 [16, 4096, 2048], P('doc', 'seq'), may hold values from -6 to 6
- sum_query: bfloat16 [16, 512, 2048], P('doc', 'seq'), may hold values from -70 to 70
- doc_len: int32 [16], P('doc'), may hold values from 1024 to 4096, as said below
- w_memory: bfloat16 [2, 2048, 2048], P(None, None, 'doc'), may hold values from -0.26367188 to 0.26367188
Outputs:
- encoder_out: bfloat16 [16, 4096, 2048], P('doc', 'seq')
- summary_out: bfloat16 [16, 512, 2048], P('doc', 'seq')
Inputs may be any that keep to these rules, and one draw needn't show every extreme that they name: `doc_len`: at least one document has all 4096 tokens valid.
All inputs are finite; a program needn't handle non-finite values.
Results may differ from a plain program's by a relative error of at most 0.012.
Values may be sent and summed in bfloat16 or wider, within the bound.
A program may use at most 64 MiB of HBM per device.

v0:
```python
import math

import jax
import jax.numpy as jnp
from jax import lax
from jax.sharding import PartitionSpec as P

HEAD_DIM = 64


def attend_heads(queries, keys_all, values_all, length, head_dim):
    row_count = queries.shape[0]
    feature_width = queries.shape[1]
    head_count = feature_width // head_dim
    block_rows = math.gcd(row_count, 512)
    grouped = queries.reshape(row_count // block_rows, block_rows, head_count, head_dim)
    key_heads = keys_all.reshape(-1, head_count, head_dim)
    value_heads = values_all.reshape(-1, head_count, head_dim)
    key_valid = jnp.arange(key_heads.shape[0]) < length

    def one_block(query_block):
        scores = jnp.einsum(
            "qhd,khd->hqk", query_block, key_heads, preferred_element_type=jnp.float32
        ) * head_dim ** (-0.5)
        scores = jnp.where(key_valid[None, None, :], scores, -1e30)
        row_max = jnp.max(scores, axis=-1, keepdims=True)
        weights = jnp.exp(scores - row_max)
        denominator = jnp.sum(weights, axis=-1)
        weighted = jnp.einsum(
            "hqk,khd->qhd",
            weights.astype(jnp.bfloat16),
            value_heads,
            preferred_element_type=jnp.float32,
        )
        return (weighted / denominator.T[:, :, None]).astype(jnp.bfloat16)

    return lax.map(one_block, grouped).reshape(row_count, feature_width)


def shards(enc_query, enc_key, enc_value, sum_query, doc_len, w_memory):
    head_dim = HEAD_DIM
    length = doc_len[0]
    head_query, head_key, head_value = (
        lax.all_to_all(enc_query[0], "seq", split_axis=1, concat_axis=0, tiled=True),
        lax.all_to_all(enc_key[0], "seq", split_axis=1, concat_axis=0, tiled=True),
        lax.all_to_all(enc_value[0], "seq", split_axis=1, concat_axis=0, tiled=True),
    )
    context = attend_heads(head_query, head_key, head_value, length, head_dim)
    encoder_out = lax.all_to_all(context, "seq", split_axis=0, concat_axis=1, tiled=True)
    made = jnp.einsum(
        "btd,kdc->btkc",
        lax.all_gather(encoder_out[None], "doc", axis=0, tiled=True),
        w_memory,
        preferred_element_type=jnp.float32,
    )
    memory_rows = made.astype(jnp.bfloat16)
    memory_local = lax.all_to_all(
        lax.all_to_all(memory_rows, "doc", split_axis=0, concat_axis=3, tiled=True),
        "seq",
        split_axis=3,
        concat_axis=1,
        tiled=True,
    )
    memory_keys = memory_local[0, :, 0, :]
    memory_values = memory_local[0, :, 1, :]
    summary_heads = lax.all_to_all(sum_query[0], "seq", split_axis=1, concat_axis=0, tiled=True)
    answer = attend_heads(summary_heads, memory_keys, memory_values, length, head_dim)
    summary_out = lax.all_to_all(answer, "seq", split_axis=0, concat_axis=1, tiled=True)
    return (encoder_out[None], summary_out[None])


def solution(mesh):
    in_specs = (
        P("doc", "seq", None),
        P("doc", "seq", None),
        P("doc", "seq", None),
        P("doc", "seq", None),
        P("doc"),
        P(None, None, "doc"),
    )
    out_specs = (P("doc", "seq", None), P("doc", "seq", None))
    return jax.shard_map(shards, mesh=mesh, in_specs=in_specs, out_specs=out_specs, check_vma=False)
```

profile of v0, /device:TPU:1, one launch (start us, length us, event | category | flops | bytes accessed | tf_op | source)
XLA Modules:
  0.0 431.8 jit_solution(14560852746288561887)
XLA Ops:
  7.2 2.1 copy.43
  9.3 12.9 %all-to-all-start = ((bf16[128,32,64]{0,2,1:T(8,128)(2,1)}), bf16[128,32,64]{0,2,1:T(8,128)(2,1)S(1)}, u32[]{:S(2)}, u32[]{:S(2)}) async-start(bf16[128,32,64]{0,2,1:T(8,128)(2,1)} %bitcast), calls=%async_computation | async-start | bytes 1048576 | tf_op jit(solution)/shard_map/all_to_all | solution.py:44
  22.2 2.1 copy.45
  24.3 14.7 %all-to-all-done = bf16[128,32,64]{0,2,1:T(8,128)(2,1)S(1)} async-done(((bf16[128,32,64]{0,2,1:T(8,128)(2,1)}), bf16[128,32,64]{0,2,1:T(8,128)(2,1)S(1)}, u32[]{:S(2)}, u32[]{:S(2)}) %all-to-all-start) | async-done | bytes 524320 | tf_op jit(solution)/shard_map/all_to_all | solution.py:44
  38.9 5.1 %all-to-all-start.1 = ((bf16[128,32,64]{0,2,1:T(8,128)(2,1)}), bf16[128,32,64]{0,2,1:T(8,128)(2,1)S(1)}, u32[]{:S(2)}, u32[]{:S(2)}) async-start(bf16[128,32,64]{0,2,1:T(8,128)(2,1)} %bitcast.2), calls=%async_computation.1 | async-start | bytes 1048576 | tf_op jit(solution)/shard_map/all_to_all | solution.py:45
  44.0 2.0 copy.47
  46.1 15.0 %all-to-all-done.1 = bf16[128,32,64]{0,2,1:T(8,128)(2,1)S(1)} async-done(((bf16[128,32,64]{0,2,1:T(8,128)(2,1)}), bf16[128,32,64]{0,2,1:T(8,128)(2,1)S(1)}, u32[]{:S(2)}, u32[]{:S(2)}) %all-to-all-start.1) | async-done | bytes 524320 | tf_op jit(solution)/shard_map/all_to_all | solution.py:45
  61.1 4.8 %all-to-all-start.2 = ((bf16[128,32,64]{0,2,1:T(8,128)(2,1)}), bf16[128,32,64]{0,2,1:T(8,128)(2,1)S(1)}, u32[]{:S(2)}, u32[]{:S(2)}) async-start(bf16[128,32,64]{0,2,1:T(8,128)(2,1)} %bitcast.4), calls=%async_computation.2 | async-start | bytes 1048576 | tf_op jit(solution)/shard_map/all_to_all | solution.py:46
  68.2 14.8 %all-to-all-done.2 = bf16[128,32,64]{0,2,1:T(8,128)(2,1)S(1)} async-done(((bf16[128,32,64]{0,2,1:T(8,128)(2,1)}), bf16[128,32,64]{0,2,1:T(8,128)(2,1)S(1)}, u32[]{:S(2)}, u32[]{:S(2)}) %all-to-all-start.2) | async-done | bytes 524320 | tf_op jit(solution)/shard_map/all_to_all | solution.py:46
  83.6 60.9 %while.3 = (s32[]{:T(128)}, bf16[8,512,1,64]{1,3,2,0:T(8,128)(2,1)}, bf16[8,512,1,64]{1,3,2,0:T(8,128)(2,1)}, bf16[4096,1,64]{0,2,1:T(8,128)(2,1)S(1)}, bf16[409...) while((s32[]{:T(128)}, bf16[8,512,1,64]{1,3,2,0:T(8,128)(2,1)}, ...), condition=%wide.region_3.4_spmd.clone, body=%wide.region_0.3_spmd.clone.sunk | while | flops 560008192 | bytes 26373200 | solution.py:37
  84.3 2.3 fusion.66
  86.5 2.2 fusion.67
  88.7 2.5 fusion.68
  91.9 2.3 fusion.66
  94.2 2.2 fusion.67
  96.3 2.5 fusion.68
  99.5 2.3 fusion.66
  101.8 2.2 fusion.67
  103.9 2.5 fusion.68
  107.1 2.3 fusion.66
  109.4 2.2 fusion.67
  111.5 2.5 fusion.68
  114.7 2.3 fusion.66
  117.0 2.2 fusion.67
  119.1 2.5 fusion.68
  122.3 2.3 fusion.66
  124.6 2.2 fusion.67
  126.8 2.5 fusion.68
  129.9 2.3 fusion.66
  132.2 2.2 fusion.67
  134.4 2.5 fusion.68
  137.6 2.3 fusion.66
  139.8 2.2 fusion.67
  142.0 2.5 fusion.68
  144.5 1.3 copy.50
  146.4 20.8 %all_to_all.132 = bf16[32,128,64]{1,2,0:T(8,128)(2,1)S(1)} all-to-all(bf16[32,128,64]{1,2,0:T(8,128)(2,1)S(1)} %copy.51), channel_id=1, replica_groups=mesh['doc'=16,'seq'=32] {'seq'}, dimensions={0} | all-to-all | bytes 1048576 | tf_op jit(solution)/shard_map/all_to_all | solution.py:49
  168.2 137.7 %all-gather.2.cloned.1.call-done = bf16[16,128,2048]{2,1,0:T(8,128)(2,1)} async-done(((bf16[1,128,2048]{2,1,0:T(8,128)(2,1)}), bf16[16,128,2048]{2,1,0:T(8,128)(2,1)}) %all-gather.2.cloned.1.call-update) | async-done | bytes 8388624 | tf_op jit(solution)/shard_map/all_gather | solution.py:52
  305.9 6.8 %fusion.39 = bf16[16,128,2,128]{3,1,2,0:T(8,128)(2,1)} fusion(bf16[16,128,2048]{2,1,0:T(8,128)(2,1)} %all-gather.2.cloned.1.call-done, bf16[2,2048,128]{2,1,0:T(8,128)(2,1)S(1)} %copy-done), kind=kOutput, calls=%fused_computation.31 | convolution fusion | flops 2148007936 | bytes 10485760 | tf_op jit(solution)/shard_map/btd,kdc->btkc/dot_general | solution.py:50
  312.7 4.3 all-to-all-start.4
  318.1 25.2 %all-to-all-done.4 = bf16[16,128,2,128]{3,1,2,0:T(8,128)(2,1)S(1)} async-done(((bf16[16,128,2,128]{3,1,2,0:T(8,128)(2,1)}), bf16[16,128,2,128]{3,1,2,0:T(8,128)(2,1)S(1)}, u32[]{:S(2)}, u32[]{:S(2)}) %all-to-all-start.4) | async-done | bytes 1048608 | tf_op jit(solution)/shard_map/all_to_all | solution.py:58
  343.3 13.0 %all-to-all-start.6 = ((bf16[32,2,512]{2,1,0:T(2,128)(2,1)}), bf16[32,2,512]{2,1,0:T(2,128)(2,1)S(1)}, u32[]{:S(2)}, u32[]{:S(2)}) async-start(bf16[32,2,512]{2,1,0:T(2,128)(2,1)} %reshape.128), calls=%async_computation.6 | async-start | bytes 131072 | tf_op jit(solution)/shard_map/all_to_all | solution.py:66
  357.0 9.5 %copy.54 = bf16[1,128,2,2048]{1,2,0,3:T(2,128)(2,1)} copy(bf16[1,128,2,2048]{1,3,2,0:T(8,128)(2,1)S(1)} %bitcast.112) | data formatting | bytes 2097152 | tf_op jit(solution)/shard_map/all_to_all | solution.py:58
  366.5 8.3 %all-to-all-start.5 = ((bf16[1,128,2,2048]{1,2,0,3:T(2,128)(2,1)}), bf16[1,128,2,2048]{1,2,0,3:T(2,128)(2,1)S(1)}, u32[]{:S(2)}, u32[]{:S(2)}) async-start(bf16[1,128,2,2048]{1,2,0,3:T(2,128)(2,1)} %copy.54), calls=%async_computation.5 | async-start | bytes 2097152 | tf_op jit(solution)/shard_map/all_to_all | solution.py:57
  375.6 27.1 %all-to-all-done.5 = bf16[1,128,2,2048]{1,2,0,3:T(2,128)(2,1)S(1)} async-done(((bf16[1,128,2,2048]{1,2,0,3:T(2,128)(2,1)}), bf16[1,128,2,2048]{1,2,0,3:T(2,128)(2,1)S(1)}, u32[]{:S(2)}, u32[]{:S(2)}) %all-to-all-start.5) | async-done | bytes 1048608 | tf_op jit(solution)/shard_map/all_to_all | solution.py:57
  403.1 3.4 fusion.33
  406.5 2.7 fusion.34
  409.2 1.8 fusion.51
  411.3 12.6 %all_to_all.133 = bf16[32,2,512]{2,1,0:T(2,128)(2,1)S(1)} all-to-all(bf16[32,2,512]{2,1,0:T(2,128)(2,1)S(1)} %reshape.130), channel_id=1, replica_groups=mesh['doc'=16,'seq'=32] {'seq'}, dimensions={0} | all-to-all | bytes 131072 | tf_op jit(solution)/shard_map/all_to_all | solution.py:68
  (39 shorter events, 13.0 us)
Async XLA Ops:
  7.2 298.8 %copy-start = (bf16[2,2048,128]{2,1,0:T(8,128)(2,1)S(1)}, bf16[2,2048,128]{2,1,0:T(8,128)(2,1)}, u32[]{:S(2)}) copy-start(bf16[2,2048,128]{2,1,0:T(8,128)(2,1)} %param.13) | copy-start | bytes 3145732
  9.3 29.6 %all-to-all-start = ((bf16[128,32,64]{0,2,1:T(8,128)(2,1)}), bf16[128,32,64]{0,2,1:T(8,128)(2,1)S(1)}, u32[]{:S(2)}, u32[]{:S(2)}) async-start(bf16[128,32,64]{0,2,1:T(8,128)(2,1)} %bitcast), calls=%async_computation | async-start | bytes 1048576 | tf_op jit(solution)/shard_map/all_to_all | solution.py:44
  38.9 22.2 %all-to-all-start.1 = ((bf16[128,32,64]{0,2,1:T(8,128)(2,1)}), bf16[128,32,64]{0,2,1:T(8,128)(2,1)S(1)}, u32[]{:S(2)}, u32[]{:S(2)}) async-start(bf16[128,32,64]{0,2,1:T(8,128)(2,1)} %bitcast.2), calls=%async_computation.1 | async-start | bytes 1048576 | tf_op jit(solution)/shard_map/all_to_all | solution.py:45
  61.1 21.9 %all-to-all-start.2 = ((bf16[128,32,64]{0,2,1:T(8,128)(2,1)}), bf16[128,32,64]{0,2,1:T(8,128)(2,1)S(1)}, u32[]{:S(2)}, u32[]{:S(2)}) async-start(bf16[128,32,64]{0,2,1:T(8,128)(2,1)} %bitcast.4), calls=%async_computation.2 | async-start | bytes 1048576 | tf_op jit(solution)/shard_map/all_to_all | solution.py:46
  66.0 240.0 %all-gather.2.cloned.1.call-start = ((), (), s32[]{:S(2)}) async-start(), calls=%async_computation.8 | async-start | bytes 8912896 | tf_op jit(solution)/shard_map/all_gather | solution.py:52
  168.2 148.8 %copy-start.1 = (bf16[1,16,2048]{2,1,0:T(8,128)(2,1)S(1)}, bf16[1,16,2048]{2,1,0:T(8,128)(2,1)}, u32[]{:S(2)}) copy-start(bf16[1,16,2048]{2,1,0:T(8,128)(2,1)} %param.11) | copy-start | bytes 196612
  312.7 30.6 %all-to-all-start.4 = ((bf16[16,128,2,128]{3,1,2,0:T(8,128)(2,1)}), bf16[16,128,2,128]{3,1,2,0:T(8,128)(2,1)S(1)}, u32[]{:S(2)}, u32[]{:S(2)}) async-start(bf16[16,128,2,128]{3,1,2,0:T(8,128)(2,1)} %fusion.39), calls=%async_computation.4 | async-start | bytes 2097152 | tf_op jit(solution)/shard_map/all_to_all | solution.py:58
  343.3 23.1 %all-to-all-start.6 = ((bf16[32,2,512]{2,1,0:T(2,128)(2,1)}), bf16[32,2,512]{2,1,0:T(2,128)(2,1)S(1)}, u32[]{:S(2)}, u32[]{:S(2)}) async-start(bf16[32,2,512]{2,1,0:T(2,128)(2,1)} %reshape.128), calls=%async_computation.6 | async-start | bytes 131072 | tf_op jit(solution)/shard_map/all_to_all | solution.py:66
  366.5 36.2 %all-to-all-start.5 = ((bf16[1,128,2,2048]{1,2,0,3:T(2,128)(2,1)}), bf16[1,128,2,2048]{1,2,0,3:T(2,128)(2,1)S(1)}, u32[]{:S(2)}, u32[]{:S(2)}) async-start(bf16[1,128,2,2048]{1,2,0,3:T(2,128)(2,1)} %copy.54), calls=%async_computation.5 | async-start | bytes 2097152 | tf_op jit(solution)/shard_map/all_to_all | solution.py:57
Sparse Core Ops, SparseCore 0:
  168.3 137.5 all-gather.1
where the time goes:
time: 433 us; the launch traced here: 432 us
  waiting for transfers between devices  235 us (54%)
  matrix products  50.5 us (12%)
  starting transfers between devices  48.4 us (11%)
  blocking collectives  33.4 us (8%)
  other arithmetic  25.1 us (6%)
  local copies, waits for them, and re-layouts  24.8 us (6%)
  between operations  14.9 us (3%)
    all_gather x1, waiting for transfers between devices, shards(): lax.all_gather(encoder_out[None], 'doc', axis=0, tiled=True)  138 us
    all_to_all x1, waiting for transfers between devices, shards(): lax.all_to_all(lax.all_to_all(memory_rows, 'doc', split_axis=0, concat_ax...  27.1 us
    all_to_all x1, waiting for transfers between devices, shards(): lax.all_to_all(memory_rows, 'doc', split_axis=0, concat_axis=3, tiled=True)  25.2 us
    dot_general x9, matrix products, one_block(): jnp.einsum('hqk,khd->qhd', weights.astype(jnp.bfloat16), value_heads, pre...  22.1 us
    dot_general x9, matrix products, one_block(): jnp.einsum('qhd,khd->hqk', query_block, key_heads, preferred_element_type...  21.5 us
    all_to_all x1, blocking collectives, shards(): lax.all_to_all(context, 'seq', split_axis=0, concat_axis=1, tiled=True)  20.8 us
    reduce_sum x9, other arithmetic, one_block(): denominator = jnp.sum(weights, axis=-1)  19.9 us
    all_to_all x1, waiting for transfers between devices, shards(): lax.all_to_all(enc_key[0], 'seq', split_axis=1, concat_axis=0, tiled=True)  15 us
  transfers between devices with their start and end apart: 7, of which 6 were waited for; matrix products, arithmetic and copies ran while one was open for 4% of the time, Pallas kernels for 0%

commit v1 on v0

--- a/solution.py
+++ b/solution.py
@@ -40,30 +40,30 @@
 def shards(enc_query, enc_key, enc_value, sum_query, doc_len, w_memory):
     head_dim = HEAD_DIM
     length = doc_len[0]
+    n_seq = lax.axis_size("seq")
+    core = lax.axis_index("seq") % 2
+    half = w_memory.shape[1] // 2
+    w_mine = lax.dynamic_slice_in_dim(w_memory, core * half, half, axis=1)
+    w_mine = lax.all_gather(w_mine, "doc", axis=2, tiled=True)
+    w_other = lax.ppermute(w_mine, "seq", perm=[(i, i ^ 1) for i in range(n_seq)])
+
     head_query, head_key, head_value = (
         lax.all_to_all(enc_query[0], "seq", split_axis=1, concat_axis=0, tiled=True),
         lax.all_to_all(enc_key[0], "seq", split_axis=1, concat_axis=0, tiled=True),
         lax.all_to_all(enc_value[0], "seq", split_axis=1, concat_axis=0, tiled=True),
     )
+    summary_heads = lax.all_to_all(sum_query[0], "seq", split_axis=1, concat_axis=0, tiled=True)
     context = attend_heads(head_query, head_key, head_value, length, head_dim)
     encoder_out = lax.all_to_all(context, "seq", split_axis=0, concat_axis=1, tiled=True)
-    made = jnp.einsum(
-        "btd,kdc->btkc",
-        lax.all_gather(encoder_out[None], "doc", axis=0, tiled=True),
-        w_memory,
-        preferred_element_type=jnp.float32,
-    )
+
+    enc_mine = lax.dynamic_slice_in_dim(encoder_out, core * half, half, axis=1)
+    enc_other = lax.dynamic_slice_in_dim(encoder_out, (1 - core) * half, half, axis=1)
+    made = jnp.einsum("tf,kfc->tkc", enc_mine, w_mine, preferred_element_type=jnp.float32)
+    made = made + jnp.einsum("tf,kfc->tkc", enc_other, w_other, preferred_element_type=jnp.float32)
     memory_rows = made.astype(jnp.bfloat16)
-    memory_local = lax.all_to_all(
-        lax.all_to_all(memory_rows, "doc", split_axis=0, concat_axis=3, tiled=True),
-        "seq",
-        split_axis=3,
-        concat_axis=1,
-        tiled=True,
-    )
-    memory_keys = memory_local[0, :, 0, :]
-    memory_values = memory_local[0, :, 1, :]
-    summary_heads = lax.all_to_all(sum_query[0], "seq", split_axis=1, concat_axis=0, tiled=True)
+    memory_local = lax.all_to_all(memory_rows, "seq", split_axis=2, concat_axis=0, tiled=True)
+    memory_keys = memory_local[:, 0, :]
+    memory_values = memory_local[:, 1, :]
     answer = attend_heads(summary_heads, memory_keys, memory_values, length, head_dim)
     summary_out = lax.all_to_all(answer, "seq", split_axis=0, concat_axis=1, tiled=True)
     return (encoder_out[None], summary_out[None])

time: 433 us -> 346 us (0.80)
  waiting for transfers between devices: 235 us -> 178 us
  blocking collectives: 33.4 us -> 0 us
  starting transfers between devices: 48.4 us -> 53.5 us
  local copies, waits for them, and re-layouts: 24.8 us -> 20 us
    all_gather x1, waiting for transfers between devices: 138 us -> 82.8 us  [shards(): w_mine = lax.all_gather(w_mine, 'doc', axis=2, tiled=True)]
    all_to_all x2 -> x0, blocking collectives: 33.4 us -> none  [the longest x1 20.8 us: shards(): lax.all_to_all(context, 'seq', split_axis=0, concat_axis=1, tiled=True)]
    all_to_all x4 -> x2, local copies, waits for them, and re-layouts: 10.5 us -> 0.38 us  [shards(): lax.all_to_all(memory_rows, 'seq', split_axis=2, concat_axis=0, tiled=True)]
    all_to_all x2 -> x3, starting transfers between devices: 12.6 us -> 20.7 us  [the longest x1 8.38 us: shards(): lax.all_to_all(memory_rows, 'seq', split_axis=2, concat_axis=0, tiled=True)]
    all_to_all x1, starting transfers between devices: 13 us -> 5.07 us  [shards(): lax.all_to_all(sum_query[0], 'seq', split_axis=1, concat_axis=0, tiled=True)]
    ppermute x0 -> x1, starting transfers between devices: none -> 4.79 us  [shards(): lax.ppermute(w_mine, 'seq', perm=[(i, i ^ 1) for i in range(n_seq)])]
    dot_general x1 -> x2, matrix products: 6.79 us -> 9.34 us  [the longest x1 4.67 us: shards(): jnp.einsum('tf,kfc->tkc', enc_other, w_other, preferred_element_type=jnp....]
    all_to_all x2 -> x3, waiting for transfers between devices: 52.4 us -> 50.4 us  [the longest x1 27.3 us: shards(): lax.all_to_all(memory_rows, 'seq', split_axis=2, concat_axis=0, tiled=True)]
  transfers between devices with their start and end apart: 7 -> 9, of which waited for: 6 -> 7; matrix products, arithmetic and copies ran while one was open for 4% -> 25% of each run, Pallas kernels for 0% -> 0%
where the time goes in v1:
time: 346 us; the launch traced here: 344 us
  waiting for transfers between devices  178 us (51%)
  starting transfers between devices  53.5 us (15%)
  matrix products  53 us (15%)
  other arithmetic  25.2 us (7%)
  local copies, waits for them, and re-layouts  20 us (6%)
  between operations  14.9 us (4%)
    all_gather x1, waiting for transfers between devices, shards(): w_mine = lax.all_gather(w_mine, 'doc', axis=2, tiled=True)  82.8 us
    all_to_all x1, waiting for transfers between devices, shards(): lax.all_to_all(memory_rows, 'seq', split_axis=2, concat_axis=0, tiled=True)  27.3 us
    dot_general x9, matrix products, one_block(): jnp.einsum('hqk,khd->qhd', weights.astype(jnp.bfloat16), value_heads, pre...  22.1 us
    dot_general x9, matrix products, one_block(): jnp.einsum('qhd,khd->hqk', query_block, key_heads, preferred_element_type...  21.5 us
    reduce_sum x9, other arithmetic, one_block(): denominator = jnp.sum(weights, axis=-1)  19.9 us
    all_to_all x1, waiting for transfers between devices, shards(): lax.all_to_all(context, 'seq', split_axis=0, concat_axis=1, tiled=True)  15.7 us
    all_to_all x1, waiting for transfers between devices, shards(): lax.all_to_all(enc_key[0], 'seq', split_axis=1, concat_axis=0, tiled=True)  15 us
    all_to_all x1, waiting for transfers between devices, shards(): lax.all_to_all(enc_value[0], 'seq', split_axis=1, concat_axis=0, tiled=True)  14.9 us
  transfers between devices with their start and end apart: 9, of which 7 were waited for; matrix products, arithmetic and copies ran while one was open for 25% of the time, Pallas kernels for 0%

profile of v1, /device:TPU:1, one launch (start us, length us, event | category | flops | bytes accessed | tf_op | source)
XLA Modules:
  0.0 344.4 jit_solution(14123356072603237988)
XLA Ops:
  9.3 2.0 copy.47
  11.3 12.9 %all-to-all-start = ((bf16[128,32,64]{0,2,1:T(8,128)(2,1)}), bf16[128,32,64]{0,2,1:T(8,128)(2,1)S(1)}, u32[]{:S(2)}, u32[]{:S(2)}) async-start(bf16[128,32,64]{0,2,1:T(8,128)(2,1)} %bitcast), calls=%async_computation | async-start | bytes 1048576 | tf_op jit(solution)/shard_map/all_to_all | solution.py:51
  24.2 2.1 copy.49
  26.3 14.7 %all-to-all-done = bf16[128,32,64]{0,2,1:T(8,128)(2,1)S(1)} async-done(((bf16[128,32,64]{0,2,1:T(8,128)(2,1)}), bf16[128,32,64]{0,2,1:T(8,128)(2,1)S(1)}, u32[]{:S(2)}, u32[]{:S(2)}) %all-to-all-start) | async-done | bytes 524320 | tf_op jit(solution)/shard_map/all_to_all | solution.py:51
  40.9 5.1 %all-to-all-start.1 = ((bf16[128,32,64]{0,2,1:T(8,128)(2,1)}), bf16[128,32,64]{0,2,1:T(8,128)(2,1)S(1)}, u32[]{:S(2)}, u32[]{:S(2)}) async-start(bf16[128,32,64]{0,2,1:T(8,128)(2,1)} %bitcast.2), calls=%async_computation.1 | async-start | bytes 1048576 | tf_op jit(solution)/shard_map/all_to_all | solution.py:52
  46.0 2.1 copy.51
  48.1 15.0 %all-to-all-done.1 = bf16[128,32,64]{0,2,1:T(8,128)(2,1)S(1)} async-done(((bf16[128,32,64]{0,2,1:T(8,128)(2,1)}), bf16[128,32,64]{0,2,1:T(8,128)(2,1)S(1)}, u32[]{:S(2)}, u32[]{:S(2)}) %all-to-all-start.1) | async-done | bytes 524320 | tf_op jit(solution)/shard_map/all_to_all | solution.py:52
  63.1 4.8 %all-to-all-start.2 = ((bf16[128,32,64]{0,2,1:T(8,128)(2,1)}), bf16[128,32,64]{0,2,1:T(8,128)(2,1)S(1)}, u32[]{:S(2)}, u32[]{:S(2)}) async-start(bf16[128,32,64]{0,2,1:T(8,128)(2,1)} %bitcast.4), calls=%async_computation.2 | async-start | bytes 1048576 | tf_op jit(solution)/shard_map/all_to_all | solution.py:53
  70.2 14.9 %all-to-all-done.2 = bf16[128,32,64]{0,2,1:T(8,128)(2,1)S(1)} async-done(((bf16[128,32,64]{0,2,1:T(8,128)(2,1)}), bf16[128,32,64]{0,2,1:T(8,128)(2,1)S(1)}, u32[]{:S(2)}, u32[]{:S(2)}) %all-to-all-start.2) | async-done | bytes 524320 | tf_op jit(solution)/shard_map/all_to_all | solution.py:53
  85.6 82.8 %all-gather.2.cloned.1.call-done = bf16[2,1024,2048]{2,1,0:T(8,128)(2,1)} async-done(((bf16[2,1024,128]{2,1,0:T(8,128)(2,1)}), bf16[2,1024,2048]{2,1,0:T(8,128)(2,1)}) %all-gather.2.cloned.1.call-update) | async-done | bytes 8388624 | tf_op jit(solution)/shard_map/all_gather | solution.py:47
  168.4 4.8 %collective-permute-start = (bf16[2,1024,2048]{2,1,0:T(8,128)(2,1)}, bf16[2,1024,2048]{2,1,0:T(8,128)(2,1)}, u32[]{:S(2)}, u32[]{:S(2)}) collective-permute-start(bf16[2,1024,2048]{2,1,0:T(8,128)(2,1)} %all-gather.2.cloned.1.call-done), channel_id=1, source_target_pairs={{0,1},{1,0},{2,3},{3,2},{4,5},{5,4},{6,7},{7,6},{8,9},{9,8},{10,11... | collective-permute-start | bytes 25165832 | tf_op jit(solution)/shard_map/ppermute | solution.py:48
  173.2 60.9 %while.3 = (s32[]{:T(128)}, bf16[8,512,1,64]{1,3,2,0:T(8,128)(2,1)}, bf16[8,512,1,64]{1,3,2,0:T(8,128)(2,1)}, bf16[4096,1,64]{0,2,1:T(8,128)(2,1)S(1)}, bf16[409...) while((s32[]{:T(128)}, bf16[8,512,1,64]{1,3,2,0:T(8,128)(2,1)}, ...), condition=%wide.region_3.4_spmd.clone, body=%wide.region_0.3_spmd.clone.sunk | while | flops 560008192 | bytes 26373200 | solution.py:37
  173.9 2.3 fusion.70
  176.2 2.2 fusion.71
  178.3 2.5 fusion.72
  181.5 2.3 fusion.70
  183.8 2.2 fusion.71
  185.9 2.5 fusion.72
  189.1 2.3 fusion.70
  191.4 2.2 fusion.71
  193.6 2.5 fusion.72
  196.7 2.3 fusion.70
  199.0 2.2 fusion.71
  201.2 2.5 fusion.72
  204.4 2.3 fusion.70
  206.6 2.2 fusion.71
  208.8 2.5 fusion.72
  212.0 2.3 fusion.70
  214.2 2.2 fusion.71
  216.4 2.5 fusion.72
  219.6 2.3 fusion.70
  221.9 2.2 fusion.71
  224.0 2.5 fusion.72
  227.2 2.3 fusion.70
  229.5 2.2 fusion.71
  231.6 2.5 fusion.72
  236.8 7.7 %all-to-all-start.3 = ((bf16[32,128,64]{1,2,0:T(8,128)(2,1)}), bf16[32,128,64]{1,2,0:T(8,128)(2,1)S(1)}, u32[]{:S(2)}, u32[]{:S(2)}) async-start(bf16[32,128,64]{1,2,0:T(8,128)(2,1)} %copy.55), calls=%async_computation.3 | async-start | bytes 1048576 | tf_op jit(solution)/shard_map/all_to_all | solution.py:57
  245.5 15.7 %all-to-all-done.3 = bf16[32,128,64]{1,2,0:T(8,128)(2,1)S(1)} async-done(((bf16[32,128,64]{1,2,0:T(8,128)(2,1)}), bf16[32,128,64]{1,2,0:T(8,128)(2,1)S(1)}, u32[]{:S(2)}, u32[]{:S(2)}) %all-to-all-start.3) | async-done | bytes 524320 | tf_op jit(solution)/shard_map/all_to_all | solution.py:57
  261.2 5.1 %all-to-all-start.5 = ((bf16[32,2,512]{2,1,0:T(2,128)(2,1)}), bf16[32,2,512]{2,1,0:T(2,128)(2,1)S(1)}, u32[]{:S(2)}, u32[]{:S(2)}) async-start(bf16[32,2,512]{2,1,0:T(2,128)(2,1)} %reshape.126), calls=%async_computation.5 | async-start | bytes 131072 | tf_op jit(solution)/shard_map/all_to_all | solution.py:55
  266.3 4.7 %fusion.52 = f32[128,2,2048]{2,0,1:T(8,128)S(1)} fusion(bf16[2,1024,2048]{2,1,0:T(8,128)(2,1)} %all-gather.2.cloned.1.call-done, bf16[128,2048]{0,1:T(8,128)(2,1)S(1)} %bitcast.109, s32[]{:T(128)S(6)} %select_n.26), kind=kOutput, calls=%fused_computation.40 | convolution fusion | flops 1073741824 | bytes 10747908 | tf_op jit(solution)/shard_map/tf,kfc->tkc/dot_general | solution.py:61
  270.9 4.7 %fusion.37 = bf16[128,2,2048]{2,0,1:T(8,128)(2,1)S(1)} fusion(f32[128,2,2048]{2,0,1:T(8,128)S(1)} %fusion.52, bf16[2,1024,2048]{2,1,0:T(8,128)(2,1)} %collective-permute-done, bf16[128,2048]{0,1:T(8,128)(2,1)S(1)} %bitcast.110, s32[]{:T(128)S(6)} %select_n.27), kind=kOutput, calls=%fused_computation.30 | convolution fusion | flops 1074790400 | bytes 11796484 | tf_op jit(solution)/shard_map/tf,kfc->tkc/dot_general | solution.py:62
  275.6 2.0 copy.58
  277.6 8.4 %all-to-all-start.4 = ((bf16[128,2,2048]{0,1,2:T(2,128)(2,1)}), bf16[128,2,2048]{0,1,2:T(2,128)(2,1)S(1)}, u32[]{:S(2)}, u32[]{:S(2)}) async-start(bf16[128,2,2048]{0,1,2:T(2,128)(2,1)} %copy.58), calls=%async_computation.4 | async-start | bytes 2097152 | tf_op jit(solution)/shard_map/all_to_all | solution.py:64
  286.8 27.3 %all-to-all-done.4 = bf16[128,2,2048]{0,1,2:T(2,128)(2,1)S(1)} async-done(((bf16[128,2,2048]{0,1,2:T(2,128)(2,1)}), bf16[128,2,2048]{0,1,2:T(2,128)(2,1)S(1)}, u32[]{:S(2)}, u32[]{:S(2)}) %all-to-all-start.4) | async-done | bytes 1048608 | tf_op jit(solution)/shard_map/all_to_all | solution.py:64
  314.5 3.4 fusion.31
  318.0 2.7 fusion.32
  323.4 4.7 %all-to-all-start.6 = ((bf16[32,2,512]{2,1,0:T(2,128)(2,1)}), bf16[32,2,512]{2,1,0:T(2,128)(2,1)S(1)}, u32[]{:S(2)}, u32[]{:S(2)}) async-start(bf16[32,2,512]{2,1,0:T(2,128)(2,1)} %reshape.128), calls=%async_computation.6 | async-start | bytes 131072 | tf_op jit(solution)/shard_map/all_to_all | solution.py:68
  329.2 7.4 %all-to-all-done.6 = bf16[32,2,512]{2,1,0:T(2,128)(2,1)S(1)} async-done(((bf16[32,2,512]{2,1,0:T(2,128)(2,1)}), bf16[32,2,512]{2,1,0:T(2,128)(2,1)S(1)}, u32[]{:S(2)}, u32[]{:S(2)}) %all-to-all-start.6) | async-done | bytes 65568 | tf_op jit(solution)/shard_map/all_to_all | solution.py:68
  (42 shorter events, 19.0 us)
Async XLA Ops:
  7.2 1.2 copy-start
  7.2 161.2 %all-gather.2.cloned.1.call-start = ((), (), s32[]{:S(2)}) async-start(), calls=%async_computation.7 | async-start | bytes 8912896 | tf_op jit(solution)/shard_map/all_gather | solution.py:47
  11.3 29.6 %all-to-all-start = ((bf16[128,32,64]{0,2,1:T(8,128)(2,1)}), bf16[128,32,64]{0,2,1:T(8,128)(2,1)S(1)}, u32[]{:S(2)}, u32[]{:S(2)}) async-start(bf16[128,32,64]{0,2,1:T(8,128)(2,1)} %bitcast), calls=%async_computation | async-start | bytes 1048576 | tf_op jit(solution)/shard_map/all_to_all | solution.py:51
  40.9 22.2 %all-to-all-start.1 = ((bf16[128,32,64]{0,2,1:T(8,128)(2,1)}), bf16[128,32,64]{0,2,1:T(8,128)(2,1)S(1)}, u32[]{:S(2)}, u32[]{:S(2)}) async-start(bf16[128,32,64]{0,2,1:T(8,128)(2,1)} %bitcast.2), calls=%async_computation.1 | async-start | bytes 1048576 | tf_op jit(solution)/shard_map/all_to_all | solution.py:52
  63.1 21.9 %all-to-all-start.2 = ((bf16[128,32,64]{0,2,1:T(8,128)(2,1)}), bf16[128,32,64]{0,2,1:T(8,128)(2,1)S(1)}, u32[]{:S(2)}, u32[]{:S(2)}) async-start(bf16[128,32,64]{0,2,1:T(8,128)(2,1)} %bitcast.4), calls=%async_computation.2 | async-start | bytes 1048576 | tf_op jit(solution)/shard_map/all_to_all | solution.py:53
  168.4 102.5 %collective-permute-start = (bf16[2,1024,2048]{2,1,0:T(8,128)(2,1)}, bf16[2,1024,2048]{2,1,0:T(8,128)(2,1)}, u32[]{:S(2)}, u32[]{:S(2)}) collective-permute-start(bf16[2,1024,2048]{2,1,0:T(8,128)(2,1)} %all-gather.2.cloned.1.call-done), channel_id=1, source_target_pairs={{0,1},{1,0},{2,3},{3,2},{4,5},{5,4},{6,7},{7,6},{8,9},{9,8},{10,11... | collective-permute-start | bytes 25165832 | tf_op jit(solution)/shard_map/ppermute | solution.py:48
  173.2 71.3 %copy-start.1 = (bf16[1,16,2048]{2,1,0:T(8,128)(2,1)S(1)}, bf16[1,16,2048]{2,1,0:T(8,128)(2,1)}, u32[]{:S(2)}) copy-start(bf16[1,16,2048]{2,1,0:T(8,128)(2,1)} %param.11) | copy-start | bytes 196612
  236.8 24.4 %all-to-all-start.3 = ((bf16[32,128,64]{1,2,0:T(8,128)(2,1)}), bf16[32,128,64]{1,2,0:T(8,128)(2,1)S(1)}, u32[]{:S(2)}, u32[]{:S(2)}) async-start(bf16[32,128,64]{1,2,0:T(8,128)(2,1)} %copy.55), calls=%async_computation.3 | async-start | bytes 1048576 | tf_op jit(solution)/shard_map/all_to_all | solution.py:57
  261.2 16.4 %all-to-all-start.5 = ((bf16[32,2,512]{2,1,0:T(2,128)(2,1)}), bf16[32,2,512]{2,1,0:T(2,128)(2,1)S(1)}, u32[]{:S(2)}, u32[]{:S(2)}) async-start(bf16[32,2,512]{2,1,0:T(2,128)(2,1)} %reshape.126), calls=%async_computation.5 | async-start | bytes 131072 | tf_op jit(solution)/shard_map/all_to_all | solution.py:55
  277.6 36.5 %all-to-all-start.4 = ((bf16[128,2,2048]{0,1,2:T(2,128)(2,1)}), bf16[128,2,2048]{0,1,2:T(2,128)(2,1)S(1)}, u32[]{:S(2)}, u32[]{:S(2)}) async-start(bf16[128,2,2048]{0,1,2:T(2,128)(2,1)} %copy.58), calls=%async_computation.4 | async-start | bytes 2097152 | tf_op jit(solution)/shard_map/all_to_all | solution.py:64
  323.4 13.2 %all-to-all-start.6 = ((bf16[32,2,512]{2,1,0:T(2,128)(2,1)}), bf16[32,2,512]{2,1,0:T(2,128)(2,1)S(1)}, u32[]{:S(2)}, u32[]{:S(2)}) async-start(bf16[32,2,512]{2,1,0:T(2,128)(2,1)} %reshape.128), calls=%async_computation.6 | async-start | bytes 131072 | tf_op jit(solution)/shard_map/all_to_all | solution.py:68
Sparse Core Ops, SparseCore 0:
  11.1 157.2 all-gather.1

commit v2 on v1

v2 whole, which is shorter than its diff:
```python
import jax
import jax.numpy as jnp
from jax import lax
from jax.experimental import pallas as pl
from jax.experimental.pallas import tpu as pltpu
from jax.sharding import PartitionSpec as P

HEAD_DIM = 64


def _attend_kernel(len_ref, q_ref, k_ref, v_ref, o_ref):
    scores = lax.dot_general(
        q_ref[...], k_ref[...], (((1,), (1,)), ((), ())), preferred_element_type=jnp.float32
    ) * HEAD_DIM ** (-0.5)
    key_pos = lax.broadcasted_iota(jnp.int32, scores.shape, 1)
    scores = jnp.where(key_pos < len_ref[0], scores, -1e30)
    row_max = jnp.max(scores, axis=1, keepdims=True)
    weights = jnp.exp(scores - row_max)
    denominator = jnp.sum(weights, axis=1, keepdims=True)
    weighted = jnp.dot(weights.astype(jnp.bfloat16), v_ref[...], preferred_element_type=jnp.float32)
    o_ref[...] = (weighted / denominator).astype(o_ref.dtype)


def attend_head(queries, keys_in, values_in, length, block_rows=256):
    nq, width = queries.shape
    nk = keys_in.shape[0]
    block_rows = min(block_rows, nq)
    grid_spec = pltpu.PrefetchScalarGridSpec(
        num_scalar_prefetch=1,
        grid=(nq // block_rows,),
        in_specs=[
            pl.BlockSpec((block_rows, width), lambda i, n: (i, 0)),
            pl.BlockSpec((nk, width), lambda i, n: (0, 0)),
            pl.BlockSpec((nk, width), lambda i, n: (0, 0)),
        ],
        out_specs=pl.BlockSpec((block_rows, width), lambda i, n: (i, 0)),
    )
    cost = pl.CostEstimate(
        flops=4 * nq * nk * width,
        transcendentals=nq * nk,
        bytes_accessed=2 * (2 * nq * width + 2 * nk * width),
    )
    return pl.pallas_call(
        _attend_kernel,
        grid_spec=grid_spec,
        out_shape=jax.ShapeDtypeStruct((nq, width), jnp.bfloat16),
        cost_estimate=cost,
        compiler_params=pltpu.CompilerParams(vmem_limit_bytes=48 * 1024 * 1024),
    )(length.reshape(1), queries, keys_in, values_in)


def shards(enc_query, enc_key, enc_value, sum_query, doc_len, w_memory):
    length = doc_len[0]
    n_seq = lax.axis_size("seq")
    core = lax.axis_index("seq") % 2
    sibling = [(i, i ^ 1) for i in range(n_seq)]
    half = w_memory.shape[2] // 2
    w_half = lax.dynamic_slice_in_dim(w_memory, core * half, half, axis=2)
    w_half = lax.all_gather(w_half, "doc", axis=2, tiled=True)

    head_query, head_key, head_value = (
        lax.all_to_all(enc_query[0], "seq", split_axis=1, concat_axis=0, tiled=True),
        lax.all_to_all(enc_key[0], "seq", split_axis=1, concat_axis=0, tiled=True),
        lax.all_to_all(enc_value[0], "seq", split_axis=1, concat_axis=0, tiled=True),
    )
    summary_heads = lax.all_to_all(sum_query[0], "seq", split_axis=1, concat_axis=0, tiled=True)
    context = attend_head(head_query, head_key, head_value, length)
    encoder_out = lax.all_to_all(context, "seq", split_axis=0, concat_axis=1, tiled=True)

    enc_pair = jnp.concatenate([encoder_out, lax.ppermute(encoder_out, "seq", sibling)], axis=0)
    made = jnp.einsum("tf,kfc->tkc", enc_pair, w_half, preferred_element_type=jnp.float32)
    made = made.astype(jnp.bfloat16).reshape(2, encoder_out.shape[0], 2, -1, 1, half)
    own, received = made[0], lax.ppermute(made[1], "seq", sibling)
    memory_rows = jnp.where(core == 0, jnp.concatenate([own, received], axis=3),
                            jnp.concatenate([received, own], axis=3))
    memory_rows = memory_rows.reshape(encoder_out.shape[0], 2, -1)
    memory_local = lax.all_to_all(memory_rows, "seq", split_axis=2, concat_axis=0, tiled=True)
    memory_keys = memory_local[:, 0, :]
    memory_values = memory_local[:, 1, :]
    answer = attend_head(summary_heads, memory_keys, memory_values, length)
    summary_out = lax.all_to_all(answer, "seq", split_axis=0, concat_axis=1, tiled=True)
    return (encoder_out[None], summary_out[None])


def solution(mesh):
    in_specs = (
        P("doc", "seq", None),
        P("doc", "seq", None),
        P("doc", "seq", None),
        P("doc", "seq", None),
        P("doc"),
        P(None, None, "doc"),
    )
    out_specs = (P("doc", "seq", None), P("doc", "seq", None))
    return jax.shard_map(shards, mesh=mesh, in_specs=in_specs, out_specs=out_specs, check_vma=False)
```

time: 346 us -> 254 us (0.73)
  waiting for transfers between devices: 178 us -> 94 us
  matrix products: 53 us -> 5.74 us
  Pallas kernels: 0 us -> 36.3 us
  other arithmetic: 25.2 us -> 0.17 us
  blocking collectives: 0 us -> 20.7 us
  local copies, waits for them, and re-layouts: 20 us -> 31.7 us
  starting transfers between devices: 53.5 us -> 49.3 us
    all_gather x1, waiting for transfers between devices: 82.8 us -> 10.9 us  [shards(): w_half = lax.all_gather(w_half, 'doc', axis=2, tiled=True)]
    dot_general x20 -> x1, matrix products: 53 us -> 5.74 us  [shards(): jnp.einsum('tf,kfc->tkc', enc_pair, w_half, preferred_element_type=jnp.fl...]
    pallas_call x0 -> x2, Pallas kernels: none -> 36.3 us  [attend_head(): pl.pallas_call(_attend_kernel, grid_spec=grid_spec, out_shape=jax.ShapeDt...]
    all_to_all x0 -> x1, blocking collectives: none -> 20.7 us  [shards(): lax.all_to_all(context, 'seq', split_axis=0, concat_axis=1, tiled=True)]
    reduce_sum x9 -> x0, other arithmetic: 19.9 us -> none  [one_block(): denominator = jnp.sum(weights, axis=-1)]
    all_to_all x1 -> x0, waiting for transfers between devices: 15.7 us -> none  [shards(): lax.all_to_all(context, 'seq', split_axis=0, concat_axis=1, tiled=True)]
    select_n x0 -> x2, local copies, waits for them, and re-layouts: none -> 9.57 us  [shards(): jnp.where(core == 0, jnp.concatenate([own, received], axis=3), jnp.concat...]
    all_to_all x1 -> x0, starting transfers between devices: 7.65 us -> none  [shards(): lax.all_to_all(context, 'seq', split_axis=0, concat_axis=1, tiled=True)]
  transfers between devices with their start and end apart: 9 -> 9, of which waited for: 7 -> 7; matrix products, arithmetic and copies ran while one was open for 25% -> 8% of each run, Pallas kernels for 0% -> 13%
where the time goes in v2:
time: 254 us; the launch traced here: 253 us
  waiting for transfers between devices  94 us (37%)
  starting transfers between devices  49.3 us (19%)
  Pallas kernels  36.3 us (14%)
  local copies, waits for them, and re-layouts  31.7 us (12%)
  blocking collectives  20.7 us (8%)
  between operations  15 us (6%)
  matrix products  5.74 us (2%)
    pallas_call x2, Pallas kernels, attend_head(): pl.pallas_call(_attend_kernel, grid_spec=grid_spec, out_shape=jax.ShapeDt...  36.3 us
    all_to_all x1, waiting for transfers between devices, shards(): lax.all_to_all(memory_rows, 'seq', split_axis=2, concat_axis=0, tiled=True)  28 us
    all_to_all x1, blocking collectives, shards(): lax.all_to_all(context, 'seq', split_axis=0, concat_axis=1, tiled=True)  20.7 us
    all_to_all x1, waiting for transfers between devices, shards(): lax.all_to_all(enc_key[0], 'seq', split_axis=1, concat_axis=0, tiled=True)  16 us
    all_to_all x1, waiting for transfers between devices, shards(): lax.all_to_all(enc_query[0], 'seq', split_axis=1, concat_axis=0, tiled=True)  15.7 us
    all_to_all x1, waiting for transfers between devices, shards(): lax.all_to_all(enc_value[0], 'seq', split_axis=1, concat_axis=0, tiled=True)  14.5 us
    all_to_all x1, starting transfers between devices, shards(): lax.all_to_all(enc_query[0], 'seq', split_axis=1, concat_axis=0, tiled=True)  12.9 us
    all_gather x1, waiting for transfers between devices, shards(): w_half = lax.all_gather(w_half, 'doc', axis=2, tiled=True)  10.9 us
  transfers between devices with their start and end apart: 9, of which 7 were waited for; matrix products, arithmetic and copies ran while one was open for 8% of the time, Pallas kernels for 13%

profile of v2, /device:TPU:1, one launch (start us, length us, event | category | flops | bytes accessed | tf_op | source)
XLA Modules:
  0.0 252.8 jit_solution(16123072606492053540)
XLA Ops:
  7.2 1.2 copy-done
  8.4 0.4 constant_dynamic-slice_fusion
  8.8 1.1 copy.52
  9.9 1.0 copy.33
  10.9 12.9 %all-to-all-start = ((bf16[128,32,64]{0,2,1:T(8,128)(2,1)}), bf16[128,32,64]{0,2,1:T(8,128)(2,1)S(1)}, u32[]{:S(2)}, u32[]{:S(2)}) async-start(bf16[128,32,64]{0,2,1:T(8,128)(2,1)} %bitcast), calls=%async_computation | async-start | bytes 1048576 | tf_op jit(solution)/shard_map/all_to_all | solution.py:62
  23.9 1.0 copy.35
  24.9 15.7 %all-to-all-done = bf16[128,32,64]{0,2,1:T(8,128)(2,1)S(1)} async-done(((bf16[128,32,64]{0,2,1:T(8,128)(2,1)}), bf16[128,32,64]{0,2,1:T(8,128)(2,1)S(1)}, u32[]{:S(2)}, u32[]{:S(2)}) %all-to-all-start) | async-done | bytes 524320 | tf_op jit(solution)/shard_map/all_to_all | solution.py:62
  40.6 5.1 %all-to-all-start.1 = ((bf16[128,32,64]{0,2,1:T(8,128)(2,1)}), bf16[128,32,64]{0,2,1:T(8,128)(2,1)S(1)}, u32[]{:S(2)}, u32[]{:S(2)}) async-start(bf16[128,32,64]{0,2,1:T(8,128)(2,1)} %bitcast.3), calls=%async_computation.1 | async-start | bytes 1048576 | tf_op jit(solution)/shard_map/all_to_all | solution.py:63
  45.7 1.1 copy.37
  46.8 16.0 %all-to-all-done.1 = bf16[128,32,64]{0,2,1:T(8,128)(2,1)S(1)} async-done(((bf16[128,32,64]{0,2,1:T(8,128)(2,1)}), bf16[128,32,64]{0,2,1:T(8,128)(2,1)S(1)}, u32[]{:S(2)}, u32[]{:S(2)}) %all-to-all-start.1) | async-done | bytes 524320 | tf_op jit(solution)/shard_map/all_to_all | solution.py:63
  62.8 5.5 %all-to-all-start.2 = ((bf16[128,32,64]{0,2,1:T(8,128)(2,1)}), bf16[128,32,64]{0,2,1:T(8,128)(2,1)}, u32[]{:S(2)}, u32[]{:S(2)}) async-start(bf16[128,32,64]{0,2,1:T(8,128)(2,1)} %bitcast.6), calls=%async_computation.2 | async-start | bytes 1048576 | tf_op jit(solution)/shard_map/all_to_all | solution.py:64
  68.9 0.5 copy.34
  69.4 1.5 copy.36
  70.9 14.5 %all-to-all-done.2 = bf16[128,32,64]{0,2,1:T(8,128)(2,1)} async-done(((bf16[128,32,64]{0,2,1:T(8,128)(2,1)}), bf16[128,32,64]{0,2,1:T(8,128)(2,1)}, u32[]{:S(2)}, u32[]{:S(2)}) %all-to-all-start.2) | async-done | bytes 524320 | tf_op jit(solution)/shard_map/all_to_all | solution.py:64
  85.4 2.5 copy.38
  87.8 1.2 copy-done.1
  89.0 32.2 %shard_map.77 = bf16[4096,64]{1,0:T(8,128)(2,1)S(1)} custom-call(s32[1]{0:T(128)S(6)} %copy.55.len_ref, bf16[4096,64]{1,0:T(8,128)(2,1)S(1)} %bitcast.39, bf16[4096,64]{1,0:T(8,128)(2,1)S(1)} %bitcast.40, bf16[4096,64]{1,0:T(8,128)(2,1)S(1)} %bitcast.41), custom_call_target="tpu_custom_call" | custom-call | flops 4294967296 | bytes 2097152 | tf_op jit(solution)/shard_map/pallas_call | solution.py:43
  121.3 1.1 copy-done.2
  122.3 1.6 copy.39
  123.9 20.7 %all_to_all.129 = bf16[32,128,64]{1,2,0:T(8,128)(2,1)S(1)} all-to-all(bf16[32,128,64]{1,2,0:T(8,128)(2,1)S(1)} %copy.39), channel_id=1, replica_groups=mesh['doc'=16,'seq'=32] {'seq'}, dimensions={0} | all-to-all | bytes 1048576 | tf_op jit(solution)/shard_map/all_to_all | solution.py:68
  144.7 0.2 copy.42
  144.9 3.5 %collective-permute-start = (bf16[128,2048]{1,0:T(8,128)(2,1)S(1)}, bf16[128,2048]{1,0:T(8,128)(2,1)S(1)}, u32[]{:S(2)}, u32[]{:S(2)}) collective-permute-start(bf16[128,2048]{1,0:T(8,128)(2,1)S(1)} %copy.42), channel_id=1, source_target_pairs={{0,1},{1,0},{2,3},{3,2},{4,5},{5,4},{6,7},{7,6},{8,9},{9,8},{10,11... | collective-permute-start | bytes 1572872 | tf_op jit(solution)/shard_map/ppermute | solution.py:70
  148.4 1.5 collective-permute-done
  149.9 10.9 %all-gather.2.cloned.1.call-done = bf16[2,2048,1024]{1,2,0:T(8,128)(2,1)} async-done(((bf16[2,2048,64]{1,2,0:T(8,128)(2,1)}), bf16[2,2048,1024]{1,2,0:T(8,128)(2,1)}) %all-gather.2.cloned.1.call-update) | async-done | bytes 8388624 | tf_op jit(solution)/shard_map/all_gather | solution.py:59
  160.8 5.7 %convolution_convert_fusion = bf16[256,2,1024]{2,0,1:T(8,128)(2,1)S(1)} fusion(bf16[2,2048,1024]{1,2,0:T(8,128)(2,1)} %all-gather.2.cloned.1.call-done, bf16[128,2048]{1,0:T(8,128)(2,1)S(1)} %collective-permute-done, bf16[128,2048]{1,0:T(8,128)(2,1)S(1)} %copy.42), kind=kOutput, calls=%fused_computation | convolution fusion | flops 2150105088 | bytes 10485760 | tf_op jit(solution)/shard_map/tf,kfc->tkc/dot_general | solution.py:71
  166.5 0.1 fusion.3
  166.6 0.3 copy.45
  166.9 2.7 %collective-permute-start.1 = (bf16[128,2,16,1,64]{0,4,2,1,3:T(8,128)(2,1)S(1)}, bf16[128,2,16,1,64]{0,4,2,1,3:T(8,128)(2,1)S(1)}, u32[]{:S(2)}, u32[]{:S(2)}) collective-permute-start(bf16[128,2,16,1,64]{0,4,2,1,3:T(8,128)(2,1)S(1)} %bitcast.53), channel_id=1, source_target_pairs={{0,1},{1,0},{2,3},{3,2},{4,5},{5,4},{6,7},{7,6},{8,9},{9,8},{10,11... | collective-permute-start | bytes 1572872 | tf_op jit(solution)/shard_map/ppermute | solution.py:73
  169.6 0.2 all_to_all.110
  169.9 0.8 reshape.39
  170.6 6.6 %all-to-all-start.4 = ((bf16[32,2,512]{2,1,0:T(2,128)(2,1)}), bf16[32,2,512]{2,1,0:T(2,128)(2,1)S(1)}, u32[]{:S(2)}, u32[]{:S(2)}) async-start(bf16[32,2,512]{2,1,0:T(2,128)(2,1)} %reshape.39), calls=%async_computation.4 | async-start | bytes 131072 | tf_op jit(solution)/shard_map/all_to_all | solution.py:66
  177.2 0.3 copy.44
  177.5 0.2 maximum_select_fusion
  177.7 0.1 copy.46
  177.8 9.5 %copy.47 = bf16[128,2,2048]{0,1,2:T(2,128)(2,1)} copy(bf16[128,2,2048]{0,2,1:T(8,128)(2,1)S(1)} %bitcast.49) | data formatting | bytes 2097152 | tf_op jit(solution)/shard_map/jit(_where)/select_n | solution.py:74
  187.3 8.3 %all-to-all-start.5 = ((bf16[128,2,2048]{0,1,2:T(2,128)(2,1)}), bf16[128,2,2048]{0,1,2:T(2,128)(2,1)S(1)}, u32[]{:S(2)}, u32[]{:S(2)}) async-start(bf16[128,2,2048]{0,1,2:T(2,128)(2,1)} %copy.47), calls=%async_computation.5 | async-start | bytes 2097152 | tf_op jit(solution)/shard_map/all_to_all | solution.py:77
  195.6 0.1 reshape.40
  195.7 28.0 %all-to-all-done.5 = bf16[128,2,2048]{0,1,2:T(2,128)(2,1)S(1)} async-done(((bf16[128,2,2048]{0,1,2:T(2,128)(2,1)}), bf16[128,2,2048]{0,1,2:T(2,128)(2,1)S(1)}, u32[]{:S(2)}, u32[]{:S(2)}) %all-to-all-start.5) | async-done | bytes 1048608 | tf_op jit(solution)/shard_map/all_to_all | solution.py:77
  223.7 1.1 copy.48
  224.8 2.0 copy.49
  226.9 0.1 slice_bitcast_fusion
  227.0 4.1 %shard_map.78 = bf16[512,64]{1,0:T(8,128)(2,1)S(1)} custom-call(s32[1]{0:T(128)S(6)} %copy.55.len_ref, bf16[512,64]{1,0:T(8,128)(2,1)S(1)} %bitcast.43, bf16[4096,64]{1,0:T(8,128)(2,1)S(1)} %get-tuple-element.7.k_ref, bf16[4096,64]{1,0:T(8,128)(2,1)S(1)} %get-tuple-element.6.v_ref), custom_call_target="tpu_custom_call" | custom-call | flops 536870912 | bytes 1179648 | tf_op jit(solution)/shard_map/pallas_call | solution.py:43
  231.1 0.8 reshape.41
  231.9 4.7 %all-to-all-start.6 = ((bf16[32,2,512]{2,1,0:T(2,128)(2,1)}), bf16[32,2,512]{2,1,0:T(2,128)(2,1)S(1)}, u32[]{:S(2)}, u32[]{:S(2)}) async-start(bf16[32,2,512]{2,1,0:T(2,128)(2,1)} %reshape.41), calls=%async_computation.6 | async-start | bytes 131072 | tf_op jit(solution)/shard_map/all_to_all | solution.py:81
  236.6 1.0 copy.51
  237.6 7.4 %all-to-all-done.6 = bf16[32,2,512]{2,1,0:T(2,128)(2,1)S(1)} async-done(((bf16[32,2,512]{2,1,0:T(2,128)(2,1)}), bf16[32,2,512]{2,1,0:T(2,128)(2,1)S(1)}, u32[]{:S(2)}, u32[]{:S(2)}) %all-to-all-start.6) | async-done | bytes 65568 | tf_op jit(solution)/shard_map/all_to_all | solution.py:81
  245.0 0.1 reshape.42
  245.2 0.8 broadcast_in_dim.7
  (23 shorter events, 0.2 us)
Async XLA Ops:
  7.2 1.2 copy-start
  7.2 153.6 %all-gather.2.cloned.1.call-start = ((), (), s32[]{:S(2)}) async-start(), calls=%async_computation.7 | async-start | bytes 8912896 | tf_op jit(solution)/shard_map/all_gather | solution.py:59
  8.4 1.5 copy-start.6
  8.8 15.1 %copy-start.7 = (bf16[1,128,2048]{2,1,0:T(8,128)(2,1)S(1)}, bf16[1,128,2048]{2,1,0:T(8,128)(2,1)}, u32[]{:S(2)}) copy-start(bf16[1,128,2048]{2,1,0:T(8,128)(2,1)} %param.7) | copy-start | bytes 1572868
  9.9 35.7 %copy-start.8 = (bf16[1,128,2048]{2,1,0:T(8,128)(2,1)S(1)}, bf16[1,128,2048]{2,1,0:T(8,128)(2,1)}, u32[]{:S(2)}) copy-start(bf16[1,128,2048]{2,1,0:T(8,128)(2,1)} %param.8) | copy-start | bytes 1572868
  10.9 29.6 %all-to-all-start = ((bf16[128,32,64]{0,2,1:T(8,128)(2,1)}), bf16[128,32,64]{0,2,1:T(8,128)(2,1)S(1)}, u32[]{:S(2)}, u32[]{:S(2)}) async-start(bf16[128,32,64]{0,2,1:T(8,128)(2,1)} %bitcast), calls=%async_computation | async-start | bytes 1048576 | tf_op jit(solution)/shard_map/all_to_all | solution.py:62
  40.6 22.2 %all-to-all-start.1 = ((bf16[128,32,64]{0,2,1:T(8,128)(2,1)}), bf16[128,32,64]{0,2,1:T(8,128)(2,1)S(1)}, u32[]{:S(2)}, u32[]{:S(2)}) async-start(bf16[128,32,64]{0,2,1:T(8,128)(2,1)} %bitcast.3), calls=%async_computation.1 | async-start | bytes 1048576 | tf_op jit(solution)/shard_map/all_to_all | solution.py:63
  62.7 6.6 %copy-start.5 = (bf16[128,32,64]{0,2,1:T(8,128)(2,1)}, bf16[128,32,64]{0,2,1:T(8,128)(2,1)S(1)}, u32[]{:S(2)}) copy-start(bf16[128,32,64]{0,2,1:T(8,128)(2,1)S(1)} %all-to-all-done.1) | copy-start | bytes 1572868
  62.8 22.6 %all-to-all-start.2 = ((bf16[128,32,64]{0,2,1:T(8,128)(2,1)}), bf16[128,32,64]{0,2,1:T(8,128)(2,1)}, u32[]{:S(2)}, u32[]{:S(2)}) async-start(bf16[128,32,64]{0,2,1:T(8,128)(2,1)} %bitcast.6), calls=%async_computation.2 | async-start | bytes 1048576 | tf_op jit(solution)/shard_map/all_to_all | solution.py:64
  87.8 1.2 copy-start.1
  121.3 1.1 copy-start.2
  144.7 21.8 %copy-start.3 = (bf16[32,128,64]{1,2,0:T(8,128)(2,1)}, bf16[32,128,64]{1,2,0:T(8,128)(2,1)S(1)}, u32[]{:S(2)}) copy-start(bf16[32,128,64]{1,2,0:T(8,128)(2,1)S(1)} %all_to_all.129) | copy-start | bytes 1572868
  144.9 5.0 %collective-permute-start = (bf16[128,2048]{1,0:T(8,128)(2,1)S(1)}, bf16[128,2048]{1,0:T(8,128)(2,1)S(1)}, u32[]{:S(2)}, u32[]{:S(2)}) collective-permute-start(bf16[128,2048]{1,0:T(8,128)(2,1)S(1)} %copy.42), channel_id=1, source_target_pairs={{0,1},{1,0},{2,3},{3,2},{4,5},{5,4},{6,7},{7,6},{8,9},{9,8},{10,11... | collective-permute-start | bytes 1572872 | tf_op jit(solution)/shard_map/ppermute | solution.py:70
  166.5 3.1 %copy-start.9 = (bf16[1,16,2048]{2,1,0:T(8,128)(2,1)S(1)}, bf16[1,16,2048]{2,1,0:T(8,128)(2,1)}, u32[]{:S(2)}) copy-start(bf16[1,16,2048]{2,1,0:T(8,128)(2,1)} %param.9) | copy-start | bytes 196612
  166.9 10.6 %collective-permute-start.1 = (bf16[128,2,16,1,64]{0,4,2,1,3:T(8,128)(2,1)S(1)}, bf16[128,2,16,1,64]{0,4,2,1,3:T(8,128)(2,1)S(1)}, u32[]{:S(2)}, u32[]{:S(2)}) collective-permute-start(bf16[128,2,16,1,64]{0,4,2,1,3:T(8,128)(2,1)S(1)} %bitcast.53), channel_id=1, source_target_pairs={{0,1},{1,0},{2,3},{3,2},{4,5},{5,4},{6,7},{7,6},{8,9},{9,8},{10,11... | collective-permute-start | bytes 1572872 | tf_op jit(solution)/shard_map/ppermute | solution.py:73
  170.6 16.6 %all-to-all-start.4 = ((bf16[32,2,512]{2,1,0:T(2,128)(2,1)}), bf16[32,2,512]{2,1,0:T(2,128)(2,1)S(1)}, u32[]{:S(2)}, u32[]{:S(2)}) async-start(bf16[32,2,512]{2,1,0:T(2,128)(2,1)} %reshape.39), calls=%async_computation.4 | async-start | bytes 131072 | tf_op jit(solution)/shard_map/all_to_all | solution.py:66
  187.3 36.4 %all-to-all-start.5 = ((bf16[128,2,2048]{0,1,2:T(2,128)(2,1)}), bf16[128,2,2048]{0,1,2:T(2,128)(2,1)S(1)}, u32[]{:S(2)}, u32[]{:S(2)}) async-start(bf16[128,2,2048]{0,1,2:T(2,128)(2,1)} %copy.47), calls=%async_computation.5 | async-start | bytes 2097152 | tf_op jit(solution)/shard_map/all_to_all | solution.py:77
  227.0 9.6 %copy-start.4 = (bf16[32,128,64]{1,2,0:T(8,128)(2,1)S(1)}, bf16[32,128,64]{1,2,0:T(8,128)(2,1)}, u32[]{:S(2)}) copy-start(bf16[32,128,64]{1,2,0:T(8,128)(2,1)} %copy-done.3) | copy-start | bytes 1572868
  231.9 13.1 %all-to-all-start.6 = ((bf16[32,2,512]{2,1,0:T(2,128)(2,1)}), bf16[32,2,512]{2,1,0:T(2,128)(2,1)S(1)}, u32[]{:S(2)}, u32[]{:S(2)}) async-start(bf16[32,2,512]{2,1,0:T(2,128)(2,1)} %reshape.41), calls=%async_computation.6 | async-start | bytes 131072 | tf_op jit(solution)/shard_map/all_to_all | solution.py:81
Sparse Core Ops, SparseCore 0:
  11.2 149.5 all-gather.1

commit v3 on v2

--- a/solution.py
+++ b/solution.py
@@ -55,8 +55,10 @@
     core = lax.axis_index("seq") % 2
     sibling = [(i, i ^ 1) for i in range(n_seq)]
     half = w_memory.shape[2] // 2
-    w_half = lax.dynamic_slice_in_dim(w_memory, core * half, half, axis=2)
-    w_half = lax.all_gather(w_half, "doc", axis=2, tiled=True)
+    w_halves = [
+        lax.all_gather(lax.dynamic_slice_in_dim(w_memory[m], core * half, half, axis=1), "doc", axis=1, tiled=True)
+        for m in range(2)
+    ]
 
     head_query, head_key, head_value = (
         lax.all_to_all(enc_query[0], "seq", split_axis=1, concat_axis=0, tiled=True),
@@ -67,16 +69,17 @@
     context = attend_head(head_query, head_key, head_value, length)
     encoder_out = lax.all_to_all(context, "seq", split_axis=0, concat_axis=1, tiled=True)
 
+    rows = encoder_out.shape[0]
     enc_pair = jnp.concatenate([encoder_out, lax.ppermute(encoder_out, "seq", sibling)], axis=0)
-    made = jnp.einsum("tf,kfc->tkc", enc_pair, w_half, preferred_element_type=jnp.float32)
-    made = made.astype(jnp.bfloat16).reshape(2, encoder_out.shape[0], 2, -1, 1, half)
-    own, received = made[0], lax.ppermute(made[1], "seq", sibling)
-    memory_rows = jnp.where(core == 0, jnp.concatenate([own, received], axis=3),
-                            jnp.concatenate([received, own], axis=3))
-    memory_rows = memory_rows.reshape(encoder_out.shape[0], 2, -1)
-    memory_local = lax.all_to_all(memory_rows, "seq", split_axis=2, concat_axis=0, tiled=True)
-    memory_keys = memory_local[:, 0, :]
-    memory_values = memory_local[:, 1, :]
+    memory = []
+    for w_half in w_halves:
+        made = jnp.dot(enc_pair, w_half, preferred_element_type=jnp.float32).astype(jnp.bfloat16)
+        made = made.reshape(2, rows, -1, half).transpose(0, 2, 1, 3)
+        own, received = made[0], lax.ppermute(made[1], "seq", sibling)
+        by_head = jnp.where(core == 0, jnp.stack([own, received], axis=1), jnp.stack([received, own], axis=1))
+        by_head = by_head.reshape(n_seq, rows, half)
+        memory.append(lax.all_to_all(by_head, "seq", split_axis=0, concat_axis=0, tiled=True).reshape(-1, half))
+    memory_keys, memory_values = memory
     answer = attend_head(summary_heads, memory_keys, memory_values, length)
     summary_out = lax.all_to_all(answer, "seq", split_axis=0, concat_axis=1, tiled=True)
     return (encoder_out[None], summary_out[None])

time: 254 us -> 294 us (1.16)
  waiting for transfers between devices: 94 us -> 137 us
  local copies, waits for them, and re-layouts: 31.7 us -> 20.8 us
  starting transfers between devices: 49.3 us -> 54.7 us
    all_gather x1 -> x2, waiting for transfers between devices: 10.9 us -> 57.2 us  [shards(): lax.all_gather(lax.dynamic_slice_in_dim(w_memory[m], core * half, half, a...]
    all_to_all x1 -> x2, waiting for transfers between devices: 28 us -> 16.1 us  [shards(): lax.all_to_all(by_head, 'seq', split_axis=0, concat_axis=0, tiled=True)]
    select_n x2 -> x0, local copies, waits for them, and re-layouts: 9.57 us -> none  [shards(): jnp.where(core == 0, jnp.concatenate([own, received], axis=3), jnp.concat...]
    all_to_all x1, waiting for transfers between devices: 0.01 us -> 7.53 us  [shards(): lax.all_to_all(sum_query[0], 'seq', split_axis=1, concat_axis=0, tiled=True)]
    ppermute x1 -> x2, starting transfers between devices: 2.74 us -> 8.1 us  [shards(): own, received = (made[0], lax.ppermute(made[1], 'seq', sibling))]
    all_to_all x1 -> x2, starting transfers between devices: 8.27 us -> 10.8 us  [shards(): lax.all_to_all(by_head, 'seq', split_axis=0, concat_axis=0, tiled=True)]
    dot_general x1 -> x2, matrix products: 5.74 us -> 6.98 us  [shards(): jnp.dot(enc_pair, w_half, preferred_element_type=jnp.float32)]
    unnamed x29 -> x24, local copies, waits for them, and re-layouts: 10.5 us -> 9.88 us
  transfers between devices with their start and end apart: 9 -> 12, of which waited for: 7 -> 9; matrix products, arithmetic and copies ran while one was open for 8% -> 8% of each run, Pallas kernels for 13% -> 11%
where the time goes in v3:
time: 294 us; the launch traced here: 293 us
  waiting for transfers between devices  137 us (47%)
  starting transfers between devices  54.7 us (19%)
  Pallas kernels  36.3 us (12%)
  local copies, waits for them, and re-layouts  20.8 us (7%)
  blocking collectives  20.8 us (7%)
  between operations  15 us (5%)
  matrix products  6.98 us (2%)
    all_gather x2, waiting for transfers between devices, shards(): lax.all_gather(lax.dynamic_slice_in_dim(w_memory[m], core * half, half, a...  57.2 us
    pallas_call x2, Pallas kernels, attend_head(): pl.pallas_call(_attend_kernel, grid_spec=grid_spec, out_shape=jax.ShapeDt...  36.3 us
    all_to_all x1, blocking collectives, shards(): lax.all_to_all(context, 'seq', split_axis=0, concat_axis=1, tiled=True)  20.8 us
    all_to_all x2, waiting for transfers between devices, shards(): lax.all_to_all(by_head, 'seq', split_axis=0, concat_axis=0, tiled=True)  16.1 us
    all_to_all x1, waiting for transfers between devices, shards(): lax.all_to_all(enc_key[0], 'seq', split_axis=1, concat_axis=0, tiled=True)  16.1 us
    all_to_all x1, waiting for transfers between devices, shards(): lax.all_to_all(enc_query[0], 'seq', split_axis=1, concat_axis=0, tiled=True)  15.6 us
    all_to_all x1, waiting for transfers between devices, shards(): lax.all_to_all(enc_value[0], 'seq', split_axis=1, concat_axis=0, tiled=True)  15.5 us
    all_to_all x1, starting transfers between devices, shards(): lax.all_to_all(enc_query[0], 'seq', split_axis=1, concat_axis=0, tiled=True)  12.9 us
  transfers between devices with their start and end apart: 12, of which 9 were waited for; matrix products, arithmetic and copies ran while one was open for 8% of the time, Pallas kernels for 11%

profile of v3, /device:TPU:1, one launch (start us, length us, event | category | flops | bytes accessed | tf_op | source)
XLA Modules:
  0.0 293.2 jit_solution(477748186087953514)
XLA Ops:
  7.2 1.3 fusion.12
  8.6 0.2 constant_dynamic-slice_fusion
  8.8 0.9 copy.86
  9.8 0.2 constant_dynamic-slice_fusion.1
  10.0 0.9 copy.84
  11.0 1.0 copy.62
  12.0 12.9 %all-to-all-start = ((bf16[128,32,64]{0,2,1:T(8,128)(2,1)}), bf16[128,32,64]{0,2,1:T(8,128)(2,1)S(1)}, u32[]{:S(2)}, u32[]{:S(2)}) async-start(bf16[128,32,64]{0,2,1:T(8,128)(2,1)} %bitcast), calls=%async_computation | async-start | bytes 1048576 | tf_op jit(solution)/shard_map/all_to_all | solution.py:64
  24.9 1.1 copy.64
  26.0 15.6 %all-to-all-done = bf16[128,32,64]{0,2,1:T(8,128)(2,1)S(1)} async-done(((bf16[128,32,64]{0,2,1:T(8,128)(2,1)}), bf16[128,32,64]{0,2,1:T(8,128)(2,1)S(1)}, u32[]{:S(2)}, u32[]{:S(2)}) %all-to-all-start) | async-done | bytes 524320 | tf_op jit(solution)/shard_map/all_to_all | solution.py:64
  41.6 5.1 %all-to-all-start.1 = ((bf16[128,32,64]{0,2,1:T(8,128)(2,1)}), bf16[128,32,64]{0,2,1:T(8,128)(2,1)S(1)}, u32[]{:S(2)}, u32[]{:S(2)}) async-start(bf16[128,32,64]{0,2,1:T(8,128)(2,1)} %bitcast.3), calls=%async_computation.1 | async-start | bytes 1048576 | tf_op jit(solution)/shard_map/all_to_all | solution.py:65
  46.7 1.0 copy.66
  47.7 16.1 %all-to-all-done.1 = bf16[128,32,64]{0,2,1:T(8,128)(2,1)S(1)} async-done(((bf16[128,32,64]{0,2,1:T(8,128)(2,1)}), bf16[128,32,64]{0,2,1:T(8,128)(2,1)S(1)}, u32[]{:S(2)}, u32[]{:S(2)}) %all-to-all-start.1) | async-done | bytes 524320 | tf_op jit(solution)/shard_map/all_to_all | solution.py:65
  63.8 5.5 %all-to-all-start.2 = ((bf16[128,32,64]{0,2,1:T(8,128)(2,1)}), bf16[128,32,64]{0,2,1:T(8,128)(2,1)}, u32[]{:S(2)}, u32[]{:S(2)}) async-start(bf16[128,32,64]{0,2,1:T(8,128)(2,1)} %bitcast.6), calls=%async_computation.2 | async-start | bytes 1048576 | tf_op jit(solution)/shard_map/all_to_all | solution.py:66
  69.9 0.5 copy.63
  70.4 0.5 copy.65
  70.9 15.5 %all-to-all-done.2 = bf16[128,32,64]{0,2,1:T(8,128)(2,1)} async-done(((bf16[128,32,64]{0,2,1:T(8,128)(2,1)}), bf16[128,32,64]{0,2,1:T(8,128)(2,1)}, u32[]{:S(2)}, u32[]{:S(2)}) %all-to-all-start.2) | async-done | bytes 524320 | tf_op jit(solution)/shard_map/all_to_all | solution.py:66
  86.4 1.5 copy.67
  87.9 32.2 %shard_map.77 = bf16[4096,64]{1,0:T(8,128)(2,1)S(1)} custom-call(s32[1]{0:T(128)S(6)} %copy.93.len_ref, bf16[4096,64]{1,0:T(8,128)(2,1)S(1)} %bitcast.54, bf16[4096,64]{1,0:T(8,128)(2,1)S(1)} %bitcast.56, bf16[4096,64]{1,0:T(8,128)(2,1)S(1)} %bitcast.58), custom_call_target="tpu_custom_call" | custom-call | flops 4294967296 | bytes 2097152 | tf_op jit(solution)/shard_map/pallas_call | solution.py:43
  120.2 1.0 copy-done
  121.2 1.6 copy.68
  122.8 20.8 %all_to_all.121 = bf16[32,128,64]{1,2,0:T(8,128)(2,1)S(1)} all-to-all(bf16[32,128,64]{1,2,0:T(8,128)(2,1)S(1)} %copy.68), channel_id=1, replica_groups=mesh['doc'=16,'seq'=32] {'seq'}, dimensions={0} | all-to-all | bytes 1048576 | tf_op jit(solution)/shard_map/all_to_all | solution.py:70
  143.5 3.6 %collective-permute-start = (bf16[128,2048]{0,1:T(8,128)(2,1)S(1)}, bf16[128,2048]{0,1:T(8,128)(2,1)S(1)}, u32[]{:S(2)}, u32[]{:S(2)}) collective-permute-start(bf16[128,2048]{0,1:T(8,128)(2,1)S(1)} %bitcast.66), channel_id=1, source_target_pairs={{0,1},{1,0},{2,3},{3,2},{4,5},{5,4},{6,7},{7,6},{8,9},{9,8},{10,11... | collective-permute-start | bytes 1572872 | tf_op jit(solution)/shard_map/ppermute | solution.py:73
  147.1 1.5 collective-permute-done
  148.6 3.5 %fusion.7 = bf16[256,1024]{1,0:T(8,128)(2,1)S(1)} fusion(bf16[1,2048,1024]{1,2,0:T(8,128)(2,1)} %all-gather.7.cloned.1.call-done, bf16[128,2048]{0,1:T(8,128)(2,1)S(1)} %collective-permute-done, bf16[128,2048]{0,1:T(8,128)(2,1)S(1)} %bitcast.67), kind=kOutput, calls=%fused_computation.5 | convolution fusion | flops 1076101120 | bytes 5767168 | tf_op jit(solution)/shard_map/dot_general | solution.py:76
  152.1 0.7 reshape.58
  152.8 0.9 copy.75
  153.7 2.3 collective-permute-start.2
  156.3 0.8 reshape.59
  157.0 3.6 %all-to-all-start.4 = ((bf16[32,2,512]{2,1,0:T(2,128)(2,1)}), bf16[32,2,512]{2,1,0:T(2,128)(2,1)S(1)}, u32[]{:S(2)}, u32[]{:S(2)}) async-start(bf16[32,2,512]{2,1,0:T(2,128)(2,1)} %reshape.59), calls=%async_computation.4 | async-start | bytes 131072 | tf_op jit(solution)/shard_map/all_to_all | solution.py:68
  160.7 0.9 maximum_select_fusion.1
  161.6 7.5 %all-to-all-done.4 = bf16[32,2,512]{2,1,0:T(2,128)(2,1)S(1)} async-done(((bf16[32,2,512]{2,1,0:T(2,128)(2,1)}), bf16[32,2,512]{2,1,0:T(2,128)(2,1)S(1)}, u32[]{:S(2)}, u32[]{:S(2)}) %all-to-all-start.4) | async-done | bytes 65568 | tf_op jit(solution)/shard_map/all_to_all | solution.py:68
  169.1 3.9 %all-to-all-start.6 = ((bf16[32,128,64]{1,2,0:T(8,128)(2,1)}), bf16[32,128,64]{1,2,0:T(8,128)(2,1)S(1)}, u32[]{:S(2)}, u32[]{:S(2)}) async-start(bf16[32,128,64]{1,2,0:T(8,128)(2,1)} %bitcast.26), calls=%async_computation.6 | async-start | bytes 1048576 | tf_op jit(solution)/shard_map/all_to_all | solution.py:81
  173.0 57.2 %all-gather.5.cloned.1.call-done = bf16[1,2048,1024]{1,2,0:T(8,128)(2,1)} async-done(((bf16[1,2048,64]{1,2,0:T(8,128)(2,1)}), bf16[1,2048,1024]{1,2,0:T(8,128)(2,1)}) %all-gather.5.cloned.1.call-update) | async-done | bytes 4194320 | tf_op jit(solution)/shard_map/all_gather | solution.py:59
  230.2 3.5 %fusion.4 = bf16[256,1024]{1,0:T(8,128)(2,1)S(1)} fusion(bf16[1,2048,1024]{1,2,0:T(8,128)(2,1)} %all-gather.5.cloned.1.call-done, bf16[128,2048]{0,1:T(8,128)(2,1)S(1)} %collective-permute-done, bf16[128,2048]{0,1:T(8,128)(2,1)S(1)} %bitcast.68), kind=kOutput, calls=%fused_computation.4 | convolution fusion | flops 1076101120 | bytes 5767168 | tf_op jit(solution)/shard_map/dot_general | solution.py:76
  234.1 1.1 fusion.13
  235.2 5.8 %collective-permute-start.1 = (bf16[16,128,64]{1,2,0:T(8,128)(2,1)S(1)}, bf16[16,128,64]{1,2,0:T(8,128)(2,1)S(1)}, u32[]{:S(2)}, u32[]{:S(2)}) collective-permute-start(bf16[16,128,64]{1,2,0:T(8,128)(2,1)S(1)} %bitcast.73), channel_id=1, source_target_pairs={{0,1},{1,0},{2,3},{3,2},{4,5},{5,4},{6,7},{7,6},{8,9},{9,8},{10,11... | collective-permute-start | bytes 786440 | tf_op jit(solution)/shard_map/ppermute | solution.py:78
  241.1 1.1 collective-permute-done.1
  242.2 0.8 maximum_select_fusion
  243.0 6.8 %all-to-all-start.5 = ((bf16[32,128,64]{1,2,0:T(8,128)(2,1)}), bf16[32,128,64]{1,2,0:T(8,128)(2,1)S(1)}, u32[]{:S(2)}, u32[]{:S(2)}) async-start(bf16[32,128,64]{1,2,0:T(8,128)(2,1)} %bitcast.19), calls=%async_computation.5 | async-start | bytes 1048576 | tf_op jit(solution)/shard_map/all_to_all | solution.py:81
  250.0 0.5 copy.76
  250.5 16.1 %all-to-all-done.5 = bf16[32,128,64]{1,2,0:T(8,128)(2,1)S(1)} async-done(((bf16[32,128,64]{1,2,0:T(8,128)(2,1)}), bf16[32,128,64]{1,2,0:T(8,128)(2,1)S(1)}, u32[]{:S(2)}, u32[]{:S(2)}) %all-to-all-start.5) | async-done | bytes 524320 | tf_op jit(solution)/shard_map/all_to_all | solution.py:81
  266.6 0.5 copy.72
  267.1 4.1 %shard_map.78 = bf16[512,64]{1,0:T(8,128)(2,1)S(1)} custom-call(s32[1]{0:T(128)S(6)} %copy.93.len_ref, bf16[512,64]{1,0:T(8,128)(2,1)S(1)} %bitcast.60, bf16[4096,64]{1,0:T(8,128)(2,1)S(1)} %bitcast.57, bf16[4096,64]{1,0:T(8,128)(2,1)S(1)} %bitcast.55), custom_call_target="tpu_custom_call" | custom-call | flops 536870912 | bytes 1179648 | tf_op jit(solution)/shard_map/pallas_call | solution.py:43
  271.1 0.8 reshape.61
  271.9 5.1 %all-to-all-start.7 = ((bf16[32,2,512]{2,1,0:T(2,128)(2,1)}), bf16[32,2,512]{2,1,0:T(2,128)(2,1)S(1)}, u32[]{:S(2)}, u32[]{:S(2)}) async-start(bf16[32,2,512]{2,1,0:T(2,128)(2,1)} %reshape.61), calls=%async_computation.7 | async-start | bytes 131072 | tf_op jit(solution)/shard_map/all_to_all | solution.py:84
  277.0 2.0 copy.78
  279.0 6.4 %all-to-all-done.7 = bf16[32,2,512]{2,1,0:T(2,128)(2,1)S(1)} async-done(((bf16[32,2,512]{2,1,0:T(2,128)(2,1)}), bf16[32,2,512]{2,1,0:T(2,128)(2,1)S(1)}, u32[]{:S(2)}, u32[]{:S(2)}) %all-to-all-start.7) | async-done | bytes 65568 | tf_op jit(solution)/shard_map/all_to_all | solution.py:84
  285.6 0.8 broadcast_in_dim.7
  (28 shorter events, 1.1 us)
Async XLA Ops:
  7.2 3.8 %copy-start.2 = (bf16[1,128,2048]{2,1,0:T(8,128)(2,1)S(1)}, bf16[1,128,2048]{2,1,0:T(8,128)(2,1)}, u32[]{:S(2)}) copy-start(bf16[1,128,2048]{2,1,0:T(8,128)(2,1)} %param.6) | copy-start | bytes 1572868
  7.2 141.5 %all-gather.7.cloned.1.call-start = ((), (), s32[]{:S(2)}) async-start(), calls=%async_computation.9 | async-start | bytes 4456448 | tf_op jit(solution)/shard_map/all_gather | solution.py:59
  7.2 17.6 %copy-start.3 = (bf16[1,128,2048]{2,1,0:T(8,128)(2,1)S(1)}, bf16[1,128,2048]{2,1,0:T(8,128)(2,1)}, u32[]{:S(2)}) copy-start(bf16[1,128,2048]{2,1,0:T(8,128)(2,1)} %param.7) | copy-start | bytes 1572868
  8.6 38.1 %copy-start.4 = (bf16[1,128,2048]{2,1,0:T(8,128)(2,1)S(1)}, bf16[1,128,2048]{2,1,0:T(8,128)(2,1)}, u32[]{:S(2)}) copy-start(bf16[1,128,2048]{2,1,0:T(8,128)(2,1)} %param.8) | copy-start | bytes 1572868
  9.8 220.5 %all-gather.5.cloned.1.call-start = ((), (), s32[]{:S(2)}) async-start(), calls=%async_computation.8 | async-start | bytes 4456448 | tf_op jit(solution)/shard_map/all_gather | solution.py:59
  12.0 29.6 %all-to-all-start = ((bf16[128,32,64]{0,2,1:T(8,128)(2,1)}), bf16[128,32,64]{0,2,1:T(8,128)(2,1)S(1)}, u32[]{:S(2)}, u32[]{:S(2)}) async-start(bf16[128,32,64]{0,2,1:T(8,128)(2,1)} %bitcast), calls=%async_computation | async-start | bytes 1048576 | tf_op jit(solution)/shard_map/all_to_all | solution.py:64
  41.6 22.2 %all-to-all-start.1 = ((bf16[128,32,64]{0,2,1:T(8,128)(2,1)}), bf16[128,32,64]{0,2,1:T(8,128)(2,1)S(1)}, u32[]{:S(2)}, u32[]{:S(2)}) async-start(bf16[128,32,64]{0,2,1:T(8,128)(2,1)} %bitcast.3), calls=%async_computation.1 | async-start | bytes 1048576 | tf_op jit(solution)/shard_map/all_to_all | solution.py:65
  63.8 22.6 %all-to-all-start.2 = ((bf16[128,32,64]{0,2,1:T(8,128)(2,1)}), bf16[128,32,64]{0,2,1:T(8,128)(2,1)}, u32[]{:S(2)}, u32[]{:S(2)}) async-start(bf16[128,32,64]{0,2,1:T(8,128)(2,1)} %bitcast.6), calls=%async_computation.2 | async-start | bytes 1048576 | tf_op jit(solution)/shard_map/all_to_all | solution.py:66
  120.1 1.0 copy-start
  143.5 86.7 %copy-start.1 = (bf16[32,128,64]{1,2,0:T(8,128)(2,1)}, bf16[32,128,64]{1,2,0:T(8,128)(2,1)S(1)}, u32[]{:S(2)}) copy-start(bf16[32,128,64]{1,2,0:T(8,128)(2,1)S(1)} %all_to_all.121) | copy-start | bytes 1572868
  143.5 12.5 %copy-start.5 = (bf16[1,16,2048]{2,1,0:T(8,128)(2,1)S(1)}, bf16[1,16,2048]{2,1,0:T(8,128)(2,1)}, u32[]{:S(2)}) copy-start(bf16[1,16,2048]{2,1,0:T(8,128)(2,1)} %param.9) | copy-start | bytes 196612
  143.5 5.1 %collective-permute-start = (bf16[128,2048]{0,1:T(8,128)(2,1)S(1)}, bf16[128,2048]{0,1:T(8,128)(2,1)S(1)}, u32[]{:S(2)}, u32[]{:S(2)}) collective-permute-start(bf16[128,2048]{0,1:T(8,128)(2,1)S(1)} %bitcast.66), channel_id=1, source_target_pairs={{0,1},{1,0},{2,3},{3,2},{4,5},{5,4},{6,7},{7,6},{8,9},{9,8},{10,11... | collective-permute-start | bytes 1572872 | tf_op jit(solution)/shard_map/ppermute | solution.py:73
  153.7 7.0 %collective-permute-start.2 = (bf16[16,128,64]{1,2,0:T(8,128)(2,1)S(1)}, bf16[16,128,64]{1,2,0:T(8,128)(2,1)S(1)}, u32[]{:S(2)}, u32[]{:S(2)}) collective-permute-start(bf16[16,128,64]{1,2,0:T(8,128)(2,1)S(1)} %get-tuple-element.13), channel_id=1, source_target_pairs={{0,1},{1,0},{2,3},{3,2},{4,5},{5,4},{6,7},{7,6},{8,9},{9,8},{10,11... | collective-permute-start | bytes 786440 | tf_op jit(solution)/shard_map/ppermute | solution.py:78
  157.0 12.1 %all-to-all-start.4 = ((bf16[32,2,512]{2,1,0:T(2,128)(2,1)}), bf16[32,2,512]{2,1,0:T(2,128)(2,1)S(1)}, u32[]{:S(2)}, u32[]{:S(2)}) async-start(bf16[32,2,512]{2,1,0:T(2,128)(2,1)} %reshape.59), calls=%async_computation.4 | async-start | bytes 131072 | tf_op jit(solution)/shard_map/all_to_all | solution.py:68
  169.1 73.9 %all-to-all-start.6 = ((bf16[32,128,64]{1,2,0:T(8,128)(2,1)}), bf16[32,128,64]{1,2,0:T(8,128)(2,1)S(1)}, u32[]{:S(2)}, u32[]{:S(2)}) async-start(bf16[32,128,64]{1,2,0:T(8,128)(2,1)} %bitcast.26), calls=%async_computation.6 | async-start | bytes 1048576 | tf_op jit(solution)/shard_map/all_to_all | solution.py:81
  235.2 7.0 %collective-permute-start.1 = (bf16[16,128,64]{1,2,0:T(8,128)(2,1)S(1)}, bf16[16,128,64]{1,2,0:T(8,128)(2,1)S(1)}, u32[]{:S(2)}, u32[]{:S(2)}) collective-permute-start(bf16[16,128,64]{1,2,0:T(8,128)(2,1)S(1)} %bitcast.73), channel_id=1, source_target_pairs={{0,1},{1,0},{2,3},{3,2},{4,5},{5,4},{6,7},{7,6},{8,9},{9,8},{10,11... | collective-permute-start | bytes 786440 | tf_op jit(solution)/shard_map/ppermute | solution.py:78
  243.0 23.6 %all-to-all-start.5 = ((bf16[32,128,64]{1,2,0:T(8,128)(2,1)}), bf16[32,128,64]{1,2,0:T(8,128)(2,1)S(1)}, u32[]{:S(2)}, u32[]{:S(2)}) async-start(bf16[32,128,64]{1,2,0:T(8,128)(2,1)} %bitcast.19), calls=%async_computation.5 | async-start | bytes 1048576 | tf_op jit(solution)/shard_map/all_to_all | solution.py:81
  271.9 13.5 %all-to-all-start.7 = ((bf16[32,2,512]{2,1,0:T(2,128)(2,1)}), bf16[32,2,512]{2,1,0:T(2,128)(2,1)S(1)}, u32[]{:S(2)}, u32[]{:S(2)}) async-start(bf16[32,2,512]{2,1,0:T(2,128)(2,1)} %reshape.61), calls=%async_computation.7 | async-start | bytes 131072 | tf_op jit(solution)/shard_map/all_to_all | solution.py:84
Sparse Core Ops, SparseCore 0:
  11.2 112.9 all-gather.6
  127.3 102.8 all-gather.4

commit v4 on v2

--- a/solution.py
+++ b/solution.py
@@ -55,28 +55,27 @@
     core = lax.axis_index("seq") % 2
     sibling = [(i, i ^ 1) for i in range(n_seq)]
     half = w_memory.shape[2] // 2
-    w_half = lax.dynamic_slice_in_dim(w_memory, core * half, half, axis=2)
-    w_half = lax.all_gather(w_half, "doc", axis=2, tiled=True)
+    w_half = lax.all_gather(lax.dynamic_slice_in_dim(w_memory, core * half, half, axis=2), "doc", axis=2, tiled=True)
 
-    head_query, head_key, head_value = (
-        lax.all_to_all(enc_query[0], "seq", split_axis=1, concat_axis=0, tiled=True),
-        lax.all_to_all(enc_key[0], "seq", split_axis=1, concat_axis=0, tiled=True),
-        lax.all_to_all(enc_value[0], "seq", split_axis=1, concat_axis=0, tiled=True),
-    )
-    summary_heads = lax.all_to_all(sum_query[0], "seq", split_axis=1, concat_axis=0, tiled=True)
+    rows, sum_rows = enc_query.shape[1], sum_query.shape[1]
+    both_query = lax.all_to_all(
+        jnp.concatenate([enc_query[0], sum_query[0]], axis=0), "seq", split_axis=1, concat_axis=0, tiled=True
+    ).reshape(n_seq, rows + sum_rows, -1)
+    head_query = both_query[:, :rows].reshape(n_seq * rows, -1)
+    summary_heads = both_query[:, rows:].reshape(n_seq * sum_rows, -1)
+    head_key = lax.all_to_all(enc_key[0], "seq", split_axis=1, concat_axis=0, tiled=True)
+    head_value = lax.all_to_all(enc_value[0], "seq", split_axis=1, concat_axis=0, tiled=True)
     context = attend_head(head_query, head_key, head_value, length)
     encoder_out = lax.all_to_all(context, "seq", split_axis=0, concat_axis=1, tiled=True)
 
     enc_pair = jnp.concatenate([encoder_out, lax.ppermute(encoder_out, "seq", sibling)], axis=0)
-    made = jnp.einsum("tf,kfc->tkc", enc_pair, w_half, preferred_element_type=jnp.float32)
-    made = made.astype(jnp.bfloat16).reshape(2, encoder_out.shape[0], 2, -1, 1, half)
+    made = jnp.einsum("tf,kfc->ktc", enc_pair, w_half, preferred_element_type=jnp.float32).astype(jnp.bfloat16)
+    made = made.reshape(2, 2, rows, -1, half).transpose(1, 3, 0, 2, 4)
     own, received = made[0], lax.ppermute(made[1], "seq", sibling)
-    memory_rows = jnp.where(core == 0, jnp.concatenate([own, received], axis=3),
-                            jnp.concatenate([received, own], axis=3))
-    memory_rows = memory_rows.reshape(encoder_out.shape[0], 2, -1)
-    memory_local = lax.all_to_all(memory_rows, "seq", split_axis=2, concat_axis=0, tiled=True)
-    memory_keys = memory_local[:, 0, :]
-    memory_values = memory_local[:, 1, :]
+    by_head = jnp.where(core == 0, jnp.stack([own, received], axis=1), jnp.stack([received, own], axis=1))
+    by_head = by_head.reshape(n_seq, 2, rows, half)
+    memory = lax.all_to_all(by_head, "seq", split_axis=0, concat_axis=2, tiled=True)
+    memory_keys, memory_values = memory[0, 0], memory[0, 1]
     answer = attend_head(summary_heads, memory_keys, memory_values, length)
     summary_out = lax.all_to_all(answer, "seq", split_axis=0, concat_axis=1, tiled=True)
     return (encoder_out[None], summary_out[None])

time: 254 us -> 245 us (0.965)
  starting transfers between devices: 49.3 us -> 42.1 us
  local copies, waits for them, and re-layouts: 31.7 us -> 26.7 us
    all_to_all x3 -> x2, starting transfers between devices: 27.7 us -> 12.8 us  [the longest x1 7.23 us: shards(): lax.all_to_all(by_head, 'seq', split_axis=0, concat_axis=2, tiled=True)]
    all_gather x1, waiting for transfers between devices: 10.9 us -> 1.88 us  [shards(): lax.all_gather(lax.dynamic_slice_in_dim(w_memory, core * half, half, axis...]
    all_to_all x3 -> x2, waiting for transfers between devices: 43.7 us -> 52.2 us  [the longest x1 26.7 us: shards(): lax.all_to_all(by_head, 'seq', split_axis=0, concat_axis=2, tiled=True)]
    select_n x2 -> x1, local copies, waits for them, and re-layouts: 9.57 us -> 1.1 us  [shards(): jnp.where(core == 0, jnp.stack([own, received], axis=1), jnp.stack([recei...]
    all_to_all x1, starting transfers between devices: 5.1 us -> 13 us  [shards(): lax.all_to_all(enc_key[0], 'seq', split_axis=1, concat_axis=0, tiled=True)]
    slice x3 -> x4, local copies, waits for them, and re-layouts: 0.61 us -> 5.54 us  [the longest x2 4.25 us: shards(): head_query = both_query[:, :rows].reshape(n_seq * rows, -1)]
    unnamed x29 -> x28, local copies, waits for them, and re-layouts: 10.5 us -> 11.1 us
  transfers between devices with their start and end apart: 9 -> 8, of which waited for: 7 -> 8; matrix products, arithmetic and copies ran while one was open for 8% -> 6% of each run, Pallas kernels for 13% -> 13%
where the time goes in v4:
time: 245 us; the launch traced here: 243 us
  waiting for transfers between devices  94.4 us (39%)
  starting transfers between devices  42.1 us (17%)
  Pallas kernels  36.3 us (15%)
  local copies, waits for them, and re-layouts  26.7 us (11%)
  blocking collectives  20.9 us (9%)
  between operations  15 us (6%)
  matrix products  6.77 us (3%)
    pallas_call x2, Pallas kernels, attend_head(): pl.pallas_call(_attend_kernel, grid_spec=grid_spec, out_shape=jax.ShapeDt...  36.3 us
    all_to_all x1, waiting for transfers between devices, shards(): lax.all_to_all(by_head, 'seq', split_axis=0, concat_axis=2, tiled=True)  26.7 us
    all_to_all x1, waiting for transfers between devices, shards(): lax.all_to_all(jnp.concatenate([enc_query[0], sum_query[0]], axis=0), 'se...  25.5 us
    all_to_all x1, blocking collectives, shards(): lax.all_to_all(context, 'seq', split_axis=0, concat_axis=1, tiled=True)  20.9 us
    all_to_all x1, waiting for transfers between devices, shards(): lax.all_to_all(enc_key[0], 'seq', split_axis=1, concat_axis=0, tiled=True)  15.6 us
    all_to_all x1, waiting for transfers between devices, shards(): lax.all_to_all(enc_value[0], 'seq', split_axis=1, concat_axis=0, tiled=True)  14.2 us
    all_to_all x1, starting transfers between devices, shards(): lax.all_to_all(enc_key[0], 'seq', split_axis=1, concat_axis=0, tiled=True)  13 us
    unnamed x28, local copies, waits for them, and re-layouts  11.1 us
  transfers between devices with their start and end apart: 8, of which 8 were waited for; matrix products, arithmetic and copies ran while one was open for 6% of the time, Pallas kernels for 13%

profile of v4, /device:TPU:1, one launch (start us, length us, event | category | flops | bytes accessed | tf_op | source)
XLA Modules:
  0.0 243.5 jit_solution(4830662232416840264)
XLA Ops:
  7.2 1.2 copy-done
  8.4 0.4 constant_dynamic-slice_fusion
  8.8 1.2 copy.50
  10.0 1.0 copy.36
  11.0 13.0 %all-to-all-start.1 = ((bf16[128,32,64]{0,2,1:T(8,128)(2,1)}), bf16[128,32,64]{0,2,1:T(8,128)(2,1)S(1)}, u32[]{:S(2)}, u32[]{:S(2)}) async-start(bf16[128,32,64]{0,2,1:T(8,128)(2,1)} %bitcast.4), calls=%async_computation.1 | async-start | bytes 1048576 | tf_op jit(solution)/shard_map/all_to_all | solution.py:66
  24.0 1.1 copy.38
  25.1 15.6 %all-to-all-done.1 = bf16[128,32,64]{0,2,1:T(8,128)(2,1)S(1)} async-done(((bf16[128,32,64]{0,2,1:T(8,128)(2,1)}), bf16[128,32,64]{0,2,1:T(8,128)(2,1)S(1)}, u32[]{:S(2)}, u32[]{:S(2)}) %all-to-all-start.1) | async-done | bytes 524320 | tf_op jit(solution)/shard_map/all_to_all | solution.py:66
  40.7 5.1 %all-to-all-start.2 = ((bf16[128,32,64]{0,2,1:T(8,128)(2,1)}), bf16[128,32,64]{0,2,1:T(8,128)(2,1)S(1)}, u32[]{:S(2)}, u32[]{:S(2)}) async-start(bf16[128,32,64]{0,2,1:T(8,128)(2,1)} %bitcast.7), calls=%async_computation.2 | async-start | bytes 1048576 | tf_op jit(solution)/shard_map/all_to_all | solution.py:67
  45.8 1.3 copy.33
  47.2 0.3 copy.34
  47.4 1.3 pad_maximum_fusion
  48.7 14.2 %all-to-all-done.2 = bf16[128,32,64]{0,2,1:T(8,128)(2,1)S(1)} async-done(((bf16[128,32,64]{0,2,1:T(8,128)(2,1)}), bf16[128,32,64]{0,2,1:T(8,128)(2,1)S(1)}, u32[]{:S(2)}, u32[]{:S(2)}) %all-to-all-start.2) | async-done | bytes 524320 | tf_op jit(solution)/shard_map/all_to_all | solution.py:67
  62.9 5.5 %all-to-all-start = ((bf16[144,32,64]{0,2,1:T(8,128)(2,1)}), bf16[144,32,64]{0,2,1:T(8,128)(2,1)}, u32[]{:S(2)}, u32[]{:S(2)}) async-start(bf16[144,32,64]{0,2,1:T(8,128)(2,1)} %pad_maximum_fusion), calls=%async_computation | async-start | bytes 2097152 | tf_op jit(solution)/shard_map/all_to_all | solution.py:61
  69.1 0.5 copy.37
  69.6 1.5 copy.39
  71.1 25.5 %all-to-all-done = bf16[144,32,64]{0,2,1:T(8,128)(2,1)} async-done(((bf16[144,32,64]{0,2,1:T(8,128)(2,1)}), bf16[144,32,64]{0,2,1:T(8,128)(2,1)}, u32[]{:S(2)}, u32[]{:S(2)}) %all-to-all-start) | async-done | bytes 589856 | tf_op jit(solution)/shard_map/all_to_all | solution.py:61
  96.7 1.9 slice.24
  98.5 2.4 copy.35
  100.9 1.2 copy-done.1
  102.2 32.2 %shard_map.77 = bf16[4096,64]{1,0:T(8,128)(2,1)S(1)} custom-call(s32[1]{0:T(128)S(6)} %copy.53.len_ref, bf16[4096,64]{1,0:T(8,128)(2,1)S(1)} %bitcast.46, bf16[4096,64]{1,0:T(8,128)(2,1)S(1)} %bitcast.44, bf16[4096,64]{1,0:T(8,128)(2,1)S(1)} %bitcast.45), custom_call_target="tpu_custom_call" | custom-call | flops 4294967296 | bytes 2097152 | tf_op jit(solution)/shard_map/pallas_call | solution.py:43
  134.4 1.0 copy-done.2
  135.4 1.6 copy.40
  137.0 20.9 %all_to_all.104 = bf16[32,128,64]{1,2,0:T(8,128)(2,1)S(1)} all-to-all(bf16[32,128,64]{1,2,0:T(8,128)(2,1)S(1)} %copy.40), channel_id=1, replica_groups=mesh['doc'=16,'seq'=32] {'seq'}, dimensions={0} | all-to-all | bytes 1048576 | tf_op jit(solution)/shard_map/all_to_all | solution.py:69
  157.9 0.2 copy.44
  158.1 3.5 %collective-permute-start = (bf16[128,2048]{1,0:T(8,128)(2,1)S(1)}, bf16[128,2048]{1,0:T(8,128)(2,1)S(1)}, u32[]{:S(2)}, u32[]{:S(2)}) collective-permute-start(bf16[128,2048]{1,0:T(8,128)(2,1)S(1)} %copy.44), channel_id=1, source_target_pairs={{0,1},{1,0},{2,3},{3,2},{4,5},{5,4},{6,7},{7,6},{8,9},{9,8},{10,11... | collective-permute-start | bytes 1572872 | tf_op jit(solution)/shard_map/ppermute | solution.py:71
  161.6 1.5 collective-permute-done
  163.1 1.9 all-gather.2.cloned.1.call-done
  165.0 6.8 %fusion = bf16[2,256,1024]{1,2,0:T(8,128)(2,1)} fusion(bf16[2,2048,1024]{1,2,0:T(8,128)(2,1)} %all-gather.2.cloned.1.call-done, bf16[128,2048]{1,0:T(8,128)(2,1)S(1)} %collective-permute-done, bf16[128,2048]{1,0:T(8,128)(2,1)S(1)} %copy.44), kind=kOutput, calls=%fused_computation.1 | convolution fusion | flops 2150105088 | bytes 10485760 | tf_op jit(solution)/shard_map/tf,kfc->ktc/dot_general | solution.py:72
  171.7 1.3 reshape.45
  173.1 0.3 copy.52
  173.5 2.8 %collective-permute-start.1 = (bf16[16,2,128,64]{2,3,1,0:T(8,128)(2,1)S(1)}, bf16[16,2,128,64]{2,3,1,0:T(8,128)(2,1)S(1)}, u32[]{:S(2)}, u32[]{:S(2)}) collective-permute-start(bf16[16,2,128,64]{2,3,1,0:T(8,128)(2,1)S(1)} %get-tuple-element.9), channel_id=1, source_target_pairs={{0,1},{1,0},{2,3},{3,2},{4,5},{5,4},{6,7},{7,6},{8,9},{9,8},{10,11... | collective-permute-start | bytes 1572872 | tf_op jit(solution)/shard_map/ppermute | solution.py:74
  176.3 1.5 collective-permute-done.1
  177.8 0.2 maximum_select_fusion
  178.0 1.1 copy.46
  179.0 7.2 %all-to-all-start.4 = ((bf16[32,2,128,64]{2,3,1,0:T(8,128)(2,1)}), bf16[32,2,128,64]{2,3,1,0:T(8,128)(2,1)S(1)}, u32[]{:S(2)}, u32[]{:S(2)}) async-start(bf16[32,2,128,64]{2,3,1,0:T(8,128)(2,1)} %bitcast.22), calls=%async_computation.4 | async-start | bytes 2097152 | tf_op jit(solution)/shard_map/all_to_all | solution.py:77
  186.3 1.1 slice.25
  187.4 0.2 copy.41
  187.6 26.7 %all-to-all-done.4 = bf16[32,2,128,64]{2,3,1,0:T(8,128)(2,1)S(1)} async-done(((bf16[32,2,128,64]{2,3,1,0:T(8,128)(2,1)}), bf16[32,2,128,64]{2,3,1,0:T(8,128)(2,1)S(1)}, u32[]{:S(2)}, u32[]{:S(2)}) %all-to-all-start.4) | async-done | bytes 1048608 | tf_op jit(solution)/shard_map/all_to_all | solution.py:77
  214.3 1.0 copy-done.5
  215.3 2.0 copy.47
  217.3 0.1 slice_bitcast_fusion
  217.5 4.1 %shard_map.78 = bf16[512,64]{1,0:T(8,128)(2,1)S(1)} custom-call(s32[1]{0:T(128)S(6)} %copy.53.len_ref, bf16[512,64]{1,0:T(8,128)(2,1)S(1)} %bitcast.48, bf16[4096,64]{1,0:T(8,128)(2,1)S(1)} %get-tuple-element.7.k_ref, bf16[4096,64]{1,0:T(8,128)(2,1)S(1)} %get-tuple-element.6.v_ref), custom_call_target="tpu_custom_call" | custom-call | flops 536870912 | bytes 1179648 | tf_op jit(solution)/shard_map/pallas_call | solution.py:43
  221.5 0.8 reshape.47
  222.3 4.9 %all-to-all-start.5 = ((bf16[32,2,512]{2,1,0:T(2,128)(2,1)}), bf16[32,2,512]{2,1,0:T(2,128)(2,1)S(1)}, u32[]{:S(2)}, u32[]{:S(2)}) async-start(bf16[32,2,512]{2,1,0:T(2,128)(2,1)} %reshape.47), calls=%async_computation.5 | async-start | bytes 131072 | tf_op jit(solution)/shard_map/all_to_all | solution.py:80
  227.2 1.0 copy.49
  228.2 7.4 %all-to-all-done.5 = bf16[32,2,512]{2,1,0:T(2,128)(2,1)S(1)} async-done(((bf16[32,2,512]{2,1,0:T(2,128)(2,1)}), bf16[32,2,512]{2,1,0:T(2,128)(2,1)S(1)}, u32[]{:S(2)}, u32[]{:S(2)}) %all-to-all-start.5) | async-done | bytes 65568 | tf_op jit(solution)/shard_map/all_to_all | solution.py:80
  235.6 0.1 reshape.48
  235.8 0.8 broadcast_in_dim.7
  (20 shorter events, 0.2 us)
Async XLA Ops:
  7.2 1.2 copy-start
  7.2 157.8 %all-gather.2.cloned.1.call-start = ((), (), s32[]{:S(2)}) async-start(), calls=%async_computation.6 | async-start | bytes 8912896 | tf_op jit(solution)/shard_map/all_gather | solution.py:58
  8.4 1.6 copy-start.7
  8.8 15.2 %copy-start.8 = (bf16[1,128,2048]{2,1,0:T(8,128)(2,1)S(1)}, bf16[1,128,2048]{2,1,0:T(8,128)(2,1)}, u32[]{:S(2)}) copy-start(bf16[1,128,2048]{2,1,0:T(8,128)(2,1)} %param.8) | copy-start | bytes 1572868
  11.0 36.2 %copy-start.9 = (bf16[1,16,2048]{2,1,0:T(8,128)(2,1)S(1)}, bf16[1,16,2048]{2,1,0:T(8,128)(2,1)}, u32[]{:S(2)}) copy-start(bf16[1,16,2048]{2,1,0:T(8,128)(2,1)} %param.9) | copy-start | bytes 196612
  11.0 29.8 %all-to-all-start.1 = ((bf16[128,32,64]{0,2,1:T(8,128)(2,1)}), bf16[128,32,64]{0,2,1:T(8,128)(2,1)S(1)}, u32[]{:S(2)}, u32[]{:S(2)}) async-start(bf16[128,32,64]{0,2,1:T(8,128)(2,1)} %bitcast.4), calls=%async_computation.1 | async-start | bytes 1048576 | tf_op jit(solution)/shard_map/all_to_all | solution.py:66
  40.7 22.2 %all-to-all-start.2 = ((bf16[128,32,64]{0,2,1:T(8,128)(2,1)}), bf16[128,32,64]{0,2,1:T(8,128)(2,1)S(1)}, u32[]{:S(2)}, u32[]{:S(2)}) async-start(bf16[128,32,64]{0,2,1:T(8,128)(2,1)} %bitcast.7), calls=%async_computation.2 | async-start | bytes 1048576 | tf_op jit(solution)/shard_map/all_to_all | solution.py:67
  62.9 6.7 %copy-start.6 = (bf16[128,32,64]{0,2,1:T(8,128)(2,1)}, bf16[128,32,64]{0,2,1:T(8,128)(2,1)S(1)}, u32[]{:S(2)}) copy-start(bf16[128,32,64]{0,2,1:T(8,128)(2,1)S(1)} %all-to-all-done.2) | copy-start | bytes 1572868
  62.9 33.8 %all-to-all-start = ((bf16[144,32,64]{0,2,1:T(8,128)(2,1)}), bf16[144,32,64]{0,2,1:T(8,128)(2,1)}, u32[]{:S(2)}, u32[]{:S(2)}) async-start(bf16[144,32,64]{0,2,1:T(8,128)(2,1)} %pad_maximum_fusion), calls=%async_computation | async-start | bytes 2097152 | tf_op jit(solution)/shard_map/all_to_all | solution.py:61
  100.9 1.2 copy-start.1
  134.4 1.0 copy-start.2
  157.9 13.9 %copy-start.3 = (bf16[32,128,64]{1,2,0:T(8,128)(2,1)}, bf16[32,128,64]{1,2,0:T(8,128)(2,1)S(1)}, u32[]{:S(2)}) copy-start(bf16[32,128,64]{1,2,0:T(8,128)(2,1)S(1)} %all_to_all.104) | copy-start | bytes 1572868
  158.1 5.0 %collective-permute-start = (bf16[128,2048]{1,0:T(8,128)(2,1)S(1)}, bf16[128,2048]{1,0:T(8,128)(2,1)S(1)}, u32[]{:S(2)}, u32[]{:S(2)}) collective-permute-start(bf16[128,2048]{1,0:T(8,128)(2,1)S(1)} %copy.44), channel_id=1, source_target_pairs={{0,1},{1,0},{2,3},{3,2},{4,5},{5,4},{6,7},{7,6},{8,9},{9,8},{10,11... | collective-permute-start | bytes 1572872 | tf_op jit(solution)/shard_map/ppermute | solution.py:71
  173.5 4.3 %collective-permute-start.1 = (bf16[16,2,128,64]{2,3,1,0:T(8,128)(2,1)S(1)}, bf16[16,2,128,64]{2,3,1,0:T(8,128)(2,1)S(1)}, u32[]{:S(2)}, u32[]{:S(2)}) collective-permute-start(bf16[16,2,128,64]{2,3,1,0:T(8,128)(2,1)S(1)} %get-tuple-element.9), channel_id=1, source_target_pairs={{0,1},{1,0},{2,3},{3,2},{4,5},{5,4},{6,7},{7,6},{8,9},{9,8},{10,11... | collective-permute-start | bytes 1572872 | tf_op jit(solution)/shard_map/ppermute | solution.py:74
  179.0 35.2 %all-to-all-start.4 = ((bf16[32,2,128,64]{2,3,1,0:T(8,128)(2,1)}), bf16[32,2,128,64]{2,3,1,0:T(8,128)(2,1)S(1)}, u32[]{:S(2)}, u32[]{:S(2)}) async-start(bf16[32,2,128,64]{2,3,1,0:T(8,128)(2,1)} %bitcast.22), calls=%async_computation.4 | async-start | bytes 2097152 | tf_op jit(solution)/shard_map/all_to_all | solution.py:77
  214.3 1.0 copy-start.5
  217.5 9.7 %copy-start.4 = (bf16[32,128,64]{1,2,0:T(8,128)(2,1)S(1)}, bf16[32,128,64]{1,2,0:T(8,128)(2,1)}, u32[]{:S(2)}) copy-start(bf16[32,128,64]{1,2,0:T(8,128)(2,1)} %copy-done.3) | copy-start | bytes 1572868
  222.3 13.3 %all-to-all-start.5 = ((bf16[32,2,512]{2,1,0:T(2,128)(2,1)}), bf16[32,2,512]{2,1,0:T(2,128)(2,1)S(1)}, u32[]{:S(2)}, u32[]{:S(2)}) async-start(bf16[32,2,512]{2,1,0:T(2,128)(2,1)} %reshape.47), calls=%async_computation.5 | async-start | bytes 131072 | tf_op jit(solution)/shard_map/all_to_all | solution.py:80
Sparse Core Ops, SparseCore 0:
  11.2 153.7 all-gather.1

commit v5 on v4

--- a/solution.py
+++ b/solution.py
@@ -55,16 +55,17 @@
     core = lax.axis_index("seq") % 2
     sibling = [(i, i ^ 1) for i in range(n_seq)]
     half = w_memory.shape[2] // 2
-    w_half = lax.all_gather(lax.dynamic_slice_in_dim(w_memory, core * half, half, axis=2), "doc", axis=2, tiled=True)
+    w_half = lax.dynamic_slice_in_dim(w_memory, core * half, half, axis=2)
+    w_half = lax.all_gather(w_half, "doc_x", axis=2, tiled=True)
+    w_half = lax.all_gather(w_half, "doc_y", axis=2, tiled=True)
 
     rows, sum_rows = enc_query.shape[1], sum_query.shape[1]
-    both_query = lax.all_to_all(
-        jnp.concatenate([enc_query[0], sum_query[0]], axis=0), "seq", split_axis=1, concat_axis=0, tiled=True
-    ).reshape(n_seq, rows + sum_rows, -1)
-    head_query = both_query[:, :rows].reshape(n_seq * rows, -1)
-    summary_heads = both_query[:, rows:].reshape(n_seq * sum_rows, -1)
-    head_key = lax.all_to_all(enc_key[0], "seq", split_axis=1, concat_axis=0, tiled=True)
-    head_value = lax.all_to_all(enc_value[0], "seq", split_axis=1, concat_axis=0, tiled=True)
+    mixed = lax.all_to_all(
+        jnp.concatenate([enc_query[0], enc_key[0], enc_value[0], sum_query[0]], axis=0),
+        "seq", split_axis=1, concat_axis=0, tiled=True,
+    ).reshape(n_seq, 3 * rows + sum_rows, -1)
+    head_query, head_key, head_value = (mixed[:, i * rows:(i + 1) * rows].reshape(n_seq * rows, -1) for i in range(3))
+    summary_heads = mixed[:, 3 * rows:].reshape(n_seq * sum_rows, -1)
     context = attend_head(head_query, head_key, head_value, length)
     encoder_out = lax.all_to_all(context, "seq", split_axis=0, concat_axis=1, tiled=True)
 
@@ -82,13 +83,16 @@
 
 
 def solution(mesh):
+    n_doc = mesh.shape["doc"]
+    split = jax.sharding.Mesh(mesh.devices.reshape(n_doc // 2, 2, mesh.shape["seq"]), ("doc_y", "doc_x", "seq"))
+    doc = ("doc_y", "doc_x")
     in_specs = (
-        P("doc", "seq", None),
-        P("doc", "seq", None),
-        P("doc", "seq", None),
-        P("doc", "seq", None),
-        P("doc"),
-        P(None, None, "doc"),
+        P(doc, "seq", None),
+        P(doc, "seq", None),
+        P(doc, "seq", None),
+        P(doc, "seq", None),
+        P(doc),
+        P(None, None, doc),
     )
-    out_specs = (P("doc", "seq", None), P("doc", "seq", None))
-    return jax.shard_map(shards, mesh=mesh, in_specs=in_specs, out_specs=out_specs, check_vma=False)
+    out_specs = (P(doc, "seq", None), P(doc, "seq", None))
+    return jax.shard_map(shards, mesh=split, in_specs=in_specs, out_specs=out_specs, check_vma=False)

time: 245 us -> 255 us (1.041)
  waiting for transfers between devices: 94.4 us -> 123 us
  starting transfers between devices: 42.1 us -> 23.1 us
    all_gather x1 -> x2, waiting for transfers between devices: 1.88 us -> 36.9 us  [the longest x1 36.9 us: shards(): w_half = lax.all_gather(w_half, 'doc_x', axis=2, tiled=True)]
    all_to_all x3 -> x1, starting transfers between devices: 23.7 us -> 8.21 us  [shards(): lax.all_to_all(jnp.concatenate([enc_query[0], enc_key[0], enc_value[0], s...]
    all_to_all x3 -> x1, waiting for transfers between devices: 55.4 us -> 49.4 us  [shards(): lax.all_to_all(jnp.concatenate([enc_query[0], enc_key[0], enc_value[0], s...]
    all_to_all x1, starting transfers between devices: 7.23 us -> 3.96 us  [shards(): lax.all_to_all(by_head, 'seq', split_axis=0, concat_axis=2, tiled=True)]
    slice x4 -> x6, local copies, waits for them, and re-layouts: 5.54 us -> 8.4 us  [the longest x4 7.12 us: shards(): mixed[:, i * rows:(i + 1) * rows].reshape(n_seq * rows, -1)]
  transfers between devices with their start and end apart: 8 -> 7, of which waited for: 8 -> 6; matrix products, arithmetic and copies ran while one was open for 6% -> 6% of each run, Pallas kernels for 13% -> 13%
where the time goes in v5:
time: 255 us; the launch traced here: 254 us
  waiting for transfers between devices  123 us (48%)
  Pallas kernels  36.3 us (14%)
  local copies, waits for them, and re-layouts  26.1 us (10%)
  starting transfers between devices  23.1 us (9%)
  blocking collectives  21.4 us (8%)
  between operations  15 us (6%)
  matrix products  6.76 us (3%)
    all_to_all x1, waiting for transfers between devices, shards(): lax.all_to_all(jnp.concatenate([enc_query[0], enc_key[0], enc_value[0], s...  49.4 us
    all_gather x1, waiting for transfers between devices, shards(): w_half = lax.all_gather(w_half, 'doc_x', axis=2, tiled=True)  36.9 us
    pallas_call x2, Pallas kernels, attend_head(): pl.pallas_call(_attend_kernel, grid_spec=grid_spec, out_shape=jax.ShapeDt...  36.3 us
    all_to_all x1, waiting for transfers between devices, shards(): lax.all_to_all(by_head, 'seq', split_axis=0, concat_axis=2, tiled=True)  26.6 us
    all_to_all x1, blocking collectives, shards(): lax.all_to_all(context, 'seq', split_axis=0, concat_axis=1, tiled=True)  21.4 us
    unnamed x28, local copies, waits for them, and re-layouts  9.74 us
    all_to_all x1, starting transfers between devices, shards(): lax.all_to_all(jnp.concatenate([enc_query[0], enc_key[0], enc_value[0], s...  8.21 us
    all_to_all x1, waiting for transfers between devices, shards(): lax.all_to_all(answer, 'seq', split_axis=0, concat_axis=1, tiled=True)  7.41 us
  transfers between devices with their start and end apart: 7, of which 6 were waited for; matrix products, arithmetic and copies ran while one was open for 6% of the time, Pallas kernels for 13%

profile of v5, /device:TPU:1, one launch (start us, length us, event | category | flops | bytes accessed | tf_op | source)
XLA Modules:
  0.0 254.0 jit_solution(1855347256338799736)
XLA Ops:
  7.2 0.0 all-gather.3.cloned.1.call-start
  7.2 1.2 copy-done
  8.4 0.4 constant_dynamic-slice_fusion
  8.8 1.1 copy.50
  9.9 0.0 all-gather.5.cloned.1.call-start
  10.0 36.9 %all-gather.3.cloned.1.call-done = bf16[2,2048,128]{1,2,0:T(8,128)(2,1)} async-done(((bf16[2,2048,64]{1,2,0:T(8,128)(2,1)}), bf16[2,2048,128]{1,2,0:T(8,128)(2,1)}) %all-gather.3.cloned.1.call-update) | async-done | bytes 1048592 | tf_op jit(solution)/shard_map/all_gather | solution.py:59
  46.9 0.3 copy.36
  47.2 0.3 copy.35
  47.5 0.3 copy.34
  47.8 1.3 copy.33
  49.1 1.8 pad_maximum_fusion
  50.9 8.2 %all-to-all-start = ((bf16[400,32,64]{0,2,1:T(8,128)(2,1)}), bf16[400,32,64]{0,2,1:T(8,128)(2,1)S(1)}, u32[]{:S(2)}, u32[]{:S(2)}) async-start(bf16[400,32,64]{0,2,1:T(8,128)(2,1)} %pad_maximum_fusion), calls=%async_computation | async-start | bytes 4194304 | tf_op jit(solution)/shard_map/all_to_all | solution.py:63
  59.7 49.4 %all-to-all-done = bf16[400,32,64]{0,2,1:T(8,128)(2,1)S(1)} async-done(((bf16[400,32,64]{0,2,1:T(8,128)(2,1)}), bf16[400,32,64]{0,2,1:T(8,128)(2,1)S(1)}, u32[]{:S(2)}, u32[]{:S(2)}) %all-to-all-start) | async-done | bytes 1638432 | tf_op jit(solution)/shard_map/all_to_all | solution.py:63
  109.2 1.7 fusion.4
  110.8 0.2 copy-done.3
  111.0 1.5 copy.37
  112.5 1.5 copy.38
  114.1 2.4 copy.39
  116.5 1.2 copy-done.1
  117.7 32.2 %shard_map.77 = bf16[4096,64]{1,0:T(8,128)(2,1)S(1)} custom-call(s32[1]{0:T(128)S(6)} %copy.53.len_ref, bf16[4096,64]{1,0:T(8,128)(2,1)S(1)} %bitcast.42, bf16[4096,64]{1,0:T(8,128)(2,1)S(1)} %bitcast.43, bf16[4096,64]{1,0:T(8,128)(2,1)S(1)} %bitcast.44), custom_call_target="tpu_custom_call" | custom-call | flops 4294967296 | bytes 2097152 | tf_op jit(solution)/shard_map/pallas_call | solution.py:43
  149.9 1.0 copy-done.2
  150.9 1.6 copy.40
  152.5 21.4 %all_to_all.66 = bf16[32,128,64]{1,2,0:T(8,128)(2,1)S(1)} all-to-all(bf16[32,128,64]{1,2,0:T(8,128)(2,1)S(1)} %copy.40), channel_id=1, replica_groups=mesh['doc_y'=8,'doc_x'=2,'seq'=32] {'seq'}, dimensions={0} | all-to-all | bytes 1048576 | tf_op jit(solution)/shard_map/all_to_all | solution.py:70
  173.9 0.2 copy.44
  174.1 3.5 %collective-permute-start = (bf16[128,2048]{1,0:T(8,128)(2,1)S(1)}, bf16[128,2048]{1,0:T(8,128)(2,1)S(1)}, u32[]{:S(2)}, u32[]{:S(2)}) collective-permute-start(bf16[128,2048]{1,0:T(8,128)(2,1)S(1)} %copy.44), channel_id=1, source_target_pairs={{0,1},{1,0},{2,3},{3,2},{4,5},{5,4},{6,7},{7,6},{8,9},{9,8},{10,11... | collective-permute-start | bytes 1572872 | tf_op jit(solution)/shard_map/ppermute | solution.py:72
  177.6 1.5 collective-permute-done
  179.1 6.8 %fusion = bf16[2,256,1024]{1,2,0:T(8,128)(2,1)} fusion(bf16[2,2048,1024]{1,2,0:T(8,128)(2,1)} %all-gather.5.cloned.1.call-done, bf16[128,2048]{1,0:T(8,128)(2,1)S(1)} %collective-permute-done, bf16[128,2048]{1,0:T(8,128)(2,1)S(1)} %copy.44), kind=kOutput, calls=%fused_computation.2 | convolution fusion | flops 2150105088 | bytes 10485760 | tf_op jit(solution)/shard_map/tf,kfc->ktc/dot_general | solution.py:73
  185.9 1.3 reshape.49
  187.2 0.3 copy.52
  187.5 0.1 slice_bitcast_fusion.3
  187.6 2.3 collective-permute-start.1
  189.9 1.5 collective-permute-done.1
  191.4 0.2 maximum_select_fusion
  191.6 1.1 copy.46
  192.7 4.0 %all-to-all-start.2 = ((bf16[32,2,128,64]{2,3,1,0:T(8,128)(2,1)}), bf16[32,2,128,64]{2,3,1,0:T(8,128)(2,1)S(1)}, u32[]{:S(2)}, u32[]{:S(2)}) async-start(bf16[32,2,128,64]{2,3,1,0:T(8,128)(2,1)} %bitcast.20), calls=%async_computation.2 | async-start | bytes 2097152 | tf_op jit(solution)/shard_map/all_to_all | solution.py:78
  196.6 1.1 slice.35
  197.7 0.2 copy.41
  197.9 26.6 %all-to-all-done.2 = bf16[32,2,128,64]{2,3,1,0:T(8,128)(2,1)S(1)} async-done(((bf16[32,2,128,64]{2,3,1,0:T(8,128)(2,1)}), bf16[32,2,128,64]{2,3,1,0:T(8,128)(2,1)S(1)}, u32[]{:S(2)}, u32[]{:S(2)}) %all-to-all-start.2) | async-done | bytes 1048608 | tf_op jit(solution)/shard_map/all_to_all | solution.py:78
  224.6 1.0 copy-done.6
  225.6 2.0 copy.47
  227.6 0.1 slice_bitcast_fusion
  227.8 4.1 %shard_map.78 = bf16[512,64]{1,0:T(8,128)(2,1)S(1)} custom-call(s32[1]{0:T(128)S(6)} %copy.53.len_ref, bf16[512,64]{1,0:T(8,128)(2,1)S(1)} %bitcast.46, bf16[4096,64]{1,0:T(8,128)(2,1)S(1)} %get-tuple-element.7.k_ref, bf16[4096,64]{1,0:T(8,128)(2,1)S(1)} %get-tuple-element.6.v_ref), custom_call_target="tpu_custom_call" | custom-call | flops 536870912 | bytes 1179648 | tf_op jit(solution)/shard_map/pallas_call | solution.py:43
  231.8 0.8 reshape.51
  232.6 5.1 %all-to-all-start.3 = ((bf16[32,2,512]{2,1,0:T(2,128)(2,1)}), bf16[32,2,512]{2,1,0:T(2,128)(2,1)S(1)}, u32[]{:S(2)}, u32[]{:S(2)}) async-start(bf16[32,2,512]{2,1,0:T(2,128)(2,1)} %reshape.51), calls=%async_computation.3 | async-start | bytes 131072 | tf_op jit(solution)/shard_map/all_to_all | solution.py:81
  237.8 1.0 copy.49
  238.8 7.4 %all-to-all-done.3 = bf16[32,2,512]{2,1,0:T(2,128)(2,1)S(1)} async-done(((bf16[32,2,512]{2,1,0:T(2,128)(2,1)}), bf16[32,2,512]{2,1,0:T(2,128)(2,1)S(1)}, u32[]{:S(2)}, u32[]{:S(2)}) %all-to-all-start.3) | async-done | bytes 65568 | tf_op jit(solution)/shard_map/all_to_all | solution.py:81
  246.2 0.1 reshape.52
  246.4 0.8 broadcast_in_dim.7
  (19 shorter events, 0.1 us)
Async XLA Ops:
  7.2 1.2 copy-start
  7.2 39.7 %all-gather.3.cloned.1.call-start = ((), (), s32[]{:S(2)}) async-start(), calls=%async_computation.4 | async-start | bytes 1572864 | tf_op jit(solution)/shard_map/all_gather | solution.py:59
  8.8 38.2 %copy-start.9 = (bf16[1,16,2048]{2,1,0:T(8,128)(2,1)S(1)}, bf16[1,16,2048]{2,1,0:T(8,128)(2,1)}, u32[]{:S(2)}) copy-start(bf16[1,16,2048]{2,1,0:T(8,128)(2,1)} %param.9) | copy-start | bytes 196612
  8.8 38.4 %copy-start.7 = (bf16[1,128,2048]{2,1,0:T(8,128)(2,1)S(1)}, bf16[1,128,2048]{2,1,0:T(8,128)(2,1)}, u32[]{:S(2)}) copy-start(bf16[1,128,2048]{2,1,0:T(8,128)(2,1)} %param.8) | copy-start | bytes 1572868
  8.8 38.7 %copy-start.8 = (bf16[1,128,2048]{2,1,0:T(8,128)(2,1)S(1)}, bf16[1,128,2048]{2,1,0:T(8,128)(2,1)}, u32[]{:S(2)}) copy-start(bf16[1,128,2048]{2,1,0:T(8,128)(2,1)} %param.7) | copy-start | bytes 1572868
  9.9 169.1 %all-gather.5.cloned.1.call-start = ((), (), s32[]{:S(2)}) async-start(), calls=%async_computation.5 | async-start | bytes 9437184 | tf_op jit(solution)/shard_map/all_gather | solution.py:60
  50.9 58.3 %all-to-all-start = ((bf16[400,32,64]{0,2,1:T(8,128)(2,1)}), bf16[400,32,64]{0,2,1:T(8,128)(2,1)S(1)}, u32[]{:S(2)}, u32[]{:S(2)}) async-start(bf16[400,32,64]{0,2,1:T(8,128)(2,1)} %pad_maximum_fusion), calls=%async_computation | async-start | bytes 4194304 | tf_op jit(solution)/shard_map/all_to_all | solution.py:63
  109.2 1.8 copy-start.3
  116.5 1.2 copy-start.1
  149.9 1.0 copy-start.2
  173.9 12.0 %copy-start.4 = (bf16[32,128,64]{1,2,0:T(8,128)(2,1)}, bf16[32,128,64]{1,2,0:T(8,128)(2,1)S(1)}, u32[]{:S(2)}) copy-start(bf16[32,128,64]{1,2,0:T(8,128)(2,1)S(1)} %all_to_all.66) | copy-start | bytes 1572868
  174.1 5.0 %collective-permute-start = (bf16[128,2048]{1,0:T(8,128)(2,1)S(1)}, bf16[128,2048]{1,0:T(8,128)(2,1)S(1)}, u32[]{:S(2)}, u32[]{:S(2)}) collective-permute-start(bf16[128,2048]{1,0:T(8,128)(2,1)S(1)} %copy.44), channel_id=1, source_target_pairs={{0,1},{1,0},{2,3},{3,2},{4,5},{5,4},{6,7},{7,6},{8,9},{9,8},{10,11... | collective-permute-start | bytes 1572872 | tf_op jit(solution)/shard_map/ppermute | solution.py:72
  187.6 3.8 %collective-permute-start.1 = (bf16[16,2,128,64]{2,3,1,0:T(8,128)(2,1)S(1)}, bf16[16,2,128,64]{2,3,1,0:T(8,128)(2,1)S(1)}, u32[]{:S(2)}, u32[]{:S(2)}) collective-permute-start(bf16[16,2,128,64]{2,3,1,0:T(8,128)(2,1)S(1)} %get-tuple-element.12), channel_id=1, source_target_pairs={{0,1},{1,0},{2,3},{3,2},{4,5},{5,4},{6,7},{7,6},{8,9},{9,8},{10,11... | collective-permute-start | bytes 1572872 | tf_op jit(solution)/shard_map/ppermute | solution.py:75
  192.7 31.9 %all-to-all-start.2 = ((bf16[32,2,128,64]{2,3,1,0:T(8,128)(2,1)}), bf16[32,2,128,64]{2,3,1,0:T(8,128)(2,1)S(1)}, u32[]{:S(2)}, u32[]{:S(2)}) async-start(bf16[32,2,128,64]{2,3,1,0:T(8,128)(2,1)} %bitcast.20), calls=%async_computation.2 | async-start | bytes 2097152 | tf_op jit(solution)/shard_map/all_to_all | solution.py:78
  224.6 1.0 copy-start.6
  227.8 10.0 %copy-start.5 = (bf16[32,128,64]{1,2,0:T(8,128)(2,1)S(1)}, bf16[32,128,64]{1,2,0:T(8,128)(2,1)}, u32[]{:S(2)}) copy-start(bf16[32,128,64]{1,2,0:T(8,128)(2,1)} %copy-done.4) | copy-start | bytes 1572868
  232.6 13.6 %all-to-all-start.3 = ((bf16[32,2,512]{2,1,0:T(2,128)(2,1)}), bf16[32,2,512]{2,1,0:T(2,128)(2,1)S(1)}, u32[]{:S(2)}, u32[]{:S(2)}) async-start(bf16[32,2,512]{2,1,0:T(2,128)(2,1)} %reshape.51), calls=%async_computation.3 | async-start | bytes 131072 | tf_op jit(solution)/shard_map/all_to_all | solution.py:81
Sparse Core Ops, SparseCore 0:
  10.7 36.1 all-gather.2
  49.0 95.9 all-gather.4

commit v6 on v5

--- a/solution.py
+++ b/solution.py
@@ -56,7 +56,9 @@
     sibling = [(i, i ^ 1) for i in range(n_seq)]
     half = w_memory.shape[2] // 2
     w_half = lax.dynamic_slice_in_dim(w_memory, core * half, half, axis=2)
-    w_half = lax.all_gather(w_half, "doc_x", axis=2, tiled=True)
+    w_pair = lax.ppermute(w_half, "doc_x", perm=[(0, 1), (1, 0)])
+    w_half = jnp.where(lax.axis_index("doc_x") == 0, jnp.concatenate([w_half, w_pair], axis=2),
+                       jnp.concatenate([w_pair, w_half], axis=2))
     w_half = lax.all_gather(w_half, "doc_y", axis=2, tiled=True)
 
     rows, sum_rows = enc_query.shape[1], sum_query.shape[1]

time: 255 us -> 240 us (0.941)
  waiting for transfers between devices: 123 us -> 94.7 us
  starting transfers between devices: 23.1 us -> 36.8 us
    all_gather x1 -> x0, waiting for transfers between devices: 36.9 us -> none  [shards(): w_half = lax.all_gather(w_half, 'doc_x', axis=2, tiled=True)]
    ppermute x0 -> x1, waiting for transfers between devices: none -> 8.14 us  [shards(): w_pair = lax.ppermute(w_half, 'doc_x', perm=[(0, 1), (1, 0)])]
    all_to_all x1, starting transfers between devices: 8.21 us -> 16.3 us  [shards(): lax.all_to_all(jnp.concatenate([enc_query[0], enc_key[0], enc_value[0], s...]
    ppermute x0 -> x1, starting transfers between devices: none -> 5.61 us  [shards(): w_pair = lax.ppermute(w_half, 'doc_x', perm=[(0, 1), (1, 0)])]
where the time goes in v6:
time: 240 us; the launch traced here: 239 us
  waiting for transfers between devices  94.7 us (39%)
  starting transfers between devices  36.8 us (15%)
  Pallas kernels  36.3 us (15%)
  local copies, waits for them, and re-layouts  25.3 us (11%)
  blocking collectives  21.4 us (9%)
  between operations  15 us (6%)
  matrix products  6.76 us (3%)
  other arithmetic  3.21 us (1%)
    all_to_all x1, waiting for transfers between devices, shards(): lax.all_to_all(jnp.concatenate([enc_query[0], enc_key[0], enc_value[0], s...  49.4 us
    pallas_call x2, Pallas kernels, attend_head(): pl.pallas_call(_attend_kernel, grid_spec=grid_spec, out_shape=jax.ShapeDt...  36.3 us
    all_to_all x1, waiting for transfers between devices, shards(): lax.all_to_all(by_head, 'seq', split_axis=0, concat_axis=2, tiled=True)  26.6 us
    all_to_all x1, blocking collectives, shards(): lax.all_to_all(context, 'seq', split_axis=0, concat_axis=1, tiled=True)  21.4 us
    all_to_all x1, starting transfers between devices, shards(): lax.all_to_all(jnp.concatenate([enc_query[0], enc_key[0], enc_value[0], s...  16.3 us
    unnamed x28, local copies, waits for them, and re-layouts  8.93 us
    ppermute x1, waiting for transfers between devices, shards(): w_pair = lax.ppermute(w_half, 'doc_x', perm=[(0, 1), (1, 0)])  8.14 us
    all_to_all x1, waiting for transfers between devices, shards(): lax.all_to_all(answer, 'seq', split_axis=0, concat_axis=1, tiled=True)  7.41 us
  transfers between devices with their start and end apart: 7, of which 6 were waited for; matrix products, arithmetic and copies ran while one was open for 6% of the time, Pallas kernels for 13%

profile of v6, /device:TPU:1, one launch (start us, length us, event | category | flops | bytes accessed | tf_op | source)
XLA Modules:
  0.0 239.4 jit_solution(3167765741574543194)
XLA Ops:
  7.2 1.2 copy-done
  8.4 0.4 constant_dynamic-slice_fusion
  8.8 0.3 copy.50
  9.1 5.6 %collective-permute-start = (bf16[2,2048,64]{1,2,0:T(8,128)(2,1)S(1)}, bf16[2,2048,64]{1,2,0:T(8,128)(2,1)S(1)}, u32[]{:S(2)}, u32[]{:S(2)}) collective-permute-start(bf16[2,2048,64]{1,2,0:T(8,128)(2,1)S(1)} %copy.50), channel_id=1, source_target_pairs={{0,32},{32,0},{1,33},{33,1},{2,34},{34,2},{3,35},{35,3},{4,36},{36... | collective-permute-start | bytes 1572872 | tf_op jit(solution)/shard_map/ppermute | solution.py:59
  14.8 8.1 %collective-permute-done = bf16[2,2048,64]{1,2,0:T(8,128)(2,1)S(1)} collective-permute-done((bf16[2,2048,64]{1,2,0:T(8,128)(2,1)S(1)}, bf16[2,2048,64]{1,2,0:T(8,128)(2,1)S(1)}, u32[]{:S(2)}, u32[]{:S(2)}) %collective-permute-start) | collective-permute-done | bytes 524320 | tf_op jit(solution)/shard_map/ppermute | solution.py:59
  22.9 1.3 maximum_select_fusion
  24.2 0.3 copy.36
  24.5 0.3 copy.35
  24.8 0.3 copy.34
  25.0 1.3 copy.33
  26.4 1.8 pad_maximum_fusion
  28.1 16.3 %all-to-all-start = ((bf16[400,32,64]{0,2,1:T(8,128)(2,1)}), bf16[400,32,64]{0,2,1:T(8,128)(2,1)S(1)}, u32[]{:S(2)}, u32[]{:S(2)}) async-start(bf16[400,32,64]{0,2,1:T(8,128)(2,1)} %pad_maximum_fusion), calls=%async_computation | async-start | bytes 4194304 | tf_op jit(solution)/shard_map/all_to_all | solution.py:65
  45.1 49.4 %all-to-all-done = bf16[400,32,64]{0,2,1:T(8,128)(2,1)S(1)} async-done(((bf16[400,32,64]{0,2,1:T(8,128)(2,1)}), bf16[400,32,64]{0,2,1:T(8,128)(2,1)S(1)}, u32[]{:S(2)}, u32[]{:S(2)}) %all-to-all-start) | async-done | bytes 1638432 | tf_op jit(solution)/shard_map/all_to_all | solution.py:65
  94.5 1.7 fusion.4
  96.2 0.1 copy-done.3
  96.4 1.5 copy.37
  97.9 1.5 copy.38
  99.4 2.4 %copy.39 = bf16[32,128,64]{2,1,0:T(8,128)(2,1)} copy(bf16[32,128,64]{1,2,0:T(8,128)(2,1)} %get-tuple-element.8) | data formatting | bytes 1048576 | tf_op jit(solution)/shard_map/slice | solution.py:69
  101.8 1.2 copy-done.1
  103.1 32.2 %shard_map.77 = bf16[4096,64]{1,0:T(8,128)(2,1)S(1)} custom-call(s32[1]{0:T(128)S(6)} %copy.53.len_ref, bf16[4096,64]{1,0:T(8,128)(2,1)S(1)} %bitcast.42, bf16[4096,64]{1,0:T(8,128)(2,1)S(1)} %bitcast.43, bf16[4096,64]{1,0:T(8,128)(2,1)S(1)} %bitcast.44), custom_call_target="tpu_custom_call" | custom-call | flops 4294967296 | bytes 2097152 | tf_op jit(solution)/shard_map/pallas_call | solution.py:43
  135.3 1.0 copy-done.2
  136.3 1.6 copy.40
  137.9 21.4 %all_to_all.66 = bf16[32,128,64]{1,2,0:T(8,128)(2,1)S(1)} all-to-all(bf16[32,128,64]{1,2,0:T(8,128)(2,1)S(1)} %copy.40), channel_id=1, replica_groups=mesh['doc_y'=8,'doc_x'=2,'seq'=32] {'seq'}, dimensions={0} | all-to-all | bytes 1048576 | tf_op jit(solution)/shard_map/all_to_all | solution.py:72
  159.3 0.2 copy.44
  159.5 3.5 %collective-permute-start.1 = (bf16[128,2048]{1,0:T(8,128)(2,1)S(1)}, bf16[128,2048]{1,0:T(8,128)(2,1)S(1)}, u32[]{:S(2)}, u32[]{:S(2)}) collective-permute-start(bf16[128,2048]{1,0:T(8,128)(2,1)S(1)} %copy.44), channel_id=1, source_target_pairs={{0,1},{1,0},{2,3},{3,2},{4,5},{5,4},{6,7},{7,6},{8,9},{9,8},{10,11... | collective-permute-start | bytes 1572872 | tf_op jit(solution)/shard_map/ppermute | solution.py:74
  163.0 1.5 collective-permute-done.1
  164.5 6.8 %fusion = bf16[2,256,1024]{1,2,0:T(8,128)(2,1)} fusion(bf16[2,2048,1024]{1,2,0:T(8,128)(2,1)} %all-gather.2.cloned.1.call-done, bf16[128,2048]{1,0:T(8,128)(2,1)S(1)} %collective-permute-done.1, bf16[128,2048]{1,0:T(8,128)(2,1)S(1)} %copy.44), kind=kOutput, calls=%fused_computation.2 | convolution fusion | flops 2150105088 | bytes 10485760 | tf_op jit(solution)/shard_map/tf,kfc->ktc/dot_general | solution.py:75
  171.3 1.3 reshape.49
  172.6 0.3 copy.52
  172.9 0.1 slice_bitcast_fusion.3
  173.0 2.3 collective-permute-start.2
  175.3 1.5 collective-permute-done.2
  176.8 0.2 maximum_select_fusion.1
  177.0 1.1 copy.46
  178.0 4.0 %all-to-all-start.2 = ((bf16[32,2,128,64]{2,3,1,0:T(8,128)(2,1)}), bf16[32,2,128,64]{2,3,1,0:T(8,128)(2,1)S(1)}, u32[]{:S(2)}, u32[]{:S(2)}) async-start(bf16[32,2,128,64]{2,3,1,0:T(8,128)(2,1)} %bitcast.20), calls=%async_computation.2 | async-start | bytes 2097152 | tf_op jit(solution)/shard_map/all_to_all | solution.py:80
  182.0 1.1 slice.35
  183.1 0.2 copy.41
  183.3 26.6 %all-to-all-done.2 = bf16[32,2,128,64]{2,3,1,0:T(8,128)(2,1)S(1)} async-done(((bf16[32,2,128,64]{2,3,1,0:T(8,128)(2,1)}), bf16[32,2,128,64]{2,3,1,0:T(8,128)(2,1)S(1)}, u32[]{:S(2)}, u32[]{:S(2)}) %all-to-all-start.2) | async-done | bytes 1048608 | tf_op jit(solution)/shard_map/all_to_all | solution.py:80
  209.9 1.0 copy-done.6
  210.9 2.0 copy.47
  213.0 0.1 slice_bitcast_fusion
  213.1 4.1 %shard_map.78 = bf16[512,64]{1,0:T(8,128)(2,1)S(1)} custom-call(s32[1]{0:T(128)S(6)} %copy.53.len_ref, bf16[512,64]{1,0:T(8,128)(2,1)S(1)} %bitcast.46, bf16[4096,64]{1,0:T(8,128)(2,1)S(1)} %get-tuple-element.7.k_ref, bf16[4096,64]{1,0:T(8,128)(2,1)S(1)} %get-tuple-element.6.v_ref), custom_call_target="tpu_custom_call" | custom-call | flops 536870912 | bytes 1179648 | tf_op jit(solution)/shard_map/pallas_call | solution.py:43
  217.2 0.8 reshape.51
  218.0 5.1 %all-to-all-start.3 = ((bf16[32,2,512]{2,1,0:T(2,128)(2,1)}), bf16[32,2,512]{2,1,0:T(2,128)(2,1)S(1)}, u32[]{:S(2)}, u32[]{:S(2)}) async-start(bf16[32,2,512]{2,1,0:T(2,128)(2,1)} %reshape.51), calls=%async_computation.3 | async-start | bytes 131072 | tf_op jit(solution)/shard_map/all_to_all | solution.py:83
  223.1 1.0 copy.49
  224.1 7.4 %all-to-all-done.3 = bf16[32,2,512]{2,1,0:T(2,128)(2,1)S(1)} async-done(((bf16[32,2,512]{2,1,0:T(2,128)(2,1)}), bf16[32,2,512]{2,1,0:T(2,128)(2,1)S(1)}, u32[]{:S(2)}, u32[]{:S(2)}) %all-to-all-start.3) | async-done | bytes 65568 | tf_op jit(solution)/shard_map/all_to_all | solution.py:83
  231.5 0.1 reshape.52
  231.7 0.8 broadcast_in_dim.7
  (19 shorter events, 0.1 us)
Async XLA Ops:
  7.2 1.2 copy-start
  7.2 157.3 %all-gather.2.cloned.1.call-start = ((), (), s32[]{:S(2)}) async-start(), calls=%async_computation.4 | async-start | bytes 9437184 | tf_op jit(solution)/shard_map/all_gather | solution.py:62
  8.8 15.4 %copy-start.9 = (bf16[1,16,2048]{2,1,0:T(8,128)(2,1)S(1)}, bf16[1,16,2048]{2,1,0:T(8,128)(2,1)}, u32[]{:S(2)}) copy-start(bf16[1,16,2048]{2,1,0:T(8,128)(2,1)} %param.9) | copy-start | bytes 196612
  9.1 15.4 %copy-start.7 = (bf16[1,128,2048]{2,1,0:T(8,128)(2,1)S(1)}, bf16[1,128,2048]{2,1,0:T(8,128)(2,1)}, u32[]{:S(2)}) copy-start(bf16[1,128,2048]{2,1,0:T(8,128)(2,1)} %param.8) | copy-start | bytes 1572868
  9.1 13.8 %collective-permute-start = (bf16[2,2048,64]{1,2,0:T(8,128)(2,1)S(1)}, bf16[2,2048,64]{1,2,0:T(8,128)(2,1)S(1)}, u32[]{:S(2)}, u32[]{:S(2)}) collective-permute-start(bf16[2,2048,64]{1,2,0:T(8,128)(2,1)S(1)} %copy.50), channel_id=1, source_target_pairs={{0,32},{32,0},{1,33},{33,1},{2,34},{34,2},{3,35},{35,3},{4,36},{36... | collective-permute-start | bytes 1572872 | tf_op jit(solution)/shard_map/ppermute | solution.py:59
  14.7 10.0 %copy-start.8 = (bf16[1,128,2048]{2,1,0:T(8,128)(2,1)S(1)}, bf16[1,128,2048]{2,1,0:T(8,128)(2,1)}, u32[]{:S(2)}) copy-start(bf16[1,128,2048]{2,1,0:T(8,128)(2,1)} %param.7) | copy-start | bytes 1572868
  28.1 66.4 %all-to-all-start = ((bf16[400,32,64]{0,2,1:T(8,128)(2,1)}), bf16[400,32,64]{0,2,1:T(8,128)(2,1)S(1)}, u32[]{:S(2)}, u32[]{:S(2)}) async-start(bf16[400,32,64]{0,2,1:T(8,128)(2,1)} %pad_maximum_fusion), calls=%async_computation | async-start | bytes 4194304 | tf_op jit(solution)/shard_map/all_to_all | solution.py:65
  94.5 1.8 copy-start.3
  101.8 1.2 copy-start.1
  135.3 1.0 copy-start.2
  159.3 12.0 %copy-start.4 = (bf16[32,128,64]{1,2,0:T(8,128)(2,1)}, bf16[32,128,64]{1,2,0:T(8,128)(2,1)S(1)}, u32[]{:S(2)}) copy-start(bf16[32,128,64]{1,2,0:T(8,128)(2,1)S(1)} %all_to_all.66) | copy-start | bytes 1572868
  159.5 5.0 %collective-permute-start.1 = (bf16[128,2048]{1,0:T(8,128)(2,1)S(1)}, bf16[128,2048]{1,0:T(8,128)(2,1)S(1)}, u32[]{:S(2)}, u32[]{:S(2)}) collective-permute-start(bf16[128,2048]{1,0:T(8,128)(2,1)S(1)} %copy.44), channel_id=1, source_target_pairs={{0,1},{1,0},{2,3},{3,2},{4,5},{5,4},{6,7},{7,6},{8,9},{9,8},{10,11... | collective-permute-start | bytes 1572872 | tf_op jit(solution)/shard_map/ppermute | solution.py:74
  173.0 3.8 %collective-permute-start.2 = (bf16[16,2,128,64]{2,3,1,0:T(8,128)(2,1)S(1)}, bf16[16,2,128,64]{2,3,1,0:T(8,128)(2,1)S(1)}, u32[]{:S(2)}, u32[]{:S(2)}) collective-permute-start(bf16[16,2,128,64]{2,3,1,0:T(8,128)(2,1)S(1)} %get-tuple-element.12), channel_id=1, source_target_pairs={{0,1},{1,0},{2,3},{3,2},{4,5},{5,4},{6,7},{7,6},{8,9},{9,8},{10,11... | collective-permute-start | bytes 1572872 | tf_op jit(solution)/shard_map/ppermute | solution.py:77
  178.0 31.9 %all-to-all-start.2 = ((bf16[32,2,128,64]{2,3,1,0:T(8,128)(2,1)}), bf16[32,2,128,64]{2,3,1,0:T(8,128)(2,1)S(1)}, u32[]{:S(2)}, u32[]{:S(2)}) async-start(bf16[32,2,128,64]{2,3,1,0:T(8,128)(2,1)} %bitcast.20), calls=%async_computation.2 | async-start | bytes 2097152 | tf_op jit(solution)/shard_map/all_to_all | solution.py:80
  209.9 1.0 copy-start.6
  213.1 10.0 %copy-start.5 = (bf16[32,128,64]{1,2,0:T(8,128)(2,1)S(1)}, bf16[32,128,64]{1,2,0:T(8,128)(2,1)}, u32[]{:S(2)}) copy-start(bf16[32,128,64]{1,2,0:T(8,128)(2,1)} %copy-done.4) | copy-start | bytes 1572868
  218.0 13.6 %all-to-all-start.3 = ((bf16[32,2,512]{2,1,0:T(2,128)(2,1)}), bf16[32,2,512]{2,1,0:T(2,128)(2,1)S(1)}, u32[]{:S(2)}, u32[]{:S(2)}) async-start(bf16[32,2,512]{2,1,0:T(2,128)(2,1)} %reshape.51), calls=%async_computation.3 | async-start | bytes 131072 | tf_op jit(solution)/shard_map/all_to_all | solution.py:83
Sparse Core Ops, SparseCore 0:
  24.3 105.3 all-gather.1

commit v7 on v6

--- a/solution.py
+++ b/solution.py
@@ -49,6 +49,88 @@
     )(length.reshape(1), queries, keys_in, values_in)
 
 
+MESH = pl.DeviceIdType.MESH
+
+
+def _attend_scatter_kernel(len_ref, q_ref, k_ref, v_ref, out_ref, ctx_buf, send_sem, recv_sem, own_sem):
+    n_dev, chunk = out_ref.shape[0], out_ref.shape[1]
+    me = lax.axis_index("seq")
+    place = (lax.axis_index("doc_y"), lax.axis_index("doc_x"))
+    barrier = pltpu.get_barrier_semaphore()
+
+    def greet(t, carry):
+        @pl.when(t != me)
+        def _():
+            pl.semaphore_signal(barrier, inc=1, device_id=place + (t,), device_id_type=MESH)
+
+        return carry
+
+    lax.fori_loop(0, n_dev, greet, 0)
+    pl.semaphore_wait(barrier, n_dev - 1)
+    length = len_ref[0]
+
+    def block(b, carry):
+        rows = pl.ds(pl.multiple_of(b * 2 * chunk, 2 * chunk), 2 * chunk)
+        scores = lax.dot_general(
+            q_ref[rows, :], k_ref[...], (((1,), (1,)), ((), ())), preferred_element_type=jnp.float32
+        ) * HEAD_DIM ** (-0.5)
+        key_pos = lax.broadcasted_iota(jnp.int32, scores.shape, 1)
+        scores = jnp.where(key_pos < length, scores, -1e30)
+        row_max = jnp.max(scores, axis=1, keepdims=True)
+        weights = jnp.exp(scores - row_max)
+        denominator = jnp.sum(weights, axis=1, keepdims=True)
+        weighted = jnp.dot(weights.astype(jnp.bfloat16), v_ref[...], preferred_element_type=jnp.float32)
+        context = (weighted / denominator).astype(jnp.bfloat16)
+        ctx_buf[pl.ds(2 * b, 2)] = context.reshape(2, chunk, context.shape[1])
+        for j in range(2):
+            owner = 2 * b + j
+
+            @pl.when(owner != me)
+            def _():
+                pltpu.make_async_remote_copy(
+                    src_ref=ctx_buf.at[owner], dst_ref=out_ref.at[me], send_sem=send_sem, recv_sem=recv_sem,
+                    device_id=place + (owner,), device_id_type=MESH,
+                ).start()
+
+        return carry
+
+    lax.fori_loop(0, n_dev // 2, block, 0)
+    own = pltpu.make_async_copy(ctx_buf.at[me], out_ref.at[me], own_sem)
+    own.start()
+    every = pltpu.make_async_remote_copy(
+        src_ref=ctx_buf.at[pl.ds(0, n_dev - 1)], dst_ref=out_ref.at[pl.ds(0, n_dev - 1)], send_sem=send_sem,
+        recv_sem=recv_sem, device_id=place + (me,), device_id_type=MESH,
+    )
+    every.wait_send()
+    every.wait_recv()
+    own.wait()
+
+
+def attend_scatter(queries, keys_in, values_in, length, n_dev):
+    nq, width = queries.shape
+    chunk = nq // n_dev
+    nk = keys_in.shape[0]
+    vmem = pl.BlockSpec(memory_space=pltpu.VMEM)
+    return pl.pallas_call(
+        _attend_scatter_kernel,
+        out_shape=jax.ShapeDtypeStruct((n_dev, chunk, width), jnp.bfloat16),
+        in_specs=[pl.BlockSpec(memory_space=pltpu.SMEM), vmem, vmem, vmem],
+        out_specs=pl.BlockSpec(memory_space=pl.ANY),
+        scratch_shapes=[
+            pltpu.VMEM((n_dev, chunk, width), jnp.bfloat16),
+            pltpu.SemaphoreType.DMA,
+            pltpu.SemaphoreType.DMA,
+            pltpu.SemaphoreType.DMA,
+        ],
+        cost_estimate=pl.CostEstimate(
+            flops=4 * nq * nk * width, transcendentals=nq * nk, bytes_accessed=2 * (2 * nq * width + 2 * nk * width)
+        ),
+        compiler_params=pltpu.CompilerParams(
+            collective_id=1, has_side_effects=True, vmem_limit_bytes=48 * 1024 * 1024
+        ),
+    )(length.reshape(1), queries, keys_in, values_in)
+
+
 def shards(enc_query, enc_key, enc_value, sum_query, doc_len, w_memory):
     length = doc_len[0]
     n_seq = lax.axis_size("seq")
@@ -68,8 +150,8 @@
     ).reshape(n_seq, 3 * rows + sum_rows, -1)
     head_query, head_key, head_value = (mixed[:, i * rows:(i + 1) * rows].reshape(n_seq * rows, -1) for i in range(3))
     summary_heads = mixed[:, 3 * rows:].reshape(n_seq * sum_rows, -1)
-    context = attend_head(head_query, head_key, head_value, length)
-    encoder_out = lax.all_to_all(context, "seq", split_axis=0, concat_axis=1, tiled=True)
+    by_head = attend_scatter(head_query, head_key, head_value, length, n_seq)
+    encoder_out = by_head.transpose(1, 0, 2).reshape(by_head.shape[1], -1)
 
     enc_pair = jnp.concatenate([encoder_out, lax.ppermute(encoder_out, "seq", sibling)], axis=0)
     made = jnp.einsum("tf,kfc->ktc", enc_pair, w_half, preferred_element_type=jnp.float32).astype(jnp.bfloat16)

time: 240 us -> 238 us (level)
  blocking collectives: 21.4 us -> 0 us
  Pallas kernels: 36.3 us -> 52.8 us
  starting transfers between devices: 36.8 us -> 39.7 us
    pallas_call x0 -> x1, Pallas kernels: none -> 48.7 us  [attend_scatter(): pl.pallas_call(_attend_scatter_kernel, out_shape=jax.ShapeDtypeStruct((n_...]
    pallas_call x2 -> x1, Pallas kernels: 36.3 us -> 4.05 us  [attend_head(): pl.pallas_call(_attend_kernel, grid_spec=grid_spec, out_shape=jax.ShapeDt...]
    all_to_all x1 -> x0, blocking collectives: 21.4 us -> none  [shards(): lax.all_to_all(context, 'seq', split_axis=0, concat_axis=1, tiled=True)]
    all_to_all x1, starting transfers between devices: 3.96 us -> 7.95 us  [shards(): lax.all_to_all(by_head, 'seq', split_axis=0, concat_axis=2, tiled=True)]
  transfers between devices with their start and end apart: 7 -> 7, of which waited for: 6 -> 6; matrix products, arithmetic and copies ran while one was open for 6% -> 6% of each run, Pallas kernels for 13% -> 21%
where the time goes in v7:
time: 238 us; the launch traced here: 237 us
  waiting for transfers between devices  94.7 us (40%)
  Pallas kernels  52.8 us (22%)
  starting transfers between devices  39.7 us (17%)
  local copies, waits for them, and re-layouts  25.3 us (11%)
  between operations  15 us (6%)
  matrix products  6.76 us (3%)
  other arithmetic  3.21 us (1%)
    all_to_all x1, waiting for transfers between devices, shards(): lax.all_to_all(jnp.concatenate([enc_query[0], enc_key[0], enc_value[0], s...  49.4 us
    pallas_call x1, Pallas kernels, attend_scatter(): pl.pallas_call(_attend_scatter_kernel, out_shape=jax.ShapeDtypeStruct((n_...  48.7 us
    all_to_all x1, waiting for transfers between devices, shards(): lax.all_to_all(by_head, 'seq', split_axis=0, concat_axis=2, tiled=True)  26.7 us
    all_to_all x1, starting transfers between devices, shards(): lax.all_to_all(jnp.concatenate([enc_query[0], enc_key[0], enc_value[0], s...  16.3 us
    unnamed x28, local copies, waits for them, and re-layouts  8.93 us
    ppermute x1, waiting for transfers between devices, shards(): w_pair = lax.ppermute(w_half, 'doc_x', perm=[(0, 1), (1, 0)])  8.14 us
    all_to_all x1, starting transfers between devices, shards(): lax.all_to_all(by_head, 'seq', split_axis=0, concat_axis=2, tiled=True)  7.95 us
    all_to_all x1, waiting for transfers between devices, shards(): lax.all_to_all(answer, 'seq', split_axis=0, concat_axis=1, tiled=True)  7.41 us
  transfers between devices with their start and end apart: 7, of which 6 were waited for; matrix products, arithmetic and copies ran while one was open for 6% of the time, Pallas kernels for 21%

profile of v7, /device:TPU:1, one launch (start us, length us, event | category | flops | bytes accessed | tf_op | source)
XLA Modules:
  0.0 237.4 jit_solution(2693352211757763691)
XLA Ops:
  7.2 0.0 all-gather.2.cloned.1.call-start
  7.2 1.2 copy-done
  8.4 0.4 constant_dynamic-slice_fusion
  8.8 0.3 copy.50
  9.1 5.6 %collective-permute-start = (bf16[2,2048,64]{1,2,0:T(8,128)(2,1)S(1)}, bf16[2,2048,64]{1,2,0:T(8,128)(2,1)S(1)}, u32[]{:S(2)}, u32[]{:S(2)}) collective-permute-start(bf16[2,2048,64]{1,2,0:T(8,128)(2,1)S(1)} %copy.50), channel_id=1, source_target_pairs={{0,32},{32,0},{1,33},{33,1},{2,34},{34,2},{3,35},{35,3},{4,36},{36... | collective-permute-start | bytes 1572872 | tf_op jit(solution)/shard_map/ppermute | solution.py:141
  14.8 8.1 %collective-permute-done = bf16[2,2048,64]{1,2,0:T(8,128)(2,1)S(1)} collective-permute-done((bf16[2,2048,64]{1,2,0:T(8,128)(2,1)S(1)}, bf16[2,2048,64]{1,2,0:T(8,128)(2,1)S(1)}, u32[]{:S(2)}, u32[]{:S(2)}) %collective-permute-start) | collective-permute-done | bytes 524320 | tf_op jit(solution)/shard_map/ppermute | solution.py:141
  22.9 1.3 maximum_select_fusion
  24.2 0.3 copy.35
  24.5 0.3 copy.34
  24.8 0.3 copy.33
  25.0 1.3 copy.32
  26.4 1.8 pad_maximum_fusion
  28.1 16.3 %all-to-all-start = ((bf16[400,32,64]{0,2,1:T(8,128)(2,1)}), bf16[400,32,64]{0,2,1:T(8,128)(2,1)S(1)}, u32[]{:S(2)}, u32[]{:S(2)}) async-start(bf16[400,32,64]{0,2,1:T(8,128)(2,1)} %pad_maximum_fusion), calls=%async_computation | async-start | bytes 4194304 | tf_op jit(solution)/shard_map/all_to_all | solution.py:147
  45.1 49.4 %all-to-all-done = bf16[400,32,64]{0,2,1:T(8,128)(2,1)S(1)} async-done(((bf16[400,32,64]{0,2,1:T(8,128)(2,1)}), bf16[400,32,64]{0,2,1:T(8,128)(2,1)S(1)}, u32[]{:S(2)}, u32[]{:S(2)}) %all-to-all-start) | async-done | bytes 1638432 | tf_op jit(solution)/shard_map/all_to_all | solution.py:147
  94.5 1.7 fusion.4
  96.2 0.1 copy-done.3
  96.4 1.5 copy.36
  97.9 1.5 copy.37
  99.4 2.4 %copy.38 = bf16[32,128,64]{2,1,0:T(8,128)(2,1)} copy(bf16[32,128,64]{1,2,0:T(8,128)(2,1)} %get-tuple-element.8) | data formatting | bytes 1048576 | tf_op jit(solution)/shard_map/slice | solution.py:151
  101.8 1.2 copy-done.1
  103.1 48.7 %shard_map.77 = bf16[32,128,64]{2,1,0:T(8,128)(2,1)S(1)} custom-call(s32[1]{0:T(128)S(6)} %copy.53.len_ref, bf16[4096,64]{1,0:T(8,128)(2,1)S(1)} %bitcast.39, bf16[4096,64]{1,0:T(8,128)(2,1)S(1)} %bitcast.40, bf16[4096,64]{1,0:T(8,128)(2,1)S(1)} %bitcast.41), custom_call_target="tpu_custom_call" | custom-call | flops 4294967296 | bytes 2097152 | tf_op jit(solution)/shard_map/pallas_call | solution.py:114
  151.8 1.0 copy-done.2
  152.8 1.6 copy.39
  154.4 0.2 copy.44
  154.6 2.6 %collective-permute-start.1 = (bf16[128,2048]{1,0:T(8,128)(2,1)S(1)}, bf16[128,2048]{1,0:T(8,128)(2,1)S(1)}, u32[]{:S(2)}, u32[]{:S(2)}) collective-permute-start(bf16[128,2048]{1,0:T(8,128)(2,1)S(1)} %copy.44), channel_id=1, source_target_pairs={{0,1},{1,0},{2,3},{3,2},{4,5},{5,4},{6,7},{7,6},{8,9},{9,8},{10,11... | collective-permute-start | bytes 1572872 | tf_op jit(solution)/shard_map/ppermute | solution.py:156
  157.2 1.5 collective-permute-done.1
  158.7 6.8 %fusion = bf16[2,256,1024]{1,2,0:T(8,128)(2,1)} fusion(bf16[2,2048,1024]{1,2,0:T(8,128)(2,1)} %all-gather.2.cloned.1.call-done, bf16[128,2048]{1,0:T(8,128)(2,1)S(1)} %collective-permute-done.1, bf16[128,2048]{1,0:T(8,128)(2,1)S(1)} %copy.44), kind=kOutput, calls=%fused_computation.2 | convolution fusion | flops 2150105088 | bytes 10485760 | tf_op jit(solution)/shard_map/tf,kfc->ktc/dot_general | solution.py:157
  165.5 1.3 reshape.49
  166.9 0.3 copy.52
  167.1 0.1 slice_bitcast_fusion.3
  167.2 2.3 collective-permute-start.2
  169.5 1.5 collective-permute-done.2
  171.0 0.2 maximum_select_fusion.1
  171.2 1.1 copy.46
  172.3 7.9 %all-to-all-start.1 = ((bf16[32,2,128,64]{2,3,1,0:T(8,128)(2,1)}), bf16[32,2,128,64]{2,3,1,0:T(8,128)(2,1)S(1)}, u32[]{:S(2)}, u32[]{:S(2)}) async-start(bf16[32,2,128,64]{2,3,1,0:T(8,128)(2,1)} %bitcast.18), calls=%async_computation.1 | async-start | bytes 2097152 | tf_op jit(solution)/shard_map/all_to_all | solution.py:162
  180.2 1.1 slice.35
  181.3 0.2 copy.40
  181.5 26.7 %all-to-all-done.1 = bf16[32,2,128,64]{2,3,1,0:T(8,128)(2,1)S(1)} async-done(((bf16[32,2,128,64]{2,3,1,0:T(8,128)(2,1)}), bf16[32,2,128,64]{2,3,1,0:T(8,128)(2,1)S(1)}, u32[]{:S(2)}, u32[]{:S(2)}) %all-to-all-start.1) | async-done | bytes 1048608 | tf_op jit(solution)/shard_map/all_to_all | solution.py:162
  208.2 1.0 copy-done.6
  209.2 2.0 copy.47
  211.3 0.1 slice_bitcast_fusion
  211.4 4.1 %shard_map.78 = bf16[512,64]{1,0:T(8,128)(2,1)S(1)} custom-call(s32[1]{0:T(128)S(6)} %copy.53.len_ref, bf16[512,64]{1,0:T(8,128)(2,1)S(1)} %bitcast.43, bf16[4096,64]{1,0:T(8,128)(2,1)S(1)} %get-tuple-element.7.k_ref, bf16[4096,64]{1,0:T(8,128)(2,1)S(1)} %get-tuple-element.6.v_ref), custom_call_target="tpu_custom_call" | custom-call | flops 536870912 | bytes 1179648 | tf_op jit(solution)/shard_map/pallas_call | solution.py:43
  215.5 0.8 reshape.51
  216.2 4.9 %all-to-all-start.2 = ((bf16[32,2,512]{2,1,0:T(2,128)(2,1)}), bf16[32,2,512]{2,1,0:T(2,128)(2,1)S(1)}, u32[]{:S(2)}, u32[]{:S(2)}) async-start(bf16[32,2,512]{2,1,0:T(2,128)(2,1)} %reshape.51), calls=%async_computation.2 | async-start | bytes 131072 | tf_op jit(solution)/shard_map/all_to_all | solution.py:165
  221.1 1.0 copy.49
  222.1 7.4 %all-to-all-done.2 = bf16[32,2,512]{2,1,0:T(2,128)(2,1)S(1)} async-done(((bf16[32,2,512]{2,1,0:T(2,128)(2,1)}), bf16[32,2,512]{2,1,0:T(2,128)(2,1)S(1)}, u32[]{:S(2)}, u32[]{:S(2)}) %all-to-all-start.2) | async-done | bytes 65568 | tf_op jit(solution)/shard_map/all_to_all | solution.py:165
  229.5 0.1 reshape.52
  229.7 0.8 broadcast_in_dim.3
  (18 shorter events, 0.1 us)
Async XLA Ops:
  7.2 1.2 copy-start
  7.2 151.6 %all-gather.2.cloned.1.call-start = ((), (), s32[]{:S(2)}) async-start(), calls=%async_computation.3 | async-start | bytes 9437184 | tf_op jit(solution)/shard_map/all_gather | solution.py:144
  8.8 15.4 %copy-start.9 = (bf16[1,16,2048]{2,1,0:T(8,128)(2,1)S(1)}, bf16[1,16,2048]{2,1,0:T(8,128)(2,1)}, u32[]{:S(2)}) copy-start(bf16[1,16,2048]{2,1,0:T(8,128)(2,1)} %param.9) | copy-start | bytes 196612
  9.1 15.4 %copy-start.7 = (bf16[1,128,2048]{2,1,0:T(8,128)(2,1)S(1)}, bf16[1,128,2048]{2,1,0:T(8,128)(2,1)}, u32[]{:S(2)}) copy-start(bf16[1,128,2048]{2,1,0:T(8,128)(2,1)} %param.8) | copy-start | bytes 1572868
  9.1 13.8 %collective-permute-start = (bf16[2,2048,64]{1,2,0:T(8,128)(2,1)S(1)}, bf16[2,2048,64]{1,2,0:T(8,128)(2,1)S(1)}, u32[]{:S(2)}, u32[]{:S(2)}) collective-permute-start(bf16[2,2048,64]{1,2,0:T(8,128)(2,1)S(1)} %copy.50), channel_id=1, source_target_pairs={{0,32},{32,0},{1,33},{33,1},{2,34},{34,2},{3,35},{35,3},{4,36},{36... | collective-permute-start | bytes 1572872 | tf_op jit(solution)/shard_map/ppermute | solution.py:141
  14.7 10.0 %copy-start.8 = (bf16[1,128,2048]{2,1,0:T(8,128)(2,1)S(1)}, bf16[1,128,2048]{2,1,0:T(8,128)(2,1)}, u32[]{:S(2)}) copy-start(bf16[1,128,2048]{2,1,0:T(8,128)(2,1)} %param.7) | copy-start | bytes 1572868
  28.1 66.4 %all-to-all-start = ((bf16[400,32,64]{0,2,1:T(8,128)(2,1)}), bf16[400,32,64]{0,2,1:T(8,128)(2,1)S(1)}, u32[]{:S(2)}, u32[]{:S(2)}) async-start(bf16[400,32,64]{0,2,1:T(8,128)(2,1)} %pad_maximum_fusion), calls=%async_computation | async-start | bytes 4194304 | tf_op jit(solution)/shard_map/all_to_all | solution.py:147
  94.5 1.8 copy-start.3
  101.8 1.2 copy-start.1
  151.8 1.0 copy-start.2
  154.4 11.1 %copy-start.4 = (bf16[128,32,64]{0,2,1:T(8,128)(2,1)}, bf16[128,32,64]{0,2,1:T(8,128)(2,1)S(1)}, u32[]{:S(2)}) copy-start(bf16[128,32,64]{0,2,1:T(8,128)(2,1)S(1)} %copy.39) | copy-start | bytes 1572868
  154.6 4.1 %collective-permute-start.1 = (bf16[128,2048]{1,0:T(8,128)(2,1)S(1)}, bf16[128,2048]{1,0:T(8,128)(2,1)S(1)}, u32[]{:S(2)}, u32[]{:S(2)}) collective-permute-start(bf16[128,2048]{1,0:T(8,128)(2,1)S(1)} %copy.44), channel_id=1, source_target_pairs={{0,1},{1,0},{2,3},{3,2},{4,5},{5,4},{6,7},{7,6},{8,9},{9,8},{10,11... | collective-permute-start | bytes 1572872 | tf_op jit(solution)/shard_map/ppermute | solution.py:156
  167.2 3.8 %collective-permute-start.2 = (bf16[16,2,128,64]{2,3,1,0:T(8,128)(2,1)S(1)}, bf16[16,2,128,64]{2,3,1,0:T(8,128)(2,1)S(1)}, u32[]{:S(2)}, u32[]{:S(2)}) collective-permute-start(bf16[16,2,128,64]{2,3,1,0:T(8,128)(2,1)S(1)} %get-tuple-element.12), channel_id=1, source_target_pairs={{0,1},{1,0},{2,3},{3,2},{4,5},{5,4},{6,7},{7,6},{8,9},{9,8},{10,11... | collective-permute-start | bytes 1572872 | tf_op jit(solution)/shard_map/ppermute | solution.py:159
  172.3 35.9 %all-to-all-start.1 = ((bf16[32,2,128,64]{2,3,1,0:T(8,128)(2,1)}), bf16[32,2,128,64]{2,3,1,0:T(8,128)(2,1)S(1)}, u32[]{:S(2)}, u32[]{:S(2)}) async-start(bf16[32,2,128,64]{2,3,1,0:T(8,128)(2,1)} %bitcast.18), calls=%async_computation.1 | async-start | bytes 2097152 | tf_op jit(solution)/shard_map/all_to_all | solution.py:162
  208.2 1.0 copy-start.6
  211.4 9.7 %copy-start.5 = (bf16[128,32,64]{0,2,1:T(8,128)(2,1)S(1)}, bf16[128,32,64]{0,2,1:T(8,128)(2,1)}, u32[]{:S(2)}) copy-start(bf16[128,32,64]{0,2,1:T(8,128)(2,1)} %copy-done.4) | copy-start | bytes 1572868
  216.2 13.3 %all-to-all-start.2 = ((bf16[32,2,512]{2,1,0:T(2,128)(2,1)}), bf16[32,2,512]{2,1,0:T(2,128)(2,1)S(1)}, u32[]{:S(2)}, u32[]{:S(2)}) async-start(bf16[32,2,512]{2,1,0:T(2,128)(2,1)} %reshape.51), calls=%async_computation.2 | async-start | bytes 131072 | tf_op jit(solution)/shard_map/all_to_all | solution.py:165
Sparse Core Ops, SparseCore 0:
  24.3 105.3 all-gather.1

commit v8 on v7

--- a/solution.py
+++ b/solution.py
@@ -131,6 +131,104 @@
     )(length.reshape(1), queries, keys_in, values_in)
 
 
+def _summary_kernel(len_ref, mem_ref, q_ref, out_ref, mem_in, ctx_buf, sems):
+    n_dev, chunk = mem_ref.shape[0], mem_ref.shape[2]
+    sum_chunk = out_ref.shape[1]
+    me = lax.axis_index("seq")
+    place = (lax.axis_index("doc_y"), lax.axis_index("doc_x"))
+    barrier = pltpu.get_barrier_semaphore()
+
+    def greet(t, carry):
+        @pl.when(t != me)
+        def _():
+            pl.semaphore_signal(barrier, inc=1, device_id=place + (t,), device_id_type=MESH)
+
+        return carry
+
+    lax.fori_loop(0, n_dev, greet, 0)
+    pl.semaphore_wait(barrier, n_dev - 1)
+
+    def send_memory(t, carry):
+        @pl.when(t != me)
+        def _():
+            pltpu.make_async_remote_copy(
+                src_ref=mem_ref.at[t], dst_ref=mem_in.at[me], send_sem=sems.at[0], recv_sem=sems.at[1],
+                device_id=place + (t,), device_id_type=MESH,
+            ).start()
+
+        return carry
+
+    lax.fori_loop(0, n_dev, send_memory, 0)
+    own = pltpu.make_async_copy(mem_ref.at[me], mem_in.at[me], sems.at[2])
+    own.start()
+    every = pltpu.make_async_remote_copy(
+        src_ref=mem_ref.at[pl.ds(0, n_dev - 1)], dst_ref=mem_in.at[pl.ds(0, n_dev - 1)], send_sem=sems.at[0],
+        recv_sem=sems.at[1], device_id=place + (me,), device_id_type=MESH,
+    )
+    every.wait_recv()
+    own.wait()
+
+    keys = mem_in[:, 0].reshape(n_dev * chunk, -1)
+    values = mem_in[:, 1].reshape(n_dev * chunk, -1)
+    scores = lax.dot_general(
+        q_ref[...], keys, (((1,), (1,)), ((), ())), preferred_element_type=jnp.float32
+    ) * HEAD_DIM ** (-0.5)
+    key_pos = lax.broadcasted_iota(jnp.int32, scores.shape, 1)
+    scores = jnp.where(key_pos < len_ref[0], scores, -1e30)
+    row_max = jnp.max(scores, axis=1, keepdims=True)
+    weights = jnp.exp(scores - row_max)
+    denominator = jnp.sum(weights, axis=1, keepdims=True)
+    weighted = jnp.dot(weights.astype(jnp.bfloat16), values, preferred_element_type=jnp.float32)
+    context = (weighted / denominator).astype(jnp.bfloat16)
+    ctx_buf[...] = context.reshape(n_dev, sum_chunk, context.shape[1])
+
+    def send_context(t, carry):
+        @pl.when(t != me)
+        def _():
+            pltpu.make_async_remote_copy(
+                src_ref=ctx_buf.at[t], dst_ref=out_ref.at[me], send_sem=sems.at[3], recv_sem=sems.at[4],
+                device_id=place + (t,), device_id_type=MESH,
+            ).start()
+
+        return carry
+
+    lax.fori_loop(0, n_dev, send_context, 0)
+    back = pltpu.make_async_copy(ctx_buf.at[me], out_ref.at[me], sems.at[5])
+    back.start()
+    every.wait_send()
+    returned = pltpu.make_async_remote_copy(
+        src_ref=ctx_buf.at[pl.ds(0, n_dev - 1)], dst_ref=out_ref.at[pl.ds(0, n_dev - 1)], send_sem=sems.at[3],
+        recv_sem=sems.at[4], device_id=place + (me,), device_id_type=MESH,
+    )
+    returned.wait_send()
+    returned.wait_recv()
+    back.wait()
+
+
+def summary_exchange(memory_by_head, summary_queries, length):
+    n_dev, _, chunk, width = memory_by_head.shape
+    nq = summary_queries.shape[0]
+    vmem = pl.BlockSpec(memory_space=pltpu.VMEM)
+    return pl.pallas_call(
+        _summary_kernel,
+        out_shape=jax.ShapeDtypeStruct((n_dev, nq // n_dev, width), jnp.bfloat16),
+        in_specs=[pl.BlockSpec(memory_space=pltpu.SMEM), vmem, vmem],
+        out_specs=pl.BlockSpec(memory_space=pl.ANY),
+        scratch_shapes=[
+            pltpu.VMEM(memory_by_head.shape, jnp.bfloat16),
+            pltpu.VMEM((n_dev, nq // n_dev, width), jnp.bfloat16),
+            pltpu.SemaphoreType.DMA((6,)),
+        ],
+        cost_estimate=pl.CostEstimate(
+            flops=4 * nq * n_dev * chunk * width, transcendentals=nq * n_dev * chunk,
+            bytes_accessed=2 * (2 * nq * width + 2 * n_dev * chunk * width),
+        ),
+        compiler_params=pltpu.CompilerParams(
+            collective_id=2, has_side_effects=True, vmem_limit_bytes=48 * 1024 * 1024
+        ),
+    )(length.reshape(1), memory_by_head, summary_queries)
+
+
 def shards(enc_query, enc_key, enc_value, sum_query, doc_len, w_memory):
     length = doc_len[0]
     n_seq = lax.axis_size("seq")
@@ -159,10 +257,8 @@
     own, received = made[0], lax.ppermute(made[1], "seq", sibling)
     by_head = jnp.where(core == 0, jnp.stack([own, received], axis=1), jnp.stack([received, own], axis=1))
     by_head = by_head.reshape(n_seq, 2, rows, half)
-    memory = lax.all_to_all(by_head, "seq", split_axis=0, concat_axis=2, tiled=True)
-    memory_keys, memory_values = memory[0, 0], memory[0, 1]
-    answer = attend_head(summary_heads, memory_keys, memory_values, length)
-    summary_out = lax.all_to_all(answer, "seq", split_axis=0, concat_axis=1, tiled=True)
+    answer = summary_exchange(by_head, summary_heads, length)
+    summary_out = answer.transpose(1, 0, 2).reshape(answer.shape[1], -1)
     return (encoder_out[None], summary_out[None])
 
 

time: 238 us -> 256 us (1.076)
  Pallas kernels: 52.8 us -> 120 us
  waiting for transfers between devices: 94.7 us -> 59.1 us
  starting transfers between devices: 39.7 us -> 26.9 us
    pallas_call x1, Pallas kernels: 4.05 us -> 71.1 us  [summary_exchange(): pl.pallas_call(_summary_kernel, out_shape=jax.ShapeDtypeStruct((n_dev, nq...]
    all_to_all x2 -> x0, waiting for transfers between devices: 34.1 us -> none  [the longest x1 26.7 us: shards(): lax.all_to_all(by_head, 'seq', split_axis=0, concat_axis=2, tiled=True)]
    all_to_all x2 -> x0, starting transfers between devices: 12.8 us -> none  [the longest x1 7.95 us: shards(): lax.all_to_all(by_head, 'seq', split_axis=0, concat_axis=2, tiled=True)]
    unnamed x28 -> x18, local copies, waits for them, and re-layouts: 8.93 us -> 8.11 us
  transfers between devices with their start and end apart: 7 -> 5, of which waited for: 6 -> 3; matrix products, arithmetic and copies ran while one was open for 6% -> 6% of each run, Pallas kernels for 21% -> 19%
where the time goes in v8:
time: 256 us
  Pallas kernels  120 us (47%)
  waiting for transfers between devices  59.1 us (23%)
  starting transfers between devices  26.9 us (11%)
  local copies, waits for them, and re-layouts  24.1 us (9%)
  between operations  14.9 us (6%)
  matrix products  6.75 us (3%)
  other arithmetic  4.15 us (2%)
    pallas_call x1, Pallas kernels, summary_exchange(): pl.pallas_call(_summary_kernel, out_shape=jax.ShapeDtypeStruct((n_dev, nq...  71.1 us
    all_to_all x1, waiting for transfers between devices, shards(): lax.all_to_all(jnp.concatenate([enc_query[0], enc_key[0], enc_value[0], s...  49.4 us
    pallas_call x1, Pallas kernels, attend_scatter(): pl.pallas_call(_attend_scatter_kernel, out_shape=jax.ShapeDtypeStruct((n_...  48.7 us
    all_to_all x1, starting transfers between devices, shards(): lax.all_to_all(jnp.concatenate([enc_query[0], enc_key[0], enc_value[0], s...  16.3 us
    ppermute x1, waiting for transfers between devices, shards(): w_pair = lax.ppermute(w_half, 'doc_x', perm=[(0, 1), (1, 0)])  8.15 us
    unnamed x18, local copies, waits for them, and re-layouts  8.11 us
    slice x4, local copies, waits for them, and re-layouts, shards(): mixed[:, i * rows:(i + 1) * rows].reshape(n_seq * rows, -1)  7.11 us
    dot_general x1, matrix products, shards(): jnp.einsum('tf,kfc->ktc', enc_pair, w_half, preferred_element_type=jnp.fl...  6.75 us
  transfers between devices with their start and end apart: 5, of which 3 were waited for; matrix products, arithmetic and copies ran while one was open for 6% of the time, Pallas kernels for 19%

profile of v8, /device:TPU:1, one launch (start us, length us, event | category | flops | bytes accessed | tf_op | source)
XLA Modules:
  0.0 255.7 jit_solution(7404605495195754207)
XLA Ops:
  7.2 0.0 copy-start
  7.2 0.0 all-gather.2.cloned.1.call-start
  7.2 1.2 copy-done
  8.4 0.4 constant_dynamic-slice_fusion
  8.8 0.0 copy-start.4
  8.8 0.3 copy.47
  9.1 5.5 %collective-permute-start = (bf16[2,2048,64]{1,2,0:T(8,128)(2,1)S(1)}, bf16[2,2048,64]{1,2,0:T(8,128)(2,1)S(1)}, u32[]{:S(2)}, u32[]{:S(2)}) collective-permute-start(bf16[2,2048,64]{1,2,0:T(8,128)(2,1)S(1)} %copy.47), channel_id=1, source_target_pairs={{0,32},{32,0},{1,33},{33,1},{2,34},{34,2},{3,35},{35,3},{4,36},{36... | collective-permute-start | bytes 1572872 | tf_op jit(solution)/shard_map/ppermute | solution.py:239
  14.6 8.1 %collective-permute-done = bf16[2,2048,64]{1,2,0:T(8,128)(2,1)S(1)} collective-permute-done((bf16[2,2048,64]{1,2,0:T(8,128)(2,1)S(1)}, bf16[2,2048,64]{1,2,0:T(8,128)(2,1)S(1)}, u32[]{:S(2)}, u32[]{:S(2)}) %collective-permute-start) | collective-permute-done | bytes 524320 | tf_op jit(solution)/shard_map/ppermute | solution.py:239
  22.8 1.2 maximum_select_fusion
  24.0 0.0 copy-start.5
  24.0 0.0 all-gather.2.cloned.1.call-update
  24.0 0.0 copy-done.4
  24.0 0.3 copy.30
  24.3 1.3 copy.31
  25.6 1.3 copy.32
  27.0 0.0 copy-done.5
  27.0 0.3 copy.33
  27.2 1.8 pad_maximum_fusion
  29.0 16.3 %all-to-all-start = ((bf16[400,32,64]{0,2,1:T(8,128)(2,1)}), bf16[400,32,64]{0,2,1:T(8,128)(2,1)S(1)}, u32[]{:S(2)}, u32[]{:S(2)}) async-start(bf16[400,32,64]{0,2,1:T(8,128)(2,1)} %pad_maximum_fusion), calls=%async_computation | async-start | bytes 4194304 | tf_op jit(solution)/shard_map/all_to_all | solution.py:245
  46.0 49.4 %all-to-all-done = bf16[400,32,64]{0,2,1:T(8,128)(2,1)S(1)} async-done(((bf16[400,32,64]{0,2,1:T(8,128)(2,1)}), bf16[400,32,64]{0,2,1:T(8,128)(2,1)S(1)}, u32[]{:S(2)}, u32[]{:S(2)}) %all-to-all-start) | async-done | bytes 1638432 | tf_op jit(solution)/shard_map/all_to_all | solution.py:245
  95.4 0.0 copy-start.3
  95.4 1.7 fusion.4
  97.1 0.2 copy-done.3
  97.3 1.5 copy.36
  98.8 1.5 copy.35
  100.3 2.4 copy.34
  102.7 0.0 copy-start.1
  102.7 1.2 copy-done.1
  104.0 48.7 %shard_map.77 = bf16[32,128,64]{2,1,0:T(8,128)(2,1)S(1)} custom-call(s32[1]{0:T(128)S(6)} %copy.50.len_ref, bf16[4096,64]{1,0:T(8,128)(2,1)S(1)} %bitcast.33, bf16[4096,64]{1,0:T(8,128)(2,1)S(1)} %bitcast.32, bf16[4096,64]{1,0:T(8,128)(2,1)S(1)} %bitcast.31), custom_call_target="tpu_custom_call" | custom-call | flops 4294967296 | bytes 2097152 | tf_op jit(solution)/shard_map/pallas_call | solution.py:114
  152.7 0.0 copy-start.2
  152.7 1.0 copy-done.2
  153.7 1.6 copy.37
  155.3 0.2 copy.41
  155.5 2.6 %collective-permute-start.1 = (bf16[128,2048]{1,0:T(8,128)(2,1)S(1)}, bf16[128,2048]{1,0:T(8,128)(2,1)S(1)}, u32[]{:S(2)}, u32[]{:S(2)}) collective-permute-start(bf16[128,2048]{1,0:T(8,128)(2,1)S(1)} %copy.41), channel_id=1, source_target_pairs={{0,1},{1,0},{2,3},{3,2},{4,5},{5,4},{6,7},{7,6},{8,9},{9,8},{10,11... | collective-permute-start | bytes 1572872 | tf_op jit(solution)/shard_map/ppermute | solution.py:254
  158.1 1.5 collective-permute-done.1
  159.6 6.8 %fusion = bf16[2,256,1024]{1,2,0:T(8,128)(2,1)} fusion(bf16[2,2048,1024]{1,2,0:T(8,128)(2,1)} %all-gather.2.cloned.1.call-done, bf16[128,2048]{1,0:T(8,128)(2,1)S(1)} %collective-permute-done.1, bf16[128,2048]{1,0:T(8,128)(2,1)S(1)} %copy.41), kind=kOutput, calls=%fused_computation.2 | convolution fusion | flops 2150105088 | bytes 10485760 | tf_op jit(solution)/shard_map/tf,kfc->ktc/dot_general | solution.py:255
  166.4 1.3 reshape.44
  167.7 0.3 copy.49
  168.0 0.9 slice_bitcast_fusion.1
  168.9 2.5 collective-permute-start.2
  171.3 1.1 slice.29
  172.4 0.2 copy.44
  172.6 1.0 copy.46
  173.6 0.0 collective-permute-done.2
  173.6 1.1 maximum_select_fusion.1
  174.8 2.0 copy.43
  176.8 71.1 %shard_map.78 = bf16[32,16,64]{2,1,0:T(8,128)(2,1)S(1)} custom-call(s32[1]{0:T(128)S(6)} %copy.50.len_ref, bf16[32,2,128,64]{3,2,1,0:T(8,128)(2,1)S(1)} %bitcast.30, bf16[512,64]{1,0:T(8,128)(2,1)S(1)} %bitcast.35), custom_call_target="tpu_custom_call" | custom-call | flops 536870912 | bytes 1179648 | tf_op jit(solution)/shard_map/pallas_call | solution.py:212
  248.0 0.8 broadcast_in_dim_reshape.7
  (2 shorter events, 0.0 us)
Async XLA Ops:
  7.2 1.2 copy-start
  7.2 152.4 %all-gather.2.cloned.1.call-start = ((), (), s32[]{:S(2)}) async-start(), calls=%async_computation.1 | async-start | bytes 9437184 | tf_op jit(solution)/shard_map/all_gather | solution.py:242
  8.8 15.3 %copy-start.4 = (bf16[1,128,2048]{2,1,0:T(8,128)(2,1)S(1)}, bf16[1,128,2048]{2,1,0:T(8,128)(2,1)}, u32[]{:S(2)}) copy-start(bf16[1,128,2048]{2,1,0:T(8,128)(2,1)} %param.6) | copy-start | bytes 1572868
  9.1 13.6 %collective-permute-start = (bf16[2,2048,64]{1,2,0:T(8,128)(2,1)S(1)}, bf16[2,2048,64]{1,2,0:T(8,128)(2,1)S(1)}, u32[]{:S(2)}, u32[]{:S(2)}) collective-permute-start(bf16[2,2048,64]{1,2,0:T(8,128)(2,1)S(1)} %copy.47), channel_id=1, source_target_pairs={{0,32},{32,0},{1,33},{33,1},{2,34},{34,2},{3,35},{35,3},{4,36},{36... | collective-permute-start | bytes 1572872 | tf_op jit(solution)/shard_map/ppermute | solution.py:239
  24.0 3.0 %copy-start.5 = (bf16[1,16,2048]{2,1,0:T(8,128)(2,1)S(1)}, bf16[1,16,2048]{2,1,0:T(8,128)(2,1)}, u32[]{:S(2)}) copy-start(bf16[1,16,2048]{2,1,0:T(8,128)(2,1)} %param.9) | copy-start | bytes 196612
  29.0 66.4 %all-to-all-start = ((bf16[400,32,64]{0,2,1:T(8,128)(2,1)}), bf16[400,32,64]{0,2,1:T(8,128)(2,1)S(1)}, u32[]{:S(2)}, u32[]{:S(2)}) async-start(bf16[400,32,64]{0,2,1:T(8,128)(2,1)} %pad_maximum_fusion), calls=%async_computation | async-start | bytes 4194304 | tf_op jit(solution)/shard_map/all_to_all | solution.py:245
  95.4 1.9 copy-start.3
  102.7 1.2 copy-start.1
  152.7 1.0 copy-start.2
  155.5 4.1 %collective-permute-start.1 = (bf16[128,2048]{1,0:T(8,128)(2,1)S(1)}, bf16[128,2048]{1,0:T(8,128)(2,1)S(1)}, u32[]{:S(2)}, u32[]{:S(2)}) collective-permute-start(bf16[128,2048]{1,0:T(8,128)(2,1)S(1)} %copy.41), channel_id=1, source_target_pairs={{0,1},{1,0},{2,3},{3,2},{4,5},{5,4},{6,7},{7,6},{8,9},{9,8},{10,11... | collective-permute-start | bytes 1572872 | tf_op jit(solution)/shard_map/ppermute | solution.py:254
  168.9 4.8 %collective-permute-start.2 = (bf16[16,2,128,64]{2,3,1,0:T(8,128)(2,1)}, bf16[16,2,128,64]{2,3,1,0:T(8,128)(2,1)S(1)}, u32[]{:S(2)}, u32[]{:S(2)}) collective-permute-start(bf16[16,2,128,64]{2,3,1,0:T(8,128)(2,1)} %get-tuple-element.10), channel_id=1, source_target_pairs={{0,1},{1,0},{2,3},{3,2},{4,5},{5,4},{6,7},{7,6},{8,9},{9,8},{10,11... | collective-permute-start | bytes 1572872 | tf_op jit(solution)/shard_map/ppermute | solution.py:257
Sparse Core Ops, SparseCore 0:
  24.1 105.3 all-gather.1

commit v9 on v8

--- a/solution.py
+++ b/solution.py
@@ -69,7 +69,8 @@
     pl.semaphore_wait(barrier, n_dev - 1)
     length = len_ref[0]
 
-    def block(b, carry):
+    def block(step, carry):
+        b = lax.rem(step + me // 2, n_dev // 2)
         rows = pl.ds(pl.multiple_of(b * 2 * chunk, 2 * chunk), 2 * chunk)
         scores = lax.dot_general(
             q_ref[rows, :], k_ref[...], (((1,), (1,)), ((), ())), preferred_element_type=jnp.float32
@@ -148,17 +149,15 @@
     lax.fori_loop(0, n_dev, greet, 0)
     pl.semaphore_wait(barrier, n_dev - 1)
 
-    def send_memory(t, carry):
-        @pl.when(t != me)
-        def _():
-            pltpu.make_async_remote_copy(
-                src_ref=mem_ref.at[t], dst_ref=mem_in.at[me], send_sem=sems.at[0], recv_sem=sems.at[1],
-                device_id=place + (t,), device_id_type=MESH,
-            ).start()
-
-        return carry
-
-    lax.fori_loop(0, n_dev, send_memory, 0)
+    def send_memory(step, carry):
+        t = lax.rem(me + step, n_dev)
+        pltpu.make_async_remote_copy(
+            src_ref=mem_ref.at[t], dst_ref=mem_in.at[me], send_sem=sems.at[0], recv_sem=sems.at[1],
+            device_id=place + (t,), device_id_type=MESH,
+        ).start()
+        return carry
+
+    lax.fori_loop(1, n_dev, send_memory, 0)
     own = pltpu.make_async_copy(mem_ref.at[me], mem_in.at[me], sems.at[2])
     own.start()
     every = pltpu.make_async_remote_copy(
@@ -182,17 +181,15 @@
     context = (weighted / denominator).astype(jnp.bfloat16)
     ctx_buf[...] = context.reshape(n_dev, sum_chunk, context.shape[1])
 
-    def send_context(t, carry):
-        @pl.when(t != me)
-        def _():
-            pltpu.make_async_remote_copy(
-                src_ref=ctx_buf.at[t], dst_ref=out_ref.at[me], send_sem=sems.at[3], recv_sem=sems.at[4],
-                device_id=place + (t,), device_id_type=MESH,
-            ).start()
-
-        return carry
-
-    lax.fori_loop(0, n_dev, send_context, 0)
+    def send_context(step, carry):
+        t = lax.rem(me + step, n_dev)
+        pltpu.make_async_remote_copy(
+            src_ref=ctx_buf.at[t], dst_ref=out_ref.at[me], send_sem=sems.at[3], recv_sem=sems.at[4],
+            device_id=place + (t,), device_id_type=MESH,
+        ).start()
+        return carry
+
+    lax.fori_loop(1, n_dev, send_context, 0)
     back = pltpu.make_async_copy(ctx_buf.at[me], out_ref.at[me], sems.at[5])
     back.start()
     every.wait_send()

time: 256 us -> 250 us (0.977)
  Pallas kernels: 120 us -> 113 us
    pallas_call x1, Pallas kernels: 71.1 us -> 67.3 us  [summary_exchange(): pl.pallas_call(_summary_kernel, out_shape=jax.ShapeDtypeStruct((n_dev, nq...]
    pallas_call x1, Pallas kernels: 48.7 us -> 45.8 us  [attend_scatter(): pl.pallas_call(_attend_scatter_kernel, out_shape=jax.ShapeDtypeStruct((n_...]
  transfers between devices with their start and end apart: 5 -> 5, of which waited for: 3 -> 3; matrix products, arithmetic and copies ran while one was open for 6% -> 6% of each run, Pallas kernels for 19% -> 18%
where the time goes in v9:
time: 250 us; the launch traced here: 249 us
  Pallas kernels  113 us (45%)
  waiting for transfers between devices  59.1 us (24%)
  starting transfers between devices  26.6 us (11%)
  local copies, waits for them, and re-layouts  24.1 us (10%)
  between operations  14.9 us (6%)
  matrix products  6.75 us (3%)
  other arithmetic  4.15 us (2%)
    pallas_call x1, Pallas kernels, summary_exchange(): pl.pallas_call(_summary_kernel, out_shape=jax.ShapeDtypeStruct((n_dev, nq...  67.3 us
    all_to_all x1, waiting for transfers between devices, shards(): lax.all_to_all(jnp.concatenate([enc_query[0], enc_key[0], enc_value[0], s...  49.4 us
    pallas_call x1, Pallas kernels, attend_scatter(): pl.pallas_call(_attend_scatter_kernel, out_shape=jax.ShapeDtypeStruct((n_...  45.8 us
    all_to_all x1, starting transfers between devices, shards(): lax.all_to_all(jnp.concatenate([enc_query[0], enc_key[0], enc_value[0], s...  16.3 us
    ppermute x1, waiting for transfers between devices, shards(): w_pair = lax.ppermute(w_half, 'doc_x', perm=[(0, 1), (1, 0)])  8.15 us
    unnamed x18, local copies, waits for them, and re-layouts  8.11 us
    slice x4, local copies, waits for them, and re-layouts, shards(): mixed[:, i * rows:(i + 1) * rows].reshape(n_seq * rows, -1)  7.11 us
    dot_general x1, matrix products, shards(): jnp.einsum('tf,kfc->ktc', enc_pair, w_half, preferred_element_type=jnp.fl...  6.75 us
  transfers between devices with their start and end apart: 5, of which 3 were waited for; matrix products, arithmetic and copies ran while one was open for 6% of the time, Pallas kernels for 18%

profile of v9, /device:TPU:1, one launch (start us, length us, event | category | flops | bytes accessed | tf_op | source)
XLA Modules:
  0.0 248.8 jit_solution(5504357759224094355)
XLA Ops:
  7.2 0.0 copy-start
  7.2 0.0 all-gather.2.cloned.1.call-start
  7.2 1.2 copy-done
  8.4 0.4 constant_dynamic-slice_fusion
  8.8 0.0 copy-start.4
  8.8 0.3 copy.47
  9.1 5.5 %collective-permute-start = (bf16[2,2048,64]{1,2,0:T(8,128)(2,1)S(1)}, bf16[2,2048,64]{1,2,0:T(8,128)(2,1)S(1)}, u32[]{:S(2)}, u32[]{:S(2)}) collective-permute-start(bf16[2,2048,64]{1,2,0:T(8,128)(2,1)S(1)} %copy.47), channel_id=1, source_target_pairs={{0,32},{32,0},{1,33},{33,1},{2,34},{34,2},{3,35},{35,3},{4,36},{36... | collective-permute-start | bytes 1572872 | tf_op jit(solution)/shard_map/ppermute | solution.py:236
  14.6 8.1 %collective-permute-done = bf16[2,2048,64]{1,2,0:T(8,128)(2,1)S(1)} collective-permute-done((bf16[2,2048,64]{1,2,0:T(8,128)(2,1)S(1)}, bf16[2,2048,64]{1,2,0:T(8,128)(2,1)S(1)}, u32[]{:S(2)}, u32[]{:S(2)}) %collective-permute-start) | collective-permute-done | bytes 524320 | tf_op jit(solution)/shard_map/ppermute | solution.py:236
  22.8 1.2 maximum_select_fusion
  24.0 0.0 copy-start.5
  24.0 0.0 all-gather.2.cloned.1.call-update
  24.0 0.0 copy-done.4
  24.0 0.3 copy.30
  24.3 1.3 copy.31
  25.6 1.3 copy.32
  27.0 0.0 copy-done.5
  27.0 0.3 copy.33
  27.2 1.8 pad_maximum_fusion
  29.0 16.3 %all-to-all-start = ((bf16[400,32,64]{0,2,1:T(8,128)(2,1)}), bf16[400,32,64]{0,2,1:T(8,128)(2,1)S(1)}, u32[]{:S(2)}, u32[]{:S(2)}) async-start(bf16[400,32,64]{0,2,1:T(8,128)(2,1)} %pad_maximum_fusion), calls=%async_computation | async-start | bytes 4194304 | tf_op jit(solution)/shard_map/all_to_all | solution.py:242
  46.0 49.4 %all-to-all-done = bf16[400,32,64]{0,2,1:T(8,128)(2,1)S(1)} async-done(((bf16[400,32,64]{0,2,1:T(8,128)(2,1)}), bf16[400,32,64]{0,2,1:T(8,128)(2,1)S(1)}, u32[]{:S(2)}, u32[]{:S(2)}) %all-to-all-start) | async-done | bytes 1638432 | tf_op jit(solution)/shard_map/all_to_all | solution.py:242
  95.4 0.0 copy-start.3
  95.4 1.7 fusion.4
  97.1 0.2 copy-done.3
  97.3 1.5 copy.36
  98.8 1.5 copy.35
  100.3 2.4 copy.34
  102.7 0.0 copy-start.1
  102.7 1.2 copy-done.1
  104.0 45.8 %shard_map.77 = bf16[32,128,64]{2,1,0:T(8,128)(2,1)S(1)} custom-call(s32[1]{0:T(128)S(6)} %copy.50.len_ref, bf16[4096,64]{1,0:T(8,128)(2,1)S(1)} %bitcast.33, bf16[4096,64]{1,0:T(8,128)(2,1)S(1)} %bitcast.32, bf16[4096,64]{1,0:T(8,128)(2,1)S(1)} %bitcast.31), custom_call_target="tpu_custom_call" | custom-call | flops 4294967296 | bytes 2097152 | tf_op jit(solution)/shard_map/pallas_call | solution.py:115
  149.8 0.0 copy-start.2
  149.8 1.0 copy-done.2
  150.8 1.6 copy.37
  152.4 0.2 copy.41
  152.6 2.4 collective-permute-start.1
  155.0 1.5 collective-permute-done.1
  156.5 6.8 %fusion = bf16[2,256,1024]{1,2,0:T(8,128)(2,1)} fusion(bf16[2,2048,1024]{1,2,0:T(8,128)(2,1)} %all-gather.2.cloned.1.call-done, bf16[128,2048]{1,0:T(8,128)(2,1)S(1)} %collective-permute-done.1, bf16[128,2048]{1,0:T(8,128)(2,1)S(1)} %copy.41), kind=kOutput, calls=%fused_computation.2 | convolution fusion | flops 2150105088 | bytes 10485760 | tf_op jit(solution)/shard_map/tf,kfc->ktc/dot_general | solution.py:252
  163.3 1.3 reshape.44
  164.6 0.3 copy.49
  164.9 0.9 slice_bitcast_fusion.1
  165.8 2.4 collective-permute-start.2
  168.2 1.1 slice.29
  169.3 0.2 copy.44
  169.5 1.0 copy.46
  170.5 0.0 collective-permute-done.2
  170.5 1.1 maximum_select_fusion.1
  171.7 2.0 copy.43
  173.7 67.3 %shard_map.78 = bf16[32,16,64]{2,1,0:T(8,128)(2,1)S(1)} custom-call(s32[1]{0:T(128)S(6)} %copy.50.len_ref, bf16[32,2,128,64]{3,2,1,0:T(8,128)(2,1)S(1)} %bitcast.30, bf16[512,64]{1,0:T(8,128)(2,1)S(1)} %bitcast.35), custom_call_target="tpu_custom_call" | custom-call | flops 536870912 | bytes 1179648 | tf_op jit(solution)/shard_map/pallas_call | solution.py:209
  241.1 0.8 broadcast_in_dim_reshape.7
  (2 shorter events, 0.0 us)
Async XLA Ops:
  7.2 1.2 copy-start
  7.2 149.3 %all-gather.2.cloned.1.call-start = ((), (), s32[]{:S(2)}) async-start(), calls=%async_computation.1 | async-start | bytes 9437184 | tf_op jit(solution)/shard_map/all_gather | solution.py:239
  8.8 15.3 %copy-start.4 = (bf16[1,128,2048]{2,1,0:T(8,128)(2,1)S(1)}, bf16[1,128,2048]{2,1,0:T(8,128)(2,1)}, u32[]{:S(2)}) copy-start(bf16[1,128,2048]{2,1,0:T(8,128)(2,1)} %param.6) | copy-start | bytes 1572868
  9.1 13.6 %collective-permute-start = (bf16[2,2048,64]{1,2,0:T(8,128)(2,1)S(1)}, bf16[2,2048,64]{1,2,0:T(8,128)(2,1)S(1)}, u32[]{:S(2)}, u32[]{:S(2)}) collective-permute-start(bf16[2,2048,64]{1,2,0:T(8,128)(2,1)S(1)} %copy.47), channel_id=1, source_target_pairs={{0,32},{32,0},{1,33},{33,1},{2,34},{34,2},{3,35},{35,3},{4,36},{36... | collective-permute-start | bytes 1572872 | tf_op jit(solution)/shard_map/ppermute | solution.py:236
  24.0 3.0 %copy-start.5 = (bf16[1,16,2048]{2,1,0:T(8,128)(2,1)S(1)}, bf16[1,16,2048]{2,1,0:T(8,128)(2,1)}, u32[]{:S(2)}) copy-start(bf16[1,16,2048]{2,1,0:T(8,128)(2,1)} %param.9) | copy-start | bytes 196612
  29.0 66.4 %all-to-all-start = ((bf16[400,32,64]{0,2,1:T(8,128)(2,1)}), bf16[400,32,64]{0,2,1:T(8,128)(2,1)S(1)}, u32[]{:S(2)}, u32[]{:S(2)}) async-start(bf16[400,32,64]{0,2,1:T(8,128)(2,1)} %pad_maximum_fusion), calls=%async_computation | async-start | bytes 4194304 | tf_op jit(solution)/shard_map/all_to_all | solution.py:242
  95.4 1.9 copy-start.3
  102.7 1.2 copy-start.1
  149.8 1.0 copy-start.2
  152.6 3.9 %collective-permute-start.1 = (bf16[128,2048]{1,0:T(8,128)(2,1)S(1)}, bf16[128,2048]{1,0:T(8,128)(2,1)S(1)}, u32[]{:S(2)}, u32[]{:S(2)}) collective-permute-start(bf16[128,2048]{1,0:T(8,128)(2,1)S(1)} %copy.41), channel_id=1, source_target_pairs={{0,1},{1,0},{2,3},{3,2},{4,5},{5,4},{6,7},{7,6},{8,9},{9,8},{10,11... | collective-permute-start | bytes 1572872 | tf_op jit(solution)/shard_map/ppermute | solution.py:251
  165.8 4.8 %collective-permute-start.2 = (bf16[16,2,128,64]{2,3,1,0:T(8,128)(2,1)}, bf16[16,2,128,64]{2,3,1,0:T(8,128)(2,1)S(1)}, u32[]{:S(2)}, u32[]{:S(2)}) collective-permute-start(bf16[16,2,128,64]{2,3,1,0:T(8,128)(2,1)} %get-tuple-element.10), channel_id=1, source_target_pairs={{0,1},{1,0},{2,3},{3,2},{4,5},{5,4},{6,7},{7,6},{8,9},{9,8},{10,11... | collective-permute-start | bytes 1572872 | tf_op jit(solution)/shard_map/ppermute | solution.py:254
Sparse Core Ops, SparseCore 0:
  24.1 105.3 all-gather.1

commit v10 on v7

--- a/solution.py
+++ b/solution.py
@@ -69,7 +69,8 @@
     pl.semaphore_wait(barrier, n_dev - 1)
     length = len_ref[0]
 
-    def block(b, carry):
+    def block(step, carry):
+        b = lax.rem(step + me // 2, n_dev // 2)
         rows = pl.ds(pl.multiple_of(b * 2 * chunk, 2 * chunk), 2 * chunk)
         scores = lax.dot_general(
             q_ref[rows, :], k_ref[...], (((1,), (1,)), ((), ())), preferred_element_type=jnp.float32

time: 238 us -> 235 us (0.987)
  Pallas kernels: 52.8 us -> 49.9 us
    pallas_call x1, Pallas kernels: 48.7 us -> 45.8 us  [attend_scatter(): pl.pallas_call(_attend_scatter_kernel, out_shape=jax.ShapeDtypeStruct((n_...]
  transfers between devices with their start and end apart: 7 -> 7, of which waited for: 6 -> 6; matrix products, arithmetic and copies ran while one was open for 6% -> 6% of each run, Pallas kernels for 21% -> 20%
where the time goes in v10:
time: 235 us; the launch traced here: 234 us
  waiting for transfers between devices  94.7 us (40%)
  Pallas kernels  49.9 us (21%)
  starting transfers between devices  39.3 us (17%)
  local copies, waits for them, and re-layouts  25.3 us (11%)
  between operations  15 us (6%)
  matrix products  6.75 us (3%)
  other arithmetic  3.21 us (1%)
    all_to_all x1, waiting for transfers between devices, shards(): lax.all_to_all(jnp.concatenate([enc_query[0], enc_key[0], enc_value[0], s...  49.4 us
    pallas_call x1, Pallas kernels, attend_scatter(): pl.pallas_call(_attend_scatter_kernel, out_shape=jax.ShapeDtypeStruct((n_...  45.8 us
    all_to_all x1, waiting for transfers between devices, shards(): lax.all_to_all(by_head, 'seq', split_axis=0, concat_axis=2, tiled=True)  26.7 us
    all_to_all x1, starting transfers between devices, shards(): lax.all_to_all(jnp.concatenate([enc_query[0], enc_key[0], enc_value[0], s...  16.3 us
    unnamed x28, local copies, waits for them, and re-layouts  8.93 us
    ppermute x1, waiting for transfers between devices, shards(): w_pair = lax.ppermute(w_half, 'doc_x', perm=[(0, 1), (1, 0)])  8.14 us
    all_to_all x1, starting transfers between devices, shards(): lax.all_to_all(by_head, 'seq', split_axis=0, concat_axis=2, tiled=True)  7.84 us
    all_to_all x1, waiting for transfers between devices, shards(): lax.all_to_all(answer, 'seq', split_axis=0, concat_axis=1, tiled=True)  7.41 us
  transfers between devices with their start and end apart: 7, of which 6 were waited for; matrix products, arithmetic and copies ran while one was open for 6% of the time, Pallas kernels for 20%

profile of v10, /device:TPU:1, one launch (start us, length us, event | category | flops | bytes accessed | tf_op | source)
XLA Modules:
  0.0 234.2 jit_solution(13934739522143251238)
XLA Ops:
  7.2 0.0 all-gather.2.cloned.1.call-start
  7.2 1.2 copy-done
  8.4 0.4 constant_dynamic-slice_fusion
  8.8 0.3 copy.50
  9.1 5.6 %collective-permute-start = (bf16[2,2048,64]{1,2,0:T(8,128)(2,1)S(1)}, bf16[2,2048,64]{1,2,0:T(8,128)(2,1)S(1)}, u32[]{:S(2)}, u32[]{:S(2)}) collective-permute-start(bf16[2,2048,64]{1,2,0:T(8,128)(2,1)S(1)} %copy.50), channel_id=1, source_target_pairs={{0,32},{32,0},{1,33},{33,1},{2,34},{34,2},{3,35},{35,3},{4,36},{36... | collective-permute-start | bytes 1572872 | tf_op jit(solution)/shard_map/ppermute | solution.py:142
  14.8 8.1 %collective-permute-done = bf16[2,2048,64]{1,2,0:T(8,128)(2,1)S(1)} collective-permute-done((bf16[2,2048,64]{1,2,0:T(8,128)(2,1)S(1)}, bf16[2,2048,64]{1,2,0:T(8,128)(2,1)S(1)}, u32[]{:S(2)}, u32[]{:S(2)}) %collective-permute-start) | collective-permute-done | bytes 524320 | tf_op jit(solution)/shard_map/ppermute | solution.py:142
  22.9 1.3 maximum_select_fusion
  24.2 0.3 copy.35
  24.5 0.3 copy.34
  24.8 0.3 copy.33
  25.0 1.3 copy.32
  26.4 1.8 pad_maximum_fusion
  28.1 16.3 %all-to-all-start = ((bf16[400,32,64]{0,2,1:T(8,128)(2,1)}), bf16[400,32,64]{0,2,1:T(8,128)(2,1)S(1)}, u32[]{:S(2)}, u32[]{:S(2)}) async-start(bf16[400,32,64]{0,2,1:T(8,128)(2,1)} %pad_maximum_fusion), calls=%async_computation | async-start | bytes 4194304 | tf_op jit(solution)/shard_map/all_to_all | solution.py:148
  45.1 49.4 %all-to-all-done = bf16[400,32,64]{0,2,1:T(8,128)(2,1)S(1)} async-done(((bf16[400,32,64]{0,2,1:T(8,128)(2,1)}), bf16[400,32,64]{0,2,1:T(8,128)(2,1)S(1)}, u32[]{:S(2)}, u32[]{:S(2)}) %all-to-all-start) | async-done | bytes 1638432 | tf_op jit(solution)/shard_map/all_to_all | solution.py:148
  94.5 1.7 fusion.4
  96.2 0.1 copy-done.3
  96.4 1.5 copy.36
  97.9 1.5 copy.37
  99.4 2.4 %copy.38 = bf16[32,128,64]{2,1,0:T(8,128)(2,1)} copy(bf16[32,128,64]{1,2,0:T(8,128)(2,1)} %get-tuple-element.8) | data formatting | bytes 1048576 | tf_op jit(solution)/shard_map/slice | solution.py:152
  101.8 1.2 copy-done.1
  103.1 45.8 %shard_map.77 = bf16[32,128,64]{2,1,0:T(8,128)(2,1)S(1)} custom-call(s32[1]{0:T(128)S(6)} %copy.53.len_ref, bf16[4096,64]{1,0:T(8,128)(2,1)S(1)} %bitcast.39, bf16[4096,64]{1,0:T(8,128)(2,1)S(1)} %bitcast.40, bf16[4096,64]{1,0:T(8,128)(2,1)S(1)} %bitcast.41), custom_call_target="tpu_custom_call" | custom-call | flops 4294967296 | bytes 2097152 | tf_op jit(solution)/shard_map/pallas_call | solution.py:115
  148.9 1.0 copy-done.2
  149.9 1.6 copy.39
  151.5 0.2 copy.44
  151.8 2.4 %collective-permute-start.1 = (bf16[128,2048]{1,0:T(8,128)(2,1)S(1)}, bf16[128,2048]{1,0:T(8,128)(2,1)S(1)}, u32[]{:S(2)}, u32[]{:S(2)}) collective-permute-start(bf16[128,2048]{1,0:T(8,128)(2,1)S(1)} %copy.44), channel_id=1, source_target_pairs={{0,1},{1,0},{2,3},{3,2},{4,5},{5,4},{6,7},{7,6},{8,9},{9,8},{10,11... | collective-permute-start | bytes 1572872 | tf_op jit(solution)/shard_map/ppermute | solution.py:157
  154.1 1.5 collective-permute-done.1
  155.6 6.8 %fusion = bf16[2,256,1024]{1,2,0:T(8,128)(2,1)} fusion(bf16[2,2048,1024]{1,2,0:T(8,128)(2,1)} %all-gather.2.cloned.1.call-done, bf16[128,2048]{1,0:T(8,128)(2,1)S(1)} %collective-permute-done.1, bf16[128,2048]{1,0:T(8,128)(2,1)S(1)} %copy.44), kind=kOutput, calls=%fused_computation.2 | convolution fusion | flops 2150105088 | bytes 10485760 | tf_op jit(solution)/shard_map/tf,kfc->ktc/dot_general | solution.py:158
  162.4 1.3 reshape.49
  163.7 0.3 copy.52
  164.0 0.1 slice_bitcast_fusion.3
  164.1 2.3 collective-permute-start.2
  166.4 1.5 collective-permute-done.2
  167.9 0.2 maximum_select_fusion.1
  168.1 1.1 copy.46
  169.2 7.8 %all-to-all-start.1 = ((bf16[32,2,128,64]{2,3,1,0:T(8,128)(2,1)}), bf16[32,2,128,64]{2,3,1,0:T(8,128)(2,1)S(1)}, u32[]{:S(2)}, u32[]{:S(2)}) async-start(bf16[32,2,128,64]{2,3,1,0:T(8,128)(2,1)} %bitcast.18), calls=%async_computation.1 | async-start | bytes 2097152 | tf_op jit(solution)/shard_map/all_to_all | solution.py:163
  177.0 1.1 slice.35
  178.1 0.2 copy.40
  178.3 26.7 %all-to-all-done.1 = bf16[32,2,128,64]{2,3,1,0:T(8,128)(2,1)S(1)} async-done(((bf16[32,2,128,64]{2,3,1,0:T(8,128)(2,1)}), bf16[32,2,128,64]{2,3,1,0:T(8,128)(2,1)S(1)}, u32[]{:S(2)}, u32[]{:S(2)}) %all-to-all-start.1) | async-done | bytes 1048608 | tf_op jit(solution)/shard_map/all_to_all | solution.py:163
  205.0 1.0 copy-done.6
  206.0 2.0 copy.47
  208.1 0.1 slice_bitcast_fusion
  208.2 4.1 %shard_map.78 = bf16[512,64]{1,0:T(8,128)(2,1)S(1)} custom-call(s32[1]{0:T(128)S(6)} %copy.53.len_ref, bf16[512,64]{1,0:T(8,128)(2,1)S(1)} %bitcast.43, bf16[4096,64]{1,0:T(8,128)(2,1)S(1)} %get-tuple-element.7.k_ref, bf16[4096,64]{1,0:T(8,128)(2,1)S(1)} %get-tuple-element.6.v_ref), custom_call_target="tpu_custom_call" | custom-call | flops 536870912 | bytes 1179648 | tf_op jit(solution)/shard_map/pallas_call | solution.py:43
  212.3 0.8 reshape.51
  213.0 4.9 %all-to-all-start.2 = ((bf16[32,2,512]{2,1,0:T(2,128)(2,1)}), bf16[32,2,512]{2,1,0:T(2,128)(2,1)S(1)}, u32[]{:S(2)}, u32[]{:S(2)}) async-start(bf16[32,2,512]{2,1,0:T(2,128)(2,1)} %reshape.51), calls=%async_computation.2 | async-start | bytes 131072 | tf_op jit(solution)/shard_map/all_to_all | solution.py:166
  217.9 1.0 copy.49
  218.9 7.4 %all-to-all-done.2 = bf16[32,2,512]{2,1,0:T(2,128)(2,1)S(1)} async-done(((bf16[32,2,512]{2,1,0:T(2,128)(2,1)}), bf16[32,2,512]{2,1,0:T(2,128)(2,1)S(1)}, u32[]{:S(2)}, u32[]{:S(2)}) %all-to-all-start.2) | async-done | bytes 65568 | tf_op jit(solution)/shard_map/all_to_all | solution.py:166
  226.3 0.1 reshape.52
  226.5 0.8 broadcast_in_dim.3
  (18 shorter events, 0.1 us)
Async XLA Ops:
  7.2 1.2 copy-start
  7.2 148.5 %all-gather.2.cloned.1.call-start = ((), (), s32[]{:S(2)}) async-start(), calls=%async_computation.3 | async-start | bytes 9437184 | tf_op jit(solution)/shard_map/all_gather | solution.py:145
  8.8 15.4 %copy-start.9 = (bf16[1,16,2048]{2,1,0:T(8,128)(2,1)S(1)}, bf16[1,16,2048]{2,1,0:T(8,128)(2,1)}, u32[]{:S(2)}) copy-start(bf16[1,16,2048]{2,1,0:T(8,128)(2,1)} %param.9) | copy-start | bytes 196612
  9.1 15.4 %copy-start.7 = (bf16[1,128,2048]{2,1,0:T(8,128)(2,1)S(1)}, bf16[1,128,2048]{2,1,0:T(8,128)(2,1)}, u32[]{:S(2)}) copy-start(bf16[1,128,2048]{2,1,0:T(8,128)(2,1)} %param.8) | copy-start | bytes 1572868
  9.1 13.8 %collective-permute-start = (bf16[2,2048,64]{1,2,0:T(8,128)(2,1)S(1)}, bf16[2,2048,64]{1,2,0:T(8,128)(2,1)S(1)}, u32[]{:S(2)}, u32[]{:S(2)}) collective-permute-start(bf16[2,2048,64]{1,2,0:T(8,128)(2,1)S(1)} %copy.50), channel_id=1, source_target_pairs={{0,32},{32,0},{1,33},{33,1},{2,34},{34,2},{3,35},{35,3},{4,36},{36... | collective-permute-start | bytes 1572872 | tf_op jit(solution)/shard_map/ppermute | solution.py:142
  14.7 10.0 %copy-start.8 = (bf16[1,128,2048]{2,1,0:T(8,128)(2,1)S(1)}, bf16[1,128,2048]{2,1,0:T(8,128)(2,1)}, u32[]{:S(2)}) copy-start(bf16[1,128,2048]{2,1,0:T(8,128)(2,1)} %param.7) | copy-start | bytes 1572868
  28.1 66.4 %all-to-all-start = ((bf16[400,32,64]{0,2,1:T(8,128)(2,1)}), bf16[400,32,64]{0,2,1:T(8,128)(2,1)S(1)}, u32[]{:S(2)}, u32[]{:S(2)}) async-start(bf16[400,32,64]{0,2,1:T(8,128)(2,1)} %pad_maximum_fusion), calls=%async_computation | async-start | bytes 4194304 | tf_op jit(solution)/shard_map/all_to_all | solution.py:148
  94.5 1.8 copy-start.3
  101.8 1.2 copy-start.1
  148.9 1.0 copy-start.2
  151.5 10.9 %copy-start.4 = (bf16[128,32,64]{0,2,1:T(8,128)(2,1)}, bf16[128,32,64]{0,2,1:T(8,128)(2,1)S(1)}, u32[]{:S(2)}) copy-start(bf16[128,32,64]{0,2,1:T(8,128)(2,1)S(1)} %copy.39) | copy-start | bytes 1572868
  151.8 3.9 %collective-permute-start.1 = (bf16[128,2048]{1,0:T(8,128)(2,1)S(1)}, bf16[128,2048]{1,0:T(8,128)(2,1)S(1)}, u32[]{:S(2)}, u32[]{:S(2)}) collective-permute-start(bf16[128,2048]{1,0:T(8,128)(2,1)S(1)} %copy.44), channel_id=1, source_target_pairs={{0,1},{1,0},{2,3},{3,2},{4,5},{5,4},{6,7},{7,6},{8,9},{9,8},{10,11... | collective-permute-start | bytes 1572872 | tf_op jit(solution)/shard_map/ppermute | solution.py:157
  164.1 3.8 %collective-permute-start.2 = (bf16[16,2,128,64]{2,3,1,0:T(8,128)(2,1)S(1)}, bf16[16,2,128,64]{2,3,1,0:T(8,128)(2,1)S(1)}, u32[]{:S(2)}, u32[]{:S(2)}) collective-permute-start(bf16[16,2,128,64]{2,3,1,0:T(8,128)(2,1)S(1)} %get-tuple-element.12), channel_id=1, source_target_pairs={{0,1},{1,0},{2,3},{3,2},{4,5},{5,4},{6,7},{7,6},{8,9},{9,8},{10,11... | collective-permute-start | bytes 1572872 | tf_op jit(solution)/shard_map/ppermute | solution.py:160
  169.2 35.8 %all-to-all-start.1 = ((bf16[32,2,128,64]{2,3,1,0:T(8,128)(2,1)}), bf16[32,2,128,64]{2,3,1,0:T(8,128)(2,1)S(1)}, u32[]{:S(2)}, u32[]{:S(2)}) async-start(bf16[32,2,128,64]{2,3,1,0:T(8,128)(2,1)} %bitcast.18), calls=%async_computation.1 | async-start | bytes 2097152 | tf_op jit(solution)/shard_map/all_to_all | solution.py:163
  205.0 1.0 copy-start.6
  208.2 9.7 %copy-start.5 = (bf16[128,32,64]{0,2,1:T(8,128)(2,1)S(1)}, bf16[128,32,64]{0,2,1:T(8,128)(2,1)}, u32[]{:S(2)}) copy-start(bf16[128,32,64]{0,2,1:T(8,128)(2,1)} %copy-done.4) | copy-start | bytes 1572868
  213.0 13.3 %all-to-all-start.2 = ((bf16[32,2,512]{2,1,0:T(2,128)(2,1)}), bf16[32,2,512]{2,1,0:T(2,128)(2,1)S(1)}, u32[]{:S(2)}, u32[]{:S(2)}) async-start(bf16[32,2,512]{2,1,0:T(2,128)(2,1)} %reshape.51), calls=%async_computation.2 | async-start | bytes 131072 | tf_op jit(solution)/shard_map/all_to_all | solution.py:166
Sparse Core Ops, SparseCore 0:
  24.3 105.3 all-gather.1

commit v11 on v10

--- a/solution.py
+++ b/solution.py
@@ -107,7 +107,7 @@
     own.wait()
 
 
-def attend_scatter(queries, keys_in, values_in, length, n_dev):
+def attend_scatter(queries, keys_in, values_in, length, n_dev, collective_id):
     nq, width = queries.shape
     chunk = nq // n_dev
     nk = keys_in.shape[0]
@@ -127,7 +127,7 @@
             flops=4 * nq * nk * width, transcendentals=nq * nk, bytes_accessed=2 * (2 * nq * width + 2 * nk * width)
         ),
         compiler_params=pltpu.CompilerParams(
-            collective_id=1, has_side_effects=True, vmem_limit_bytes=48 * 1024 * 1024
+            collective_id=collective_id, has_side_effects=True, vmem_limit_bytes=48 * 1024 * 1024
         ),
     )(length.reshape(1), queries, keys_in, values_in)
 
@@ -151,7 +151,7 @@
     ).reshape(n_seq, 3 * rows + sum_rows, -1)
     head_query, head_key, head_value = (mixed[:, i * rows:(i + 1) * rows].reshape(n_seq * rows, -1) for i in range(3))
     summary_heads = mixed[:, 3 * rows:].reshape(n_seq * sum_rows, -1)
-    by_head = attend_scatter(head_query, head_key, head_value, length, n_seq)
+    by_head = attend_scatter(head_query, head_key, head_value, length, n_seq, 1)
     encoder_out = by_head.transpose(1, 0, 2).reshape(by_head.shape[1], -1)
 
     enc_pair = jnp.concatenate([encoder_out, lax.ppermute(encoder_out, "seq", sibling)], axis=0)
@@ -162,8 +162,8 @@
     by_head = by_head.reshape(n_seq, 2, rows, half)
     memory = lax.all_to_all(by_head, "seq", split_axis=0, concat_axis=2, tiled=True)
     memory_keys, memory_values = memory[0, 0], memory[0, 1]
-    answer = attend_head(summary_heads, memory_keys, memory_values, length)
-    summary_out = lax.all_to_all(answer, "seq", split_axis=0, concat_axis=1, tiled=True)
+    answer = attend_scatter(summary_heads, memory_keys, memory_values, length, n_seq, 2)
+    summary_out = answer.transpose(1, 0, 2).reshape(answer.shape[1], -1)
     return (encoder_out[None], summary_out[None])
 
 

time: 235 us -> 237 us (level)
  Pallas kernels: 49.9 us -> 64.6 us
  waiting for transfers between devices: 94.7 us -> 86.5 us
  starting transfers between devices: 39.3 us -> 34.5 us
    pallas_call x1 -> x2, Pallas kernels: 45.8 us -> 64.6 us  [attend_scatter(): pl.pallas_call(_attend_scatter_kernel, out_shape=jax.ShapeDtypeStruct((n_...]
    all_to_all x1 -> x0, waiting for transfers between devices: 7.41 us -> none  [shards(): lax.all_to_all(answer, 'seq', split_axis=0, concat_axis=1, tiled=True)]
    all_to_all x1 -> x0, starting transfers between devices: 4.87 us -> none  [shards(): lax.all_to_all(answer, 'seq', split_axis=0, concat_axis=1, tiled=True)]
    pallas_call x1 -> x0, Pallas kernels: 4.05 us -> none  [attend_head(): pl.pallas_call(_attend_kernel, grid_spec=grid_spec, out_shape=jax.ShapeDt...]
    unnamed x28 -> x20, local copies, waits for them, and re-layouts: 8.93 us -> 9.08 us
  transfers between devices with their start and end apart: 7 -> 6, of which waited for: 6 -> 5; matrix products, arithmetic and copies ran while one was open for 6% -> 7% of each run, Pallas kernels for 20% -> 19%
where the time goes in v11:
time: 237 us; the launch traced here: 236 us
  waiting for transfers between devices  86.5 us (36%)
  Pallas kernels  64.6 us (27%)
  starting transfers between devices  34.5 us (15%)
  local copies, waits for them, and re-layouts  25.5 us (11%)
  between operations  14.9 us (6%)
  matrix products  6.74 us (3%)
  other arithmetic  3.18 us (1%)
    pallas_call x2, Pallas kernels, attend_scatter(): pl.pallas_call(_attend_scatter_kernel, out_shape=jax.ShapeDtypeStruct((n_...  64.6 us
    all_to_all x1, waiting for transfers between devices, shards(): lax.all_to_all(jnp.concatenate([enc_query[0], enc_key[0], enc_value[0], s...  49.4 us
    all_to_all x1, waiting for transfers between devices, shards(): lax.all_to_all(by_head, 'seq', split_axis=0, concat_axis=2, tiled=True)  25.8 us
    all_to_all x1, starting transfers between devices, shards(): lax.all_to_all(jnp.concatenate([enc_query[0], enc_key[0], enc_value[0], s...  16.3 us
    unnamed x20, local copies, waits for them, and re-layouts  9.08 us
    ppermute x1, waiting for transfers between devices, shards(): w_pair = lax.ppermute(w_half, 'doc_x', perm=[(0, 1), (1, 0)])  8.15 us
    all_to_all x1, starting transfers between devices, shards(): lax.all_to_all(by_head, 'seq', split_axis=0, concat_axis=2, tiled=True)  7.84 us
    slice x4, local copies, waits for them, and re-layouts, shards(): mixed[:, i * rows:(i + 1) * rows].reshape(n_seq * rows, -1)  7.15 us
  transfers between devices with their start and end apart: 6, of which 5 were waited for; matrix products, arithmetic and copies ran while one was open for 7% of the time, Pallas kernels for 19%

profile of v11, /device:TPU:1, one launch (start us, length us, event | category | flops | bytes accessed | tf_op | source)
XLA Modules:
  0.0 235.9 jit_solution(16265689922553980157)
XLA Ops:
  7.2 0.0 copy-start
  7.2 0.0 all-gather.2.cloned.1.call-start
  7.2 1.2 copy-done
  8.4 0.4 constant_dynamic-slice_fusion
  8.8 0.0 copy-start.6
  8.8 0.3 copy.49
  9.1 0.0 copy-start.5
  9.1 5.6 %collective-permute-start = (bf16[2,2048,64]{1,2,0:T(8,128)(2,1)S(1)}, bf16[2,2048,64]{1,2,0:T(8,128)(2,1)S(1)}, u32[]{:S(2)}, u32[]{:S(2)}) collective-permute-start(bf16[2,2048,64]{1,2,0:T(8,128)(2,1)S(1)} %copy.49), channel_id=1, source_target_pairs={{0,32},{32,0},{1,33},{33,1},{2,34},{34,2},{3,35},{35,3},{4,36},{36... | collective-permute-start | bytes 1572872 | tf_op jit(solution)/shard_map/ppermute | solution.py:142
  14.7 8.1 %collective-permute-done = bf16[2,2048,64]{1,2,0:T(8,128)(2,1)S(1)} collective-permute-done((bf16[2,2048,64]{1,2,0:T(8,128)(2,1)S(1)}, bf16[2,2048,64]{1,2,0:T(8,128)(2,1)S(1)}, u32[]{:S(2)}, u32[]{:S(2)}) %collective-permute-start) | collective-permute-done | bytes 524320 | tf_op jit(solution)/shard_map/ppermute | solution.py:142
  22.9 1.2 maximum_select_fusion
  24.1 0.0 all-gather.2.cloned.1.call-update
  24.2 0.3 copy.34
  24.5 0.3 copy.33
  24.7 1.3 copy.32
  26.1 1.3 copy.31
  27.4 1.8 pad_maximum_fusion
  29.1 16.3 %all-to-all-start = ((bf16[400,32,64]{0,2,1:T(8,128)(2,1)}), bf16[400,32,64]{0,2,1:T(8,128)(2,1)S(1)}, u32[]{:S(2)}, u32[]{:S(2)}) async-start(bf16[400,32,64]{0,2,1:T(8,128)(2,1)} %pad_maximum_fusion), calls=%async_computation | async-start | bytes 4194304 | tf_op jit(solution)/shard_map/all_to_all | solution.py:148
  46.1 49.4 %all-to-all-done = bf16[400,32,64]{0,2,1:T(8,128)(2,1)S(1)} async-done(((bf16[400,32,64]{0,2,1:T(8,128)(2,1)}), bf16[400,32,64]{0,2,1:T(8,128)(2,1)S(1)}, u32[]{:S(2)}, u32[]{:S(2)}) %all-to-all-start) | async-done | bytes 1638432 | tf_op jit(solution)/shard_map/all_to_all | solution.py:148
  95.5 1.7 fusion.4
  97.3 0.2 copy-done.3
  97.4 1.5 copy.35
  99.0 1.5 copy.36
  100.5 2.4 %copy.37 = bf16[32,128,64]{2,1,0:T(8,128)(2,1)} copy(bf16[32,128,64]{1,2,0:T(8,128)(2,1)} %get-tuple-element.8) | data formatting | bytes 1048576 | tf_op jit(solution)/shard_map/slice | solution.py:152
  102.9 1.2 copy-done.1
  104.1 45.8 %shard_map.77 = bf16[32,128,64]{2,1,0:T(8,128)(2,1)S(1)} custom-call(s32[1]{0:T(128)S(6)} %copy.52.len_ref, bf16[4096,64]{1,0:T(8,128)(2,1)S(1)} %bitcast.38, bf16[4096,64]{1,0:T(8,128)(2,1)S(1)} %bitcast.39, bf16[4096,64]{1,0:T(8,128)(2,1)S(1)} %bitcast.40), custom_call_target="tpu_custom_call" | custom-call | flops 4294967296 | bytes 2097152 | tf_op jit(solution)/shard_map/pallas_call | solution.py:115
  150.0 1.0 copy-done.2
  151.0 1.6 copy.38
  152.6 0.2 copy.43
  152.8 2.4 %collective-permute-start.1 = (bf16[128,2048]{1,0:T(8,128)(2,1)S(1)}, bf16[128,2048]{1,0:T(8,128)(2,1)S(1)}, u32[]{:S(2)}, u32[]{:S(2)}) collective-permute-start(bf16[128,2048]{1,0:T(8,128)(2,1)S(1)} %copy.43), channel_id=1, source_target_pairs={{0,1},{1,0},{2,3},{3,2},{4,5},{5,4},{6,7},{7,6},{8,9},{9,8},{10,11... | collective-permute-start | bytes 1572872 | tf_op jit(solution)/shard_map/ppermute | solution.py:157
  155.2 1.5 collective-permute-done.1
  156.7 6.7 %fusion = bf16[2,256,1024]{1,2,0:T(8,128)(2,1)} fusion(bf16[2,2048,1024]{1,2,0:T(8,128)(2,1)} %all-gather.2.cloned.1.call-done, bf16[128,2048]{1,0:T(8,128)(2,1)S(1)} %collective-permute-done.1, bf16[128,2048]{1,0:T(8,128)(2,1)S(1)} %copy.43), kind=kOutput, calls=%fused_computation.2 | convolution fusion | flops 2150105088 | bytes 10485760 | tf_op jit(solution)/shard_map/tf,kfc->ktc/dot_general | solution.py:158
  163.4 1.3 reshape.45
  164.8 0.3 copy.51
  165.0 0.1 slice_bitcast_fusion.3
  165.1 2.3 collective-permute-start.2
  167.4 1.5 collective-permute-done.2
  168.9 0.2 maximum_select_fusion.1
  169.1 1.1 copy.45
  170.2 7.8 %all-to-all-start.1 = ((bf16[32,2,128,64]{2,3,1,0:T(8,128)(2,1)}), bf16[32,2,128,64]{2,3,1,0:T(8,128)(2,1)S(1)}, u32[]{:S(2)}, u32[]{:S(2)}) async-start(bf16[32,2,128,64]{2,3,1,0:T(8,128)(2,1)} %bitcast.50), calls=%async_computation.1 | async-start | bytes 2097152 | tf_op jit(solution)/shard_map/all_to_all | solution.py:163
  178.0 1.1 slice.35
  179.1 1.0 copy.48
  180.1 0.2 copy.39
  180.3 25.8 %all-to-all-done.1 = bf16[32,2,128,64]{2,3,1,0:T(8,128)(2,1)S(1)} async-done(((bf16[32,2,128,64]{2,3,1,0:T(8,128)(2,1)}), bf16[32,2,128,64]{2,3,1,0:T(8,128)(2,1)S(1)}, u32[]{:S(2)}, u32[]{:S(2)}) %all-to-all-start.1) | async-done | bytes 1048608 | tf_op jit(solution)/shard_map/all_to_all | solution.py:163
  206.2 1.0 copy-done.4
  207.1 2.0 copy.46
  209.2 0.1 slice_bitcast_fusion
  209.3 18.8 %shard_map.78 = bf16[32,16,64]{2,1,0:T(8,128)(2,1)S(1)} custom-call(s32[1]{0:T(128)S(6)} %copy.52.len_ref, bf16[512,64]{1,0:T(8,128)(2,1)S(1)} %bitcast.42, bf16[4096,64]{1,0:T(8,128)(2,1)S(1)} %get-tuple-element.7.k_ref, bf16[4096,64]{1,0:T(8,128)(2,1)S(1)} %get-tuple-element.6.v_ref), custom_call_target="tpu_custom_call" | custom-call | flops 536870912 | bytes 1179648 | tf_op jit(solution)/shard_map/pallas_call | solution.py:115
  228.2 0.8 broadcast_in_dim_reshape.7
  (8 shorter events, 0.0 us)
Async XLA Ops:
  7.2 1.2 copy-start
  7.2 149.5 %all-gather.2.cloned.1.call-start = ((), (), s32[]{:S(2)}) async-start(), calls=%async_computation.2 | async-start | bytes 9437184 | tf_op jit(solution)/shard_map/all_gather | solution.py:145
  8.8 15.4 %copy-start.6 = (bf16[1,16,2048]{2,1,0:T(8,128)(2,1)S(1)}, bf16[1,16,2048]{2,1,0:T(8,128)(2,1)}, u32[]{:S(2)}) copy-start(bf16[1,16,2048]{2,1,0:T(8,128)(2,1)} %param.9) | copy-start | bytes 196612
  9.1 15.3 %copy-start.5 = (bf16[1,128,2048]{2,1,0:T(8,128)(2,1)S(1)}, bf16[1,128,2048]{2,1,0:T(8,128)(2,1)}, u32[]{:S(2)}) copy-start(bf16[1,128,2048]{2,1,0:T(8,128)(2,1)} %param.8) | copy-start | bytes 1572868
  9.1 13.8 %collective-permute-start = (bf16[2,2048,64]{1,2,0:T(8,128)(2,1)S(1)}, bf16[2,2048,64]{1,2,0:T(8,128)(2,1)S(1)}, u32[]{:S(2)}, u32[]{:S(2)}) collective-permute-start(bf16[2,2048,64]{1,2,0:T(8,128)(2,1)S(1)} %copy.49), channel_id=1, source_target_pairs={{0,32},{32,0},{1,33},{33,1},{2,34},{34,2},{3,35},{35,3},{4,36},{36... | collective-permute-start | bytes 1572872 | tf_op jit(solution)/shard_map/ppermute | solution.py:142
  29.1 66.4 %all-to-all-start = ((bf16[400,32,64]{0,2,1:T(8,128)(2,1)}), bf16[400,32,64]{0,2,1:T(8,128)(2,1)S(1)}, u32[]{:S(2)}, u32[]{:S(2)}) async-start(bf16[400,32,64]{0,2,1:T(8,128)(2,1)} %pad_maximum_fusion), calls=%async_computation | async-start | bytes 4194304 | tf_op jit(solution)/shard_map/all_to_all | solution.py:148
  95.5 1.9 copy-start.3
  102.9 1.2 copy-start.1
  149.9 1.0 copy-start.2
  152.8 3.9 %collective-permute-start.1 = (bf16[128,2048]{1,0:T(8,128)(2,1)S(1)}, bf16[128,2048]{1,0:T(8,128)(2,1)S(1)}, u32[]{:S(2)}, u32[]{:S(2)}) collective-permute-start(bf16[128,2048]{1,0:T(8,128)(2,1)S(1)} %copy.43), channel_id=1, source_target_pairs={{0,1},{1,0},{2,3},{3,2},{4,5},{5,4},{6,7},{7,6},{8,9},{9,8},{10,11... | collective-permute-start | bytes 1572872 | tf_op jit(solution)/shard_map/ppermute | solution.py:157
  165.1 3.8 %collective-permute-start.2 = (bf16[16,2,128,64]{2,3,1,0:T(8,128)(2,1)S(1)}, bf16[16,2,128,64]{2,3,1,0:T(8,128)(2,1)S(1)}, u32[]{:S(2)}, u32[]{:S(2)}) collective-permute-start(bf16[16,2,128,64]{2,3,1,0:T(8,128)(2,1)S(1)} %get-tuple-element.12), channel_id=1, source_target_pairs={{0,1},{1,0},{2,3},{3,2},{4,5},{5,4},{6,7},{7,6},{8,9},{9,8},{10,11... | collective-permute-start | bytes 1572872 | tf_op jit(solution)/shard_map/ppermute | solution.py:160
  170.2 36.0 %all-to-all-start.1 = ((bf16[32,2,128,64]{2,3,1,0:T(8,128)(2,1)}), bf16[32,2,128,64]{2,3,1,0:T(8,128)(2,1)S(1)}, u32[]{:S(2)}, u32[]{:S(2)}) async-start(bf16[32,2,128,64]{2,3,1,0:T(8,128)(2,1)} %bitcast.50), calls=%async_computation.1 | async-start | bytes 2097152 | tf_op jit(solution)/shard_map/all_to_all | solution.py:163
  206.2 1.0 copy-start.4
Sparse Core Ops, SparseCore 0:
  24.3 105.3 all-gather.1

commit v12 on v10

--- a/solution.py
+++ b/solution.py
@@ -52,7 +52,7 @@
 MESH = pl.DeviceIdType.MESH
 
 
-def _attend_scatter_kernel(len_ref, q_ref, k_ref, v_ref, out_ref, ctx_buf, send_sem, recv_sem, own_sem):
+def _attend_scatter_kernel(len_ref, x_ref, out_ref, ctx_buf, send_sem, recv_sem, own_sem):
     n_dev, chunk = out_ref.shape[0], out_ref.shape[1]
     me = lax.axis_index("seq")
     place = (lax.axis_index("doc_y"), lax.axis_index("doc_x"))
@@ -71,16 +71,18 @@
 
     def block(step, carry):
         b = lax.rem(step + me // 2, n_dev // 2)
-        rows = pl.ds(pl.multiple_of(b * 2 * chunk, 2 * chunk), 2 * chunk)
+        queries = x_ref[pl.ds(2 * b, 2), 0:chunk, :].reshape(2 * chunk, -1)
+        keys = x_ref[:, chunk:2 * chunk, :].reshape(n_dev * chunk, -1)
         scores = lax.dot_general(
-            q_ref[rows, :], k_ref[...], (((1,), (1,)), ((), ())), preferred_element_type=jnp.float32
+            queries, keys, (((1,), (1,)), ((), ())), preferred_element_type=jnp.float32
         ) * HEAD_DIM ** (-0.5)
         key_pos = lax.broadcasted_iota(jnp.int32, scores.shape, 1)
         scores = jnp.where(key_pos < length, scores, -1e30)
         row_max = jnp.max(scores, axis=1, keepdims=True)
         weights = jnp.exp(scores - row_max)
         denominator = jnp.sum(weights, axis=1, keepdims=True)
-        weighted = jnp.dot(weights.astype(jnp.bfloat16), v_ref[...], preferred_element_type=jnp.float32)
+        values = x_ref[:, 2 * chunk:3 * chunk, :].reshape(n_dev * chunk, -1)
+        weighted = jnp.dot(weights.astype(jnp.bfloat16), values, preferred_element_type=jnp.float32)
         context = (weighted / denominator).astype(jnp.bfloat16)
         ctx_buf[pl.ds(2 * b, 2)] = context.reshape(2, chunk, context.shape[1])
         for j in range(2):
@@ -107,15 +109,14 @@
     own.wait()
 
 
-def attend_scatter(queries, keys_in, values_in, length, n_dev):
-    nq, width = queries.shape
-    chunk = nq // n_dev
-    nk = keys_in.shape[0]
+def attend_scatter(mixed, length, n_dev, chunk):
+    width = mixed.shape[2]
+    nq = nk = n_dev * chunk
     vmem = pl.BlockSpec(memory_space=pltpu.VMEM)
     return pl.pallas_call(
         _attend_scatter_kernel,
         out_shape=jax.ShapeDtypeStruct((n_dev, chunk, width), jnp.bfloat16),
-        in_specs=[pl.BlockSpec(memory_space=pltpu.SMEM), vmem, vmem, vmem],
+        in_specs=[pl.BlockSpec(memory_space=pltpu.SMEM), vmem],
         out_specs=pl.BlockSpec(memory_space=pl.ANY),
         scratch_shapes=[
             pltpu.VMEM((n_dev, chunk, width), jnp.bfloat16),
@@ -129,7 +130,7 @@
         compiler_params=pltpu.CompilerParams(
             collective_id=1, has_side_effects=True, vmem_limit_bytes=48 * 1024 * 1024
         ),
-    )(length.reshape(1), queries, keys_in, values_in)
+    )(length.reshape(1), mixed)
 
 
 def shards(enc_query, enc_key, enc_value, sum_query, doc_len, w_memory):
@@ -145,13 +146,11 @@
     w_half = lax.all_gather(w_half, "doc_y", axis=2, tiled=True)
 
     rows, sum_rows = enc_query.shape[1], sum_query.shape[1]
-    mixed = lax.all_to_all(
-        jnp.concatenate([enc_query[0], enc_key[0], enc_value[0], sum_query[0]], axis=0),
-        "seq", split_axis=1, concat_axis=0, tiled=True,
-    ).reshape(n_seq, 3 * rows + sum_rows, -1)
-    head_query, head_key, head_value = (mixed[:, i * rows:(i + 1) * rows].reshape(n_seq * rows, -1) for i in range(3))
+    mixed = jnp.concatenate([enc_query[0], enc_key[0], enc_value[0], sum_query[0]], axis=0)
+    mixed = mixed.reshape(3 * rows + sum_rows, n_seq, -1).transpose(1, 0, 2)
+    mixed = lax.all_to_all(mixed, "seq", split_axis=0, concat_axis=0, tiled=True)
     summary_heads = mixed[:, 3 * rows:].reshape(n_seq * sum_rows, -1)
-    by_head = attend_scatter(head_query, head_key, head_value, length, n_seq)
+    by_head = attend_scatter(mixed, length, n_seq, rows)
     encoder_out = by_head.transpose(1, 0, 2).reshape(by_head.shape[1], -1)
 
     enc_pair = jnp.concatenate([encoder_out, lax.ppermute(encoder_out, "seq", sibling)], axis=0)

time: 235 us -> 232 us (0.987)
  local copies, waits for them, and re-layouts: 25.3 us -> 20.8 us
    slice x4 -> x0, local copies, waits for them, and re-layouts: 7.16 us -> none  [shards(): mixed[:, i * rows:(i + 1) * rows].reshape(n_seq * rows, -1)]
    all_to_all x0 -> x1, local copies, waits for them, and re-layouts: none -> 2.97 us  [shards(): lax.all_to_all(mixed, 'seq', split_axis=0, concat_axis=0, tiled=True)]
    unnamed x28 -> x23, local copies, waits for them, and re-layouts: 8.93 us -> 10.6 us
  transfers between devices with their start and end apart: 7 -> 7, of which waited for: 6 -> 6; matrix products, arithmetic and copies ran while one was open for 6% -> 4% of each run, Pallas kernels for 20% -> 20%
where the time goes in v12:
time: 232 us; the launch traced here: 231 us
  waiting for transfers between devices  95.8 us (41%)
  Pallas kernels  49.9 us (22%)
  starting transfers between devices  39.5 us (17%)
  local copies, waits for them, and re-layouts  20.8 us (9%)
  between operations  15 us (6%)
  matrix products  6.82 us (3%)
  other arithmetic  3.2 us (1%)
    all_to_all x1, waiting for transfers between devices, shards(): lax.all_to_all(mixed, 'seq', split_axis=0, concat_axis=0, tiled=True)  49.4 us
    pallas_call x1, Pallas kernels, attend_scatter(): pl.pallas_call(_attend_scatter_kernel, out_shape=jax.ShapeDtypeStruct((n_...  45.8 us
    all_to_all x1, waiting for transfers between devices, shards(): lax.all_to_all(by_head, 'seq', split_axis=0, concat_axis=2, tiled=True)  27.8 us
    all_to_all x1, starting transfers between devices, shards(): lax.all_to_all(mixed, 'seq', split_axis=0, concat_axis=0, tiled=True)  16.3 us
    unnamed x23, local copies, waits for them, and re-layouts  10.6 us
    ppermute x1, waiting for transfers between devices, shards(): w_pair = lax.ppermute(w_half, 'doc_x', perm=[(0, 1), (1, 0)])  8.15 us
    all_to_all x1, starting transfers between devices, shards(): lax.all_to_all(by_head, 'seq', split_axis=0, concat_axis=2, tiled=True)  7.96 us
    all_to_all x1, waiting for transfers between devices, shards(): lax.all_to_all(answer, 'seq', split_axis=0, concat_axis=1, tiled=True)  7.41 us
  transfers between devices with their start and end apart: 7, of which 6 were waited for; matrix products, arithmetic and copies ran while one was open for 4% of the time, Pallas kernels for 20%

profile of v12, /device:TPU:1, one launch (start us, length us, event | category | flops | bytes accessed | tf_op | source)
XLA Modules:
  0.0 230.9 jit_solution(5537044845808276368)
XLA Ops:
  7.2 0.0 copy-start
  7.2 0.0 all-gather.2.cloned.1.call-start
  7.2 1.2 copy-done
  8.4 0.4 constant_dynamic-slice_fusion
  8.8 0.0 copy-start.7
  8.8 0.3 copy.61
  9.1 0.0 copy-start.6
  9.1 5.6 %collective-permute-start = (bf16[2,2048,64]{1,2,0:T(8,128)(2,1)S(1)}, bf16[2,2048,64]{1,2,0:T(8,128)(2,1)S(1)}, u32[]{:S(2)}, u32[]{:S(2)}) collective-permute-start(bf16[2,2048,64]{1,2,0:T(8,128)(2,1)S(1)} %copy.61), channel_id=1, source_target_pairs={{0,32},{32,0},{1,33},{33,1},{2,34},{34,2},{3,35},{35,3},{4,36},{36... | collective-permute-start | bytes 1572872 | tf_op jit(solution)/shard_map/ppermute | solution.py:143
  14.7 8.1 %collective-permute-done = bf16[2,2048,64]{1,2,0:T(8,128)(2,1)S(1)} collective-permute-done((bf16[2,2048,64]{1,2,0:T(8,128)(2,1)S(1)}, bf16[2,2048,64]{1,2,0:T(8,128)(2,1)S(1)}, u32[]{:S(2)}, u32[]{:S(2)}) %collective-permute-start) | collective-permute-done | bytes 524320 | tf_op jit(solution)/shard_map/ppermute | solution.py:143
  22.9 1.2 maximum_select_fusion
  24.1 0.0 all-gather.2.cloned.1.call-update
  24.2 0.3 copy.60
  24.5 0.3 copy.46
  24.7 1.3 copy.45
  26.1 1.3 copy.44
  27.4 1.8 maximum_bitcast_fusion
  29.2 16.3 %all-to-all-start = ((bf16[32,400,64]{1,2,0:T(8,128)(2,1)}), bf16[32,400,64]{1,2,0:T(8,128)(2,1)S(1)}, u32[]{:S(2)}, u32[]{:S(2)}) async-start(bf16[32,400,64]{1,2,0:T(8,128)(2,1)} %maximum_bitcast_fusion), calls=%async_computation | async-start | bytes 4194304 | tf_op jit(solution)/shard_map/all_to_all | solution.py:151
  46.1 49.4 %all-to-all-done = bf16[32,400,64]{1,2,0:T(8,128)(2,1)S(1)} async-done(((bf16[32,400,64]{1,2,0:T(8,128)(2,1)}), bf16[32,400,64]{1,2,0:T(8,128)(2,1)S(1)}, u32[]{:S(2)}, u32[]{:S(2)}) %all-to-all-start) | async-done | bytes 1638432 | tf_op jit(solution)/shard_map/all_to_all | solution.py:151
  95.6 1.4 copy-done.2
  97.0 3.0 %copy.48.x_ref = bf16[32,400,64]{2,1,0:T(8,128)(2,1)} copy(bf16[32,400,64]{1,2,0:T(8,128)(2,1)S(1)} %all-to-all-done) | data formatting | bytes 3276800 | tf_op jit(solution)/shard_map/all_to_all | solution.py:151
  99.9 1.9 copy-done.1
  101.9 45.8 %shard_map.77 = bf16[32,128,64]{2,1,0:T(8,128)(2,1)S(1)} custom-call(s32[1]{0:T(128)S(6)} %copy.64.len_ref, bf16[32,400,64]{2,1,0:T(8,128)(2,1)S(1)} %copy-done.1), custom_call_target="tpu_custom_call" | custom-call | flops 4294967296 | bytes 2097152 | tf_op jit(solution)/shard_map/pallas_call | solution.py:116
  147.7 0.4 copy.49
  148.1 0.2 copy.54
  148.3 2.4 %collective-permute-start.1 = (bf16[128,2048]{1,0:T(8,128)(2,1)S(1)}, bf16[128,2048]{1,0:T(8,128)(2,1)S(1)}, u32[]{:S(2)}, u32[]{:S(2)}) collective-permute-start(bf16[128,2048]{1,0:T(8,128)(2,1)S(1)} %copy.54), channel_id=1, source_target_pairs={{0,1},{1,0},{2,3},{3,2},{4,5},{5,4},{6,7},{7,6},{8,9},{9,8},{10,11... | collective-permute-start | bytes 1572872 | tf_op jit(solution)/shard_map/ppermute | solution.py:156
  150.7 1.5 collective-permute-done.1
  152.2 6.8 %fusion = bf16[2,256,1024]{1,2,0:T(8,128)(2,1)} fusion(bf16[2,2048,1024]{1,2,0:T(8,128)(2,1)} %all-gather.2.cloned.1.call-done, bf16[128,2048]{1,0:T(8,128)(2,1)S(1)} %collective-permute-done.1, bf16[128,2048]{1,0:T(8,128)(2,1)S(1)} %copy.54), kind=kOutput, calls=%fused_computation.2 | convolution fusion | flops 2150105088 | bytes 10485760 | tf_op jit(solution)/shard_map/tf,kfc->ktc/dot_general | solution.py:157
  159.0 1.3 reshape.33
  160.4 0.3 copy.63
  160.7 0.1 slice_bitcast_fusion.3
  160.8 2.3 collective-permute-start.2
  163.1 1.5 collective-permute-done.2
  164.6 0.2 maximum_select_fusion.1
  164.7 1.1 copy.56
  165.8 8.0 %all-to-all-start.1 = ((bf16[32,2,128,64]{2,3,1,0:T(8,128)(2,1)}), bf16[32,2,128,64]{2,3,1,0:T(8,128)(2,1)S(1)}, u32[]{:S(2)}, u32[]{:S(2)}) async-start(bf16[32,2,128,64]{2,3,1,0:T(8,128)(2,1)} %bitcast.44), calls=%async_computation.1 | async-start | bytes 2097152 | tf_op jit(solution)/shard_map/all_to_all | solution.py:162
  173.8 0.2 copy.50
  174.0 27.8 %all-to-all-done.1 = bf16[32,2,128,64]{2,3,1,0:T(8,128)(2,1)S(1)} async-done(((bf16[32,2,128,64]{2,3,1,0:T(8,128)(2,1)}), bf16[32,2,128,64]{2,3,1,0:T(8,128)(2,1)S(1)}, u32[]{:S(2)}, u32[]{:S(2)}) %all-to-all-start.1) | async-done | bytes 1048608 | tf_op jit(solution)/shard_map/all_to_all | solution.py:162
  201.8 1.0 copy-done.5
  202.8 2.0 copy.57
  204.8 0.1 slice_bitcast_fusion
  205.0 0.0 copy-start.4
  205.0 4.1 %shard_map.78 = bf16[512,64]{1,0:T(8,128)(2,1)S(1)} custom-call(s32[1]{0:T(128)S(6)} %copy.64.len_ref, bf16[512,64]{1,0:T(8,128)(2,1)S(1)} %bitcast.38, bf16[4096,64]{1,0:T(8,128)(2,1)S(1)} %get-tuple-element.9.k_ref, bf16[4096,64]{1,0:T(8,128)(2,1)S(1)} %get-tuple-element.8.v_ref), custom_call_target="tpu_custom_call" | custom-call | flops 536870912 | bytes 1179648 | tf_op jit(solution)/shard_map/pallas_call | solution.py:43
  209.0 0.8 reshape.35
  209.8 4.9 %all-to-all-start.2 = ((bf16[32,2,512]{2,1,0:T(2,128)(2,1)}), bf16[32,2,512]{2,1,0:T(2,128)(2,1)S(1)}, u32[]{:S(2)}, u32[]{:S(2)}) async-start(bf16[32,2,512]{2,1,0:T(2,128)(2,1)} %reshape.35), calls=%async_computation.2 | async-start | bytes 131072 | tf_op jit(solution)/shard_map/all_to_all | solution.py:165
  214.7 1.0 copy.59
  215.7 7.4 %all-to-all-done.2 = bf16[32,2,512]{2,1,0:T(2,128)(2,1)S(1)} async-done(((bf16[32,2,512]{2,1,0:T(2,128)(2,1)}), bf16[32,2,512]{2,1,0:T(2,128)(2,1)S(1)}, u32[]{:S(2)}, u32[]{:S(2)}) %all-to-all-start.2) | async-done | bytes 65568 | tf_op jit(solution)/shard_map/all_to_all | solution.py:165
  223.1 0.1 reshape.36
  223.3 0.8 broadcast_in_dim.3
  (12 shorter events, 0.1 us)
Async XLA Ops:
  7.2 1.2 copy-start
  7.2 145.0 %all-gather.2.cloned.1.call-start = ((), (), s32[]{:S(2)}) async-start(), calls=%async_computation.3 | async-start | bytes 9437184 | tf_op jit(solution)/shard_map/all_gather | solution.py:146
  8.8 15.4 %copy-start.7 = (bf16[1,16,2048]{2,1,0:T(8,128)(2,1)S(1)}, bf16[1,16,2048]{2,1,0:T(8,128)(2,1)}, u32[]{:S(2)}) copy-start(bf16[1,16,2048]{2,1,0:T(8,128)(2,1)} %param.9) | copy-start | bytes 196612
  9.1 15.3 %copy-start.6 = (bf16[1,128,2048]{2,1,0:T(8,128)(2,1)S(1)}, bf16[1,128,2048]{2,1,0:T(8,128)(2,1)}, u32[]{:S(2)}) copy-start(bf16[1,128,2048]{2,1,0:T(8,128)(2,1)} %param.8) | copy-start | bytes 1572868
  9.1 13.8 %collective-permute-start = (bf16[2,2048,64]{1,2,0:T(8,128)(2,1)S(1)}, bf16[2,2048,64]{1,2,0:T(8,128)(2,1)S(1)}, u32[]{:S(2)}, u32[]{:S(2)}) collective-permute-start(bf16[2,2048,64]{1,2,0:T(8,128)(2,1)S(1)} %copy.61), channel_id=1, source_target_pairs={{0,32},{32,0},{1,33},{33,1},{2,34},{34,2},{3,35},{35,3},{4,36},{36... | collective-permute-start | bytes 1572872 | tf_op jit(solution)/shard_map/ppermute | solution.py:143
  29.2 66.4 %all-to-all-start = ((bf16[32,400,64]{1,2,0:T(8,128)(2,1)}), bf16[32,400,64]{1,2,0:T(8,128)(2,1)S(1)}, u32[]{:S(2)}, u32[]{:S(2)}) async-start(bf16[32,400,64]{1,2,0:T(8,128)(2,1)} %maximum_bitcast_fusion), calls=%async_computation | async-start | bytes 4194304 | tf_op jit(solution)/shard_map/all_to_all | solution.py:151
  95.6 1.4 copy-start.2
  99.9 1.9 copy-start.1
  148.1 11.0 %copy-start.3 = (bf16[128,32,64]{0,2,1:T(8,128)(2,1)}, bf16[128,32,64]{0,2,1:T(8,128)(2,1)S(1)}, u32[]{:S(2)}) copy-start(bf16[128,32,64]{0,2,1:T(8,128)(2,1)S(1)} %copy.49) | copy-start | bytes 1572868
  148.3 3.9 %collective-permute-start.1 = (bf16[128,2048]{1,0:T(8,128)(2,1)S(1)}, bf16[128,2048]{1,0:T(8,128)(2,1)S(1)}, u32[]{:S(2)}, u32[]{:S(2)}) collective-permute-start(bf16[128,2048]{1,0:T(8,128)(2,1)S(1)} %copy.54), channel_id=1, source_target_pairs={{0,1},{1,0},{2,3},{3,2},{4,5},{5,4},{6,7},{7,6},{8,9},{9,8},{10,11... | collective-permute-start | bytes 1572872 | tf_op jit(solution)/shard_map/ppermute | solution.py:156
  160.8 3.8 %collective-permute-start.2 = (bf16[16,2,128,64]{2,3,1,0:T(8,128)(2,1)S(1)}, bf16[16,2,128,64]{2,3,1,0:T(8,128)(2,1)S(1)}, u32[]{:S(2)}, u32[]{:S(2)}) collective-permute-start(bf16[16,2,128,64]{2,3,1,0:T(8,128)(2,1)S(1)} %get-tuple-element.11), channel_id=1, source_target_pairs={{0,1},{1,0},{2,3},{3,2},{4,5},{5,4},{6,7},{7,6},{8,9},{9,8},{10,11... | collective-permute-start | bytes 1572872 | tf_op jit(solution)/shard_map/ppermute | solution.py:159
  165.8 8.0 %slice-start = ((bf16[32,400,64]{1,2,0:T(8,128)(2,1)}), bf16[32,16,64]{1,2,0:T(8,128)(2,1)S(1)}, s32[]{:S(2)}) async-start(bf16[32,400,64]{1,2,0:T(8,128)(2,1)} %copy-done.2), calls=%async_computation.4 | async-start | bytes 1048576 | tf_op jit(solution)/shard_map/slice | solution.py:152
  165.8 35.9 %all-to-all-start.1 = ((bf16[32,2,128,64]{2,3,1,0:T(8,128)(2,1)}), bf16[32,2,128,64]{2,3,1,0:T(8,128)(2,1)S(1)}, u32[]{:S(2)}, u32[]{:S(2)}) async-start(bf16[32,2,128,64]{2,3,1,0:T(8,128)(2,1)} %bitcast.44), calls=%async_computation.1 | async-start | bytes 2097152 | tf_op jit(solution)/shard_map/all_to_all | solution.py:162
  201.8 1.0 copy-start.5
  205.0 9.7 %copy-start.4 = (bf16[128,32,64]{0,2,1:T(8,128)(2,1)S(1)}, bf16[128,32,64]{0,2,1:T(8,128)(2,1)}, u32[]{:S(2)}) copy-start(bf16[128,32,64]{0,2,1:T(8,128)(2,1)} %copy-done.3) | copy-start | bytes 1572868
  209.8 13.3 %all-to-all-start.2 = ((bf16[32,2,512]{2,1,0:T(2,128)(2,1)}), bf16[32,2,512]{2,1,0:T(2,128)(2,1)S(1)}, u32[]{:S(2)}, u32[]{:S(2)}) async-start(bf16[32,2,512]{2,1,0:T(2,128)(2,1)} %reshape.35), calls=%async_computation.2 | async-start | bytes 131072 | tf_op jit(solution)/shard_map/all_to_all | solution.py:165
Sparse Core Ops, SparseCore 0:
  24.3 105.3 all-gather.1

commit v13 on v12

--- a/solution.py
+++ b/solution.py
@@ -70,7 +70,7 @@
     length = len_ref[0]
 
     def block(step, carry):
-        b = lax.rem(step + me // 2, n_dev // 2)
+        b = lax.rem(step + me // 2 + 1, n_dev // 2)
         queries = x_ref[pl.ds(2 * b, 2), 0:chunk, :].reshape(2 * chunk, -1)
         keys = x_ref[:, chunk:2 * chunk, :].reshape(n_dev * chunk, -1)
         scores = lax.dot_general(

time: 232 us -> 230 us (level)
  transfers between devices with their start and end apart: 7 -> 7, of which waited for: 6 -> 6; matrix products, arithmetic and copies ran while one was open for 4% -> 4% of each run, Pallas kernels for 20% -> 19%
where the time goes in v13:
time: 230 us; the launch traced here: 229 us
  waiting for transfers between devices  95.8 us (42%)
  Pallas kernels  47.9 us (21%)
  starting transfers between devices  39.5 us (17%)
  local copies, waits for them, and re-layouts  20.8 us (9%)
  between operations  15 us (7%)
  matrix products  6.82 us (3%)
  other arithmetic  3.2 us (1%)
    all_to_all x1, waiting for transfers between devices, shards(): lax.all_to_all(mixed, 'seq', split_axis=0, concat_axis=0, tiled=True)  49.4 us
    pallas_call x1, Pallas kernels, attend_scatter(): pl.pallas_call(_attend_scatter_kernel, out_shape=jax.ShapeDtypeStruct((n_...  43.8 us
    all_to_all x1, waiting for transfers between devices, shards(): lax.all_to_all(by_head, 'seq', split_axis=0, concat_axis=2, tiled=True)  27.8 us
    all_to_all x1, starting transfers between devices, shards(): lax.all_to_all(mixed, 'seq', split_axis=0, concat_axis=0, tiled=True)  16.3 us
    unnamed x23, local copies, waits for them, and re-layouts  10.6 us
    ppermute x1, waiting for transfers between devices, shards(): w_pair = lax.ppermute(w_half, 'doc_x', perm=[(0, 1), (1, 0)])  8.15 us
    all_to_all x1, starting transfers between devices, shards(): lax.all_to_all(by_head, 'seq', split_axis=0, concat_axis=2, tiled=True)  7.97 us
    all_to_all x1, waiting for transfers between devices, shards(): lax.all_to_all(answer, 'seq', split_axis=0, concat_axis=1, tiled=True)  7.41 us
  transfers between devices with their start and end apart: 7, of which 6 were waited for; matrix products, arithmetic and copies ran while one was open for 4% of the time, Pallas kernels for 19%

profile of v13, /device:TPU:1, one launch (start us, length us, event | category | flops | bytes accessed | tf_op | source)
XLA Modules:
  0.0 228.9 jit_solution(15700824635192781018)
XLA Ops:
  7.2 0.0 copy-start
  7.2 0.0 all-gather.2.cloned.1.call-start
  7.2 1.2 copy-done
  8.4 0.4 constant_dynamic-slice_fusion
  8.8 0.0 copy-start.7
  8.8 0.3 copy.61
  9.1 0.0 copy-start.6
  9.1 5.6 %collective-permute-start = (bf16[2,2048,64]{1,2,0:T(8,128)(2,1)S(1)}, bf16[2,2048,64]{1,2,0:T(8,128)(2,1)S(1)}, u32[]{:S(2)}, u32[]{:S(2)}) collective-permute-start(bf16[2,2048,64]{1,2,0:T(8,128)(2,1)S(1)} %copy.61), channel_id=1, source_target_pairs={{0,32},{32,0},{1,33},{33,1},{2,34},{34,2},{3,35},{35,3},{4,36},{36... | collective-permute-start | bytes 1572872 | tf_op jit(solution)/shard_map/ppermute | solution.py:143
  14.7 8.1 %collective-permute-done = bf16[2,2048,64]{1,2,0:T(8,128)(2,1)S(1)} collective-permute-done((bf16[2,2048,64]{1,2,0:T(8,128)(2,1)S(1)}, bf16[2,2048,64]{1,2,0:T(8,128)(2,1)S(1)}, u32[]{:S(2)}, u32[]{:S(2)}) %collective-permute-start) | collective-permute-done | bytes 524320 | tf_op jit(solution)/shard_map/ppermute | solution.py:143
  22.9 1.2 maximum_select_fusion
  24.1 0.0 all-gather.2.cloned.1.call-update
  24.2 0.3 copy.60
  24.5 0.3 copy.46
  24.7 1.3 copy.45
  26.1 1.3 copy.44
  27.4 1.8 maximum_bitcast_fusion
  29.2 16.3 %all-to-all-start = ((bf16[32,400,64]{1,2,0:T(8,128)(2,1)}), bf16[32,400,64]{1,2,0:T(8,128)(2,1)S(1)}, u32[]{:S(2)}, u32[]{:S(2)}) async-start(bf16[32,400,64]{1,2,0:T(8,128)(2,1)} %maximum_bitcast_fusion), calls=%async_computation | async-start | bytes 4194304 | tf_op jit(solution)/shard_map/all_to_all | solution.py:151
  46.1 49.4 %all-to-all-done = bf16[32,400,64]{1,2,0:T(8,128)(2,1)S(1)} async-done(((bf16[32,400,64]{1,2,0:T(8,128)(2,1)}), bf16[32,400,64]{1,2,0:T(8,128)(2,1)S(1)}, u32[]{:S(2)}, u32[]{:S(2)}) %all-to-all-start) | async-done | bytes 1638432 | tf_op jit(solution)/shard_map/all_to_all | solution.py:151
  95.6 1.4 copy-done.2
  97.0 3.0 %copy.48.x_ref = bf16[32,400,64]{2,1,0:T(8,128)(2,1)} copy(bf16[32,400,64]{1,2,0:T(8,128)(2,1)S(1)} %all-to-all-done) | data formatting | bytes 3276800 | tf_op jit(solution)/shard_map/all_to_all | solution.py:151
  99.9 1.9 copy-done.1
  101.9 43.8 %shard_map.77 = bf16[32,128,64]{2,1,0:T(8,128)(2,1)S(1)} custom-call(s32[1]{0:T(128)S(6)} %copy.64.len_ref, bf16[32,400,64]{2,1,0:T(8,128)(2,1)S(1)} %copy-done.1), custom_call_target="tpu_custom_call" | custom-call | flops 4294967296 | bytes 2097152 | tf_op jit(solution)/shard_map/pallas_call | solution.py:116
  145.7 0.4 copy.49
  146.1 0.0 copy-start.3
  146.1 0.2 copy.54
  146.3 2.4 %collective-permute-start.1 = (bf16[128,2048]{1,0:T(8,128)(2,1)S(1)}, bf16[128,2048]{1,0:T(8,128)(2,1)S(1)}, u32[]{:S(2)}, u32[]{:S(2)}) collective-permute-start(bf16[128,2048]{1,0:T(8,128)(2,1)S(1)} %copy.54), channel_id=1, source_target_pairs={{0,1},{1,0},{2,3},{3,2},{4,5},{5,4},{6,7},{7,6},{8,9},{9,8},{10,11... | collective-permute-start | bytes 1572872 | tf_op jit(solution)/shard_map/ppermute | solution.py:156
  148.7 1.5 collective-permute-done.1
  150.2 6.8 %fusion = bf16[2,256,1024]{1,2,0:T(8,128)(2,1)} fusion(bf16[2,2048,1024]{1,2,0:T(8,128)(2,1)} %all-gather.2.cloned.1.call-done, bf16[128,2048]{1,0:T(8,128)(2,1)S(1)} %collective-permute-done.1, bf16[128,2048]{1,0:T(8,128)(2,1)S(1)} %copy.54), kind=kOutput, calls=%fused_computation.2 | convolution fusion | flops 2150105088 | bytes 10485760 | tf_op jit(solution)/shard_map/tf,kfc->ktc/dot_general | solution.py:157
  157.0 1.3 reshape.33
  158.4 0.3 copy.63
  158.6 0.1 slice_bitcast_fusion.3
  158.8 2.3 collective-permute-start.2
  161.1 1.5 collective-permute-done.2
  162.6 0.2 maximum_select_fusion.1
  162.7 1.1 copy.56
  163.8 8.0 %all-to-all-start.1 = ((bf16[32,2,128,64]{2,3,1,0:T(8,128)(2,1)}), bf16[32,2,128,64]{2,3,1,0:T(8,128)(2,1)S(1)}, u32[]{:S(2)}, u32[]{:S(2)}) async-start(bf16[32,2,128,64]{2,3,1,0:T(8,128)(2,1)} %bitcast.44), calls=%async_computation.1 | async-start | bytes 2097152 | tf_op jit(solution)/shard_map/all_to_all | solution.py:162
  171.8 0.2 copy.50
  172.0 27.8 %all-to-all-done.1 = bf16[32,2,128,64]{2,3,1,0:T(8,128)(2,1)S(1)} async-done(((bf16[32,2,128,64]{2,3,1,0:T(8,128)(2,1)}), bf16[32,2,128,64]{2,3,1,0:T(8,128)(2,1)S(1)}, u32[]{:S(2)}, u32[]{:S(2)}) %all-to-all-start.1) | async-done | bytes 1048608 | tf_op jit(solution)/shard_map/all_to_all | solution.py:162
  199.8 1.0 copy-done.5
  200.8 2.0 copy.57
  202.8 0.1 slice_bitcast_fusion
  203.0 4.0 %shard_map.78 = bf16[512,64]{1,0:T(8,128)(2,1)S(1)} custom-call(s32[1]{0:T(128)S(6)} %copy.64.len_ref, bf16[512,64]{1,0:T(8,128)(2,1)S(1)} %bitcast.38, bf16[4096,64]{1,0:T(8,128)(2,1)S(1)} %get-tuple-element.9.k_ref, bf16[4096,64]{1,0:T(8,128)(2,1)S(1)} %get-tuple-element.8.v_ref), custom_call_target="tpu_custom_call" | custom-call | flops 536870912 | bytes 1179648 | tf_op jit(solution)/shard_map/pallas_call | solution.py:43
  207.0 0.8 reshape.35
  207.8 4.9 %all-to-all-start.2 = ((bf16[32,2,512]{2,1,0:T(2,128)(2,1)}), bf16[32,2,512]{2,1,0:T(2,128)(2,1)S(1)}, u32[]{:S(2)}, u32[]{:S(2)}) async-start(bf16[32,2,512]{2,1,0:T(2,128)(2,1)} %reshape.35), calls=%async_computation.2 | async-start | bytes 131072 | tf_op jit(solution)/shard_map/all_to_all | solution.py:165
  212.7 1.0 copy.59
  213.7 7.4 %all-to-all-done.2 = bf16[32,2,512]{2,1,0:T(2,128)(2,1)S(1)} async-done(((bf16[32,2,512]{2,1,0:T(2,128)(2,1)}), bf16[32,2,512]{2,1,0:T(2,128)(2,1)S(1)}, u32[]{:S(2)}, u32[]{:S(2)}) %all-to-all-start.2) | async-done | bytes 65568 | tf_op jit(solution)/shard_map/all_to_all | solution.py:165
  221.1 0.1 reshape.36
  221.3 0.8 broadcast_in_dim.3
  (12 shorter events, 0.1 us)
Async XLA Ops:
  7.2 1.2 copy-start
  7.2 143.0 %all-gather.2.cloned.1.call-start = ((), (), s32[]{:S(2)}) async-start(), calls=%async_computation.3 | async-start | bytes 9437184 | tf_op jit(solution)/shard_map/all_gather | solution.py:146
  8.8 15.4 %copy-start.7 = (bf16[1,16,2048]{2,1,0:T(8,128)(2,1)S(1)}, bf16[1,16,2048]{2,1,0:T(8,128)(2,1)}, u32[]{:S(2)}) copy-start(bf16[1,16,2048]{2,1,0:T(8,128)(2,1)} %param.9) | copy-start | bytes 196612
  9.1 15.3 %copy-start.6 = (bf16[1,128,2048]{2,1,0:T(8,128)(2,1)S(1)}, bf16[1,128,2048]{2,1,0:T(8,128)(2,1)}, u32[]{:S(2)}) copy-start(bf16[1,128,2048]{2,1,0:T(8,128)(2,1)} %param.8) | copy-start | bytes 1572868
  9.1 13.8 %collective-permute-start = (bf16[2,2048,64]{1,2,0:T(8,128)(2,1)S(1)}, bf16[2,2048,64]{1,2,0:T(8,128)(2,1)S(1)}, u32[]{:S(2)}, u32[]{:S(2)}) collective-permute-start(bf16[2,2048,64]{1,2,0:T(8,128)(2,1)S(1)} %copy.61), channel_id=1, source_target_pairs={{0,32},{32,0},{1,33},{33,1},{2,34},{34,2},{3,35},{35,3},{4,36},{36... | collective-permute-start | bytes 1572872 | tf_op jit(solution)/shard_map/ppermute | solution.py:143
  29.2 66.4 %all-to-all-start = ((bf16[32,400,64]{1,2,0:T(8,128)(2,1)}), bf16[32,400,64]{1,2,0:T(8,128)(2,1)S(1)}, u32[]{:S(2)}, u32[]{:S(2)}) async-start(bf16[32,400,64]{1,2,0:T(8,128)(2,1)} %maximum_bitcast_fusion), calls=%async_computation | async-start | bytes 4194304 | tf_op jit(solution)/shard_map/all_to_all | solution.py:151
  95.6 1.4 copy-start.2
  99.9 1.9 copy-start.1
  146.1 10.9 %copy-start.3 = (bf16[128,32,64]{0,2,1:T(8,128)(2,1)}, bf16[128,32,64]{0,2,1:T(8,128)(2,1)S(1)}, u32[]{:S(2)}) copy-start(bf16[128,32,64]{0,2,1:T(8,128)(2,1)S(1)} %copy.49) | copy-start | bytes 1572868
  146.3 3.9 %collective-permute-start.1 = (bf16[128,2048]{1,0:T(8,128)(2,1)S(1)}, bf16[128,2048]{1,0:T(8,128)(2,1)S(1)}, u32[]{:S(2)}, u32[]{:S(2)}) collective-permute-start(bf16[128,2048]{1,0:T(8,128)(2,1)S(1)} %copy.54), channel_id=1, source_target_pairs={{0,1},{1,0},{2,3},{3,2},{4,5},{5,4},{6,7},{7,6},{8,9},{9,8},{10,11... | collective-permute-start | bytes 1572872 | tf_op jit(solution)/shard_map/ppermute | solution.py:156
  158.8 3.8 %collective-permute-start.2 = (bf16[16,2,128,64]{2,3,1,0:T(8,128)(2,1)S(1)}, bf16[16,2,128,64]{2,3,1,0:T(8,128)(2,1)S(1)}, u32[]{:S(2)}, u32[]{:S(2)}) collective-permute-start(bf16[16,2,128,64]{2,3,1,0:T(8,128)(2,1)S(1)} %get-tuple-element.11), channel_id=1, source_target_pairs={{0,1},{1,0},{2,3},{3,2},{4,5},{5,4},{6,7},{7,6},{8,9},{9,8},{10,11... | collective-permute-start | bytes 1572872 | tf_op jit(solution)/shard_map/ppermute | solution.py:159
  163.8 8.0 %slice-start = ((bf16[32,400,64]{1,2,0:T(8,128)(2,1)}), bf16[32,16,64]{1,2,0:T(8,128)(2,1)S(1)}, s32[]{:S(2)}) async-start(bf16[32,400,64]{1,2,0:T(8,128)(2,1)} %copy-done.2), calls=%async_computation.4 | async-start | bytes 1048576 | tf_op jit(solution)/shard_map/slice | solution.py:152
  163.8 36.0 %all-to-all-start.1 = ((bf16[32,2,128,64]{2,3,1,0:T(8,128)(2,1)}), bf16[32,2,128,64]{2,3,1,0:T(8,128)(2,1)S(1)}, u32[]{:S(2)}, u32[]{:S(2)}) async-start(bf16[32,2,128,64]{2,3,1,0:T(8,128)(2,1)} %bitcast.44), calls=%async_computation.1 | async-start | bytes 2097152 | tf_op jit(solution)/shard_map/all_to_all | solution.py:162
  199.8 1.0 copy-start.5
  203.0 9.7 %copy-start.4 = (bf16[128,32,64]{0,2,1:T(8,128)(2,1)S(1)}, bf16[128,32,64]{0,2,1:T(8,128)(2,1)}, u32[]{:S(2)}) copy-start(bf16[128,32,64]{0,2,1:T(8,128)(2,1)} %copy-done.3) | copy-start | bytes 1572868
  207.8 13.3 %all-to-all-start.2 = ((bf16[32,2,512]{2,1,0:T(2,128)(2,1)}), bf16[32,2,512]{2,1,0:T(2,128)(2,1)S(1)}, u32[]{:S(2)}, u32[]{:S(2)}) async-start(bf16[32,2,512]{2,1,0:T(2,128)(2,1)} %reshape.35), calls=%async_computation.2 | async-start | bytes 131072 | tf_op jit(solution)/shard_map/all_to_all | solution.py:165
Sparse Core Ops, SparseCore 0:
  24.3 105.3 all-gather.1

commit v14 on v13

--- a/solution.py
+++ b/solution.py
@@ -54,6 +54,7 @@
 
 def _attend_scatter_kernel(len_ref, x_ref, out_ref, ctx_buf, send_sem, recv_sem, own_sem):
     n_dev, chunk = out_ref.shape[0], out_ref.shape[1]
+    group = 4
     me = lax.axis_index("seq")
     place = (lax.axis_index("doc_y"), lax.axis_index("doc_x"))
     barrier = pltpu.get_barrier_semaphore()
@@ -70,8 +71,8 @@
     length = len_ref[0]
 
     def block(step, carry):
-        b = lax.rem(step + me // 2 + 1, n_dev // 2)
-        queries = x_ref[pl.ds(2 * b, 2), 0:chunk, :].reshape(2 * chunk, -1)
+        b = lax.rem(step + me // group + 1, n_dev // group)
+        queries = x_ref[pl.ds(group * b, group), 0:chunk, :].reshape(group * chunk, -1)
         keys = x_ref[:, chunk:2 * chunk, :].reshape(n_dev * chunk, -1)
         scores = lax.dot_general(
             queries, keys, (((1,), (1,)), ((), ())), preferred_element_type=jnp.float32
@@ -84,9 +85,9 @@
         values = x_ref[:, 2 * chunk:3 * chunk, :].reshape(n_dev * chunk, -1)
         weighted = jnp.dot(weights.astype(jnp.bfloat16), values, preferred_element_type=jnp.float32)
         context = (weighted / denominator).astype(jnp.bfloat16)
-        ctx_buf[pl.ds(2 * b, 2)] = context.reshape(2, chunk, context.shape[1])
-        for j in range(2):
-            owner = 2 * b + j
+        ctx_buf[pl.ds(group * b, group)] = context.reshape(group, chunk, context.shape[1])
+        for j in range(group):
+            owner = group * b + j
 
             @pl.when(owner != me)
             def _():
@@ -97,7 +98,7 @@
 
         return carry
 
-    lax.fori_loop(0, n_dev // 2, block, 0)
+    lax.fori_loop(0, n_dev // group, block, 0)
     own = pltpu.make_async_copy(ctx_buf.at[me], out_ref.at[me], own_sem)
     own.start()
     every = pltpu.make_async_remote_copy(

time: 230 us -> 239 us (1.039)
  Pallas kernels: 47.9 us -> 58 us
    pallas_call x1, Pallas kernels: 43.8 us -> 54 us  [attend_scatter(): pl.pallas_call(_attend_scatter_kernel, out_shape=jax.ShapeDtypeStruct((n_...]
  transfers between devices with their start and end apart: 7 -> 7, of which waited for: 6 -> 6; matrix products, arithmetic and copies ran while one was open for 4% -> 4% of each run, Pallas kernels for 19% -> 23%
where the time goes in v14:
time: 239 us
  waiting for transfers between devices  96 us (40%)
  Pallas kernels  58 us (24%)
  starting transfers between devices  38.6 us (16%)
  local copies, waits for them, and re-layouts  20.8 us (9%)
  between operations  15 us (6%)
  matrix products  6.82 us (3%)
  other arithmetic  3.2 us (1%)
    pallas_call x1, Pallas kernels, attend_scatter(): pl.pallas_call(_attend_scatter_kernel, out_shape=jax.ShapeDtypeStruct((n_...  54 us
    all_to_all x1, waiting for transfers between devices, shards(): lax.all_to_all(mixed, 'seq', split_axis=0, concat_axis=0, tiled=True)  49.4 us
    all_to_all x1, waiting for transfers between devices, shards(): lax.all_to_all(by_head, 'seq', split_axis=0, concat_axis=2, tiled=True)  27.9 us
    all_to_all x1, starting transfers between devices, shards(): lax.all_to_all(mixed, 'seq', split_axis=0, concat_axis=0, tiled=True)  16.3 us
    unnamed x23, local copies, waits for them, and re-layouts  10.6 us
    ppermute x1, waiting for transfers between devices, shards(): w_pair = lax.ppermute(w_half, 'doc_x', perm=[(0, 1), (1, 0)])  8.15 us
    all_to_all x1, starting transfers between devices, shards(): lax.all_to_all(by_head, 'seq', split_axis=0, concat_axis=2, tiled=True)  7.47 us
    all_to_all x1, waiting for transfers between devices, shards(): lax.all_to_all(answer, 'seq', split_axis=0, concat_axis=1, tiled=True)  7.41 us
  transfers between devices with their start and end apart: 7, of which 6 were waited for; matrix products, arithmetic and copies ran while one was open for 4% of the time, Pallas kernels for 23%

profile of v14, /device:TPU:1, one launch (start us, length us, event | category | flops | bytes accessed | tf_op | source)
XLA Modules:
  0.0 238.5 jit_solution(13953649822777885836)
XLA Ops:
  7.2 0.0 copy-start
  7.2 0.0 all-gather.2.cloned.1.call-start
  7.2 1.2 copy-done
  8.4 0.4 constant_dynamic-slice_fusion
  8.8 0.3 copy.61
  9.1 0.0 copy-start.6
  9.1 5.6 %collective-permute-start = (bf16[2,2048,64]{1,2,0:T(8,128)(2,1)S(1)}, bf16[2,2048,64]{1,2,0:T(8,128)(2,1)S(1)}, u32[]{:S(2)}, u32[]{:S(2)}) collective-permute-start(bf16[2,2048,64]{1,2,0:T(8,128)(2,1)S(1)} %copy.61), channel_id=1, source_target_pairs={{0,32},{32,0},{1,33},{33,1},{2,34},{34,2},{3,35},{35,3},{4,36},{36... | collective-permute-start | bytes 1572872 | tf_op jit(solution)/shard_map/ppermute | solution.py:144
  14.7 8.1 %collective-permute-done = bf16[2,2048,64]{1,2,0:T(8,128)(2,1)S(1)} collective-permute-done((bf16[2,2048,64]{1,2,0:T(8,128)(2,1)S(1)}, bf16[2,2048,64]{1,2,0:T(8,128)(2,1)S(1)}, u32[]{:S(2)}, u32[]{:S(2)}) %collective-permute-start) | collective-permute-done | bytes 524320 | tf_op jit(solution)/shard_map/ppermute | solution.py:144
  22.9 1.2 maximum_select_fusion
  24.1 0.0 all-gather.2.cloned.1.call-update
  24.2 0.3 copy.60
  24.5 0.3 copy.46
  24.7 1.3 copy.45
  26.1 1.3 copy.44
  27.4 1.8 maximum_bitcast_fusion
  29.2 16.3 %all-to-all-start = ((bf16[32,400,64]{1,2,0:T(8,128)(2,1)}), bf16[32,400,64]{1,2,0:T(8,128)(2,1)S(1)}, u32[]{:S(2)}, u32[]{:S(2)}) async-start(bf16[32,400,64]{1,2,0:T(8,128)(2,1)} %maximum_bitcast_fusion), calls=%async_computation | async-start | bytes 4194304 | tf_op jit(solution)/shard_map/all_to_all | solution.py:152
  46.1 49.4 %all-to-all-done = bf16[32,400,64]{1,2,0:T(8,128)(2,1)S(1)} async-done(((bf16[32,400,64]{1,2,0:T(8,128)(2,1)}), bf16[32,400,64]{1,2,0:T(8,128)(2,1)S(1)}, u32[]{:S(2)}, u32[]{:S(2)}) %all-to-all-start) | async-done | bytes 1638432 | tf_op jit(solution)/shard_map/all_to_all | solution.py:152
  95.6 1.4 copy-done.2
  97.0 3.0 %copy.48.x_ref = bf16[32,400,64]{2,1,0:T(8,128)(2,1)} copy(bf16[32,400,64]{1,2,0:T(8,128)(2,1)S(1)} %all-to-all-done) | data formatting | bytes 3276800 | tf_op jit(solution)/shard_map/all_to_all | solution.py:152
  99.9 1.9 copy-done.1
  101.9 54.0 %shard_map.77 = bf16[32,128,64]{2,1,0:T(8,128)(2,1)S(1)} custom-call(s32[1]{0:T(128)S(6)} %copy.64.len_ref, bf16[32,400,64]{2,1,0:T(8,128)(2,1)S(1)} %copy-done.1), custom_call_target="tpu_custom_call" | custom-call | flops 4294967296 | bytes 2097152 | tf_op jit(solution)/shard_map/pallas_call | solution.py:117
  155.8 0.4 copy.49
  156.2 0.0 copy-start.3
  156.2 0.2 copy.54
  156.5 2.2 collective-permute-start.1
  158.7 1.5 collective-permute-done.1
  160.3 6.8 %fusion = bf16[2,256,1024]{1,2,0:T(8,128)(2,1)} fusion(bf16[2,2048,1024]{1,2,0:T(8,128)(2,1)} %all-gather.2.cloned.1.call-done, bf16[128,2048]{1,0:T(8,128)(2,1)S(1)} %collective-permute-done.1, bf16[128,2048]{1,0:T(8,128)(2,1)S(1)} %copy.54), kind=kOutput, calls=%fused_computation.2 | convolution fusion | flops 2150105088 | bytes 10485760 | tf_op jit(solution)/shard_map/tf,kfc->ktc/dot_general | solution.py:158
  167.1 1.3 reshape.33
  168.4 0.3 copy.63
  168.7 0.1 slice_bitcast_fusion.3
  168.8 2.2 collective-permute-start.2
  171.1 1.5 collective-permute-done.2
  172.6 0.2 maximum_select_fusion.1
  172.8 1.1 copy.56
  173.9 7.5 %all-to-all-start.1 = ((bf16[32,2,128,64]{2,3,1,0:T(8,128)(2,1)}), bf16[32,2,128,64]{2,3,1,0:T(8,128)(2,1)S(1)}, u32[]{:S(2)}, u32[]{:S(2)}) async-start(bf16[32,2,128,64]{2,3,1,0:T(8,128)(2,1)} %bitcast.44), calls=%async_computation.1 | async-start | bytes 2097152 | tf_op jit(solution)/shard_map/all_to_all | solution.py:163
  181.4 0.2 copy.50
  181.6 27.9 %all-to-all-done.1 = bf16[32,2,128,64]{2,3,1,0:T(8,128)(2,1)S(1)} async-done(((bf16[32,2,128,64]{2,3,1,0:T(8,128)(2,1)}), bf16[32,2,128,64]{2,3,1,0:T(8,128)(2,1)S(1)}, u32[]{:S(2)}, u32[]{:S(2)}) %all-to-all-start.1) | async-done | bytes 1048608 | tf_op jit(solution)/shard_map/all_to_all | solution.py:163
  209.5 1.0 copy-done.5
  210.5 2.0 copy.57
  212.5 0.1 slice_bitcast_fusion
  212.7 0.0 copy-start.4
  212.7 4.1 %shard_map.78 = bf16[512,64]{1,0:T(8,128)(2,1)S(1)} custom-call(s32[1]{0:T(128)S(6)} %copy.64.len_ref, bf16[512,64]{1,0:T(8,128)(2,1)S(1)} %bitcast.38, bf16[4096,64]{1,0:T(8,128)(2,1)S(1)} %get-tuple-element.9.k_ref, bf16[4096,64]{1,0:T(8,128)(2,1)S(1)} %get-tuple-element.8.v_ref), custom_call_target="tpu_custom_call" | custom-call | flops 536870912 | bytes 1179648 | tf_op jit(solution)/shard_map/pallas_call | solution.py:43
  216.8 0.8 reshape.35
  217.5 4.7 %all-to-all-start.2 = ((bf16[32,2,512]{2,1,0:T(2,128)(2,1)}), bf16[32,2,512]{2,1,0:T(2,128)(2,1)S(1)}, u32[]{:S(2)}, u32[]{:S(2)}) async-start(bf16[32,2,512]{2,1,0:T(2,128)(2,1)} %reshape.35), calls=%async_computation.2 | async-start | bytes 131072 | tf_op jit(solution)/shard_map/all_to_all | solution.py:166
  222.2 1.0 copy.59
  223.3 7.4 %all-to-all-done.2 = bf16[32,2,512]{2,1,0:T(2,128)(2,1)S(1)} async-done(((bf16[32,2,512]{2,1,0:T(2,128)(2,1)}), bf16[32,2,512]{2,1,0:T(2,128)(2,1)S(1)}, u32[]{:S(2)}, u32[]{:S(2)}) %all-to-all-start.2) | async-done | bytes 65568 | tf_op jit(solution)/shard_map/all_to_all | solution.py:166
  230.7 0.1 reshape.36
  230.8 0.8 broadcast_in_dim.3
  (12 shorter events, 0.1 us)
Async XLA Ops:
  7.2 1.2 copy-start
  7.2 153.1 %all-gather.2.cloned.1.call-start = ((), (), s32[]{:S(2)}) async-start(), calls=%async_computation.3 | async-start | bytes 9437184 | tf_op jit(solution)/shard_map/all_gather | solution.py:147
  8.8 15.4 %copy-start.7 = (bf16[1,16,2048]{2,1,0:T(8,128)(2,1)S(1)}, bf16[1,16,2048]{2,1,0:T(8,128)(2,1)}, u32[]{:S(2)}) copy-start(bf16[1,16,2048]{2,1,0:T(8,128)(2,1)} %param.9) | copy-start | bytes 196612
  9.1 15.3 %copy-start.6 = (bf16[1,128,2048]{2,1,0:T(8,128)(2,1)S(1)}, bf16[1,128,2048]{2,1,0:T(8,128)(2,1)}, u32[]{:S(2)}) copy-start(bf16[1,128,2048]{2,1,0:T(8,128)(2,1)} %param.8) | copy-start | bytes 1572868
  9.1 13.8 %collective-permute-start = (bf16[2,2048,64]{1,2,0:T(8,128)(2,1)S(1)}, bf16[2,2048,64]{1,2,0:T(8,128)(2,1)S(1)}, u32[]{:S(2)}, u32[]{:S(2)}) collective-permute-start(bf16[2,2048,64]{1,2,0:T(8,128)(2,1)S(1)} %copy.61), channel_id=1, source_target_pairs={{0,32},{32,0},{1,33},{33,1},{2,34},{34,2},{3,35},{35,3},{4,36},{36... | collective-permute-start | bytes 1572872 | tf_op jit(solution)/shard_map/ppermute | solution.py:144
  29.2 66.4 %all-to-all-start = ((bf16[32,400,64]{1,2,0:T(8,128)(2,1)}), bf16[32,400,64]{1,2,0:T(8,128)(2,1)S(1)}, u32[]{:S(2)}, u32[]{:S(2)}) async-start(bf16[32,400,64]{1,2,0:T(8,128)(2,1)} %maximum_bitcast_fusion), calls=%async_computation | async-start | bytes 4194304 | tf_op jit(solution)/shard_map/all_to_all | solution.py:152
  95.6 1.4 copy-start.2
  99.9 1.9 copy-start.1
  156.2 10.9 %copy-start.3 = (bf16[128,32,64]{0,2,1:T(8,128)(2,1)}, bf16[128,32,64]{0,2,1:T(8,128)(2,1)S(1)}, u32[]{:S(2)}) copy-start(bf16[128,32,64]{0,2,1:T(8,128)(2,1)S(1)} %copy.49) | copy-start | bytes 1572868
  156.5 3.8 %collective-permute-start.1 = (bf16[128,2048]{1,0:T(8,128)(2,1)S(1)}, bf16[128,2048]{1,0:T(8,128)(2,1)S(1)}, u32[]{:S(2)}, u32[]{:S(2)}) collective-permute-start(bf16[128,2048]{1,0:T(8,128)(2,1)S(1)} %copy.54), channel_id=1, source_target_pairs={{0,1},{1,0},{2,3},{3,2},{4,5},{5,4},{6,7},{7,6},{8,9},{9,8},{10,11... | collective-permute-start | bytes 1572872 | tf_op jit(solution)/shard_map/ppermute | solution.py:157
  168.8 3.8 %collective-permute-start.2 = (bf16[16,2,128,64]{2,3,1,0:T(8,128)(2,1)S(1)}, bf16[16,2,128,64]{2,3,1,0:T(8,128)(2,1)S(1)}, u32[]{:S(2)}, u32[]{:S(2)}) collective-permute-start(bf16[16,2,128,64]{2,3,1,0:T(8,128)(2,1)S(1)} %get-tuple-element.11), channel_id=1, source_target_pairs={{0,1},{1,0},{2,3},{3,2},{4,5},{5,4},{6,7},{7,6},{8,9},{9,8},{10,11... | collective-permute-start | bytes 1572872 | tf_op jit(solution)/shard_map/ppermute | solution.py:160
  173.9 7.5 %slice-start = ((bf16[32,400,64]{1,2,0:T(8,128)(2,1)}), bf16[32,16,64]{1,2,0:T(8,128)(2,1)S(1)}, s32[]{:S(2)}) async-start(bf16[32,400,64]{1,2,0:T(8,128)(2,1)} %copy-done.2), calls=%async_computation.4 | async-start | bytes 1048576 | tf_op jit(solution)/shard_map/slice | solution.py:153
  173.9 35.6 %all-to-all-start.1 = ((bf16[32,2,128,64]{2,3,1,0:T(8,128)(2,1)}), bf16[32,2,128,64]{2,3,1,0:T(8,128)(2,1)S(1)}, u32[]{:S(2)}, u32[]{:S(2)}) async-start(bf16[32,2,128,64]{2,3,1,0:T(8,128)(2,1)} %bitcast.44), calls=%async_computation.1 | async-start | bytes 2097152 | tf_op jit(solution)/shard_map/all_to_all | solution.py:163
  209.5 1.0 copy-start.5
  212.7 9.6 %copy-start.4 = (bf16[128,32,64]{0,2,1:T(8,128)(2,1)S(1)}, bf16[128,32,64]{0,2,1:T(8,128)(2,1)}, u32[]{:S(2)}) copy-start(bf16[128,32,64]{0,2,1:T(8,128)(2,1)} %copy-done.3) | copy-start | bytes 1572868
  217.5 13.1 %all-to-all-start.2 = ((bf16[32,2,512]{2,1,0:T(2,128)(2,1)}), bf16[32,2,512]{2,1,0:T(2,128)(2,1)S(1)}, u32[]{:S(2)}, u32[]{:S(2)}) async-start(bf16[32,2,512]{2,1,0:T(2,128)(2,1)} %reshape.35), calls=%async_computation.2 | async-start | bytes 131072 | tf_op jit(solution)/shard_map/all_to_all | solution.py:166
Sparse Core Ops, SparseCore 0:
  24.3 105.3 all-gather.1
